TPU v7x, 32 devices: a whole 2x2x4 slice. The times are simulated.
32 devices in a mesh: dp: 8 (over y, x, core), mp: 4 (over z).
Axes of the slice: x: 2, y: 2, z: 4, core: 2. Of those that a mesh axis runs over, the one named last changes fastest.
Arguments:
- tokens: bfloat16 [8192, 1536], P(('dp', 'mp')), may hold values from -6 to 6
- cotangent: bfloat16 [8192, 1536], P(('dp', 'mp')), may hold values from -6 to 6
- lengths: int32 [8, 8], P('dp'), may hold values from 1 to 512, 1024 in all within a row
- granularity: int32 [8], P('dp'), may hold values from 0 to 3
- ln1_gain: float32 [1536], replicated, may hold values from 0.5 to 1.5
- ln1_bias: float32 [1536], replicated, may hold values from -1.5 to 1.5
- w_qkv: bfloat16 [1536, 3, 1536], P('dp', None, 'mp'), may hold values from -0.21875 to 0.21875
- w_out: bfloat16 [1536, 1536], P(('mp', 'dp')), may hold values from -0.4375 to 0.4375
- ln2_gain: float32 [1536], replicated, may hold values from 0.5 to 1.5
- ln2_bias: float32 [1536], replicated, may hold values from -1.5 to 1.5
- w_up: bfloat16 [1536, 6144], P('dp', 'mp'), may hold values from -0.15625 to 0.15625
- w_down: bfloat16 [6144, 1536], P(('mp', 'dp')), may hold values from -0.15625 to 0.15625
Outputs:
- output: bfloat16 [8192, 1536], P(('dp', 'mp'))
- input_grad: bfloat16 [8192, 1536], P(('dp', 'mp'))
- grad_ln1_gain: float32 [1536], replicated
- grad_ln1_bias: float32 [1536], replicated
- grad_w_qkv: float32 [1536, 3, 1536], P('dp', None, 'mp')
- grad_w_out: float32 [1536, 1536], P(('mp', 'dp'))
- grad_ln2_gain: float32 [1536], replicated
- grad_ln2_bias: float32 [1536], replicated
- grad_w_up: float32 [1536, 6144], P('dp', 'mp')
- grad_w_down: float32 [6144, 1536], P(('mp', 'dp'))
Inputs may be any that keep to these rules, and one draw needn't show every extreme that they name: Row i lists the lengths of the 8 sequences packed in order into batch piece i; each row sums to 1024 and its longest sequence has exactly 512 tokens. Batch piece i uses the first 768 * 2^g hidden units of the feed-forward layer, g = granularity[i].
All inputs are finite; a program needn't handle non-finite values.
Results may differ from a plain program's by a relative error of at most 0.018.
Values may be sent and summed in bfloat16 or wider, within the bound.
No kernel may reach another device: no remote copies, remote signals or barrier semaphores. Data moves between devices by JAX's collectives and lax.ppermute only.
A program may use at most 128 MiB of HBM per device.

v0:
```python
import math

import jax
import jax.numpy as jnp
from jax import lax
from jax.sharding import PartitionSpec as P

HDIM = 128
PREFIX0 = 768


EPSILON = 1e-05
MASKED = -1e30


def piece_layout(seq_lengths, total_rows):
    seg_ends = jnp.cumsum(seq_lengths)
    starts = seg_ends - seq_lengths
    places = jnp.arange(total_rows, dtype=jnp.int32)
    seg_ids = jnp.sum((places[:, None] >= seg_ends[None, :]).astype(jnp.int32), axis=1)
    member = seg_ids[:, None] == jnp.arange(seq_lengths.shape[0], dtype=jnp.int32)[None, :]
    offsets = jnp.sum(jnp.where(member, starts[None, :], 0), axis=1)
    return (seg_ids, places - offsets)


def rotary_tables(positions, head_dim):
    half_dim = head_dim // 2
    frequencies = jnp.exp(
        jnp.arange(half_dim, dtype=jnp.float32) * (-2.0 * math.log(10000.0) / head_dim)
    )
    angles = positions.astype(jnp.float32)[:, None] * frequencies[None, :]
    return (jnp.cos(angles), jnp.sin(angles))


def rotate(values, cosine, sine):
    half_dim = values.shape[-1] // 2
    first_half = values[..., :half_dim]
    second_half = values[..., half_dim:]
    cos_rows = cosine[:, None, :]
    sin_rows = sine[:, None, :]
    return jnp.concatenate(
        [
            first_half * cos_rows - second_half * sin_rows,
            second_half * cos_rows + first_half * sin_rows,
        ],
        axis=-1,
    )


def norm_forward(values, norm_gain, norm_bias):
    center = values - jnp.mean(values, axis=-1, keepdims=True)
    inverse = lax.rsqrt(jnp.mean(center * center, axis=-1, keepdims=True) + EPSILON)
    normalized = center * inverse
    return (normalized * norm_gain + norm_bias, normalized, inverse)


def norm_backward(upstream, normalized, inverse, norm_gain):
    scaled = upstream * norm_gain
    return inverse * (
        scaled
        - jnp.mean(scaled, axis=-1, keepdims=True)
        - normalized * jnp.mean(scaled * normalized, axis=-1, keepdims=True)
    )


def gelu_back(pre_values, upstream):
    return jax.vjp(lambda pre_value: jax.nn.gelu(pre_value, approximate=True), pre_values)[1](
        upstream
    )[0]


def on_device(
    tokens,
    cotangent,
    lengths,
    granularity,
    ln1_gain,
    ln1_bias,
    w_qkv,
    w_out,
    ln2_gain,
    ln2_bias,
    w_up,
    w_down,
):
    mp_count = lax.axis_size("mp")
    mp_index = lax.axis_index("mp")
    wide_qkv, wide_up, wide_out, wide_down = (
        lax.all_gather(w_qkv, "dp", axis=0, tiled=True),
        lax.all_gather(w_up, "dp", axis=0, tiled=True),
        lax.all_gather(w_out, "dp", axis=0, tiled=True),
        lax.all_gather(w_down, "dp", axis=0, tiled=True),
    )
    local_rows = tokens.shape[0]
    total_rows = local_rows * mp_count
    head_width = wide_out.shape[0]
    local_heads = head_width // HDIM
    unit_count = wide_up.shape[1]
    block_rows = min(512, total_rows)
    block_count = total_rows // block_rows
    score_scale = HDIM ** (-0.5)
    seg_ids, positions = piece_layout(lengths[0], total_rows)
    places = jnp.arange(total_rows, dtype=jnp.int32)
    cosine, sine = rotary_tables(positions, HDIM)
    tokens_float = tokens.astype(jnp.float32)
    normed_one, unit_one, inverse_one = norm_forward(tokens_float, ln1_gain, ln1_bias)
    inputs_one = lax.all_gather(normed_one.astype(jnp.bfloat16), "mp", axis=0, tiled=True)
    projected = jnp.einsum("td,dch->tch", inputs_one, wide_qkv, preferred_element_type=jnp.float32)
    projected = projected.reshape(total_rows, 3, local_heads, HDIM)
    queries = rotate(projected[:, 0], cosine, sine).astype(jnp.bfloat16)
    keys_rot = rotate(projected[:, 1], cosine, sine).astype(jnp.bfloat16)
    values_all = projected[:, 2].astype(jnp.bfloat16)

    def block_scores(row_start):
        query_block = lax.dynamic_slice_in_dim(queries, row_start, block_rows, 0)
        seg_block = lax.dynamic_slice_in_dim(seg_ids, row_start, block_rows, 0)
        place_block = row_start + jnp.arange(block_rows, dtype=jnp.int32)
        scores = score_scale * jnp.einsum(
            "qhd,khd->hqk", query_block, keys_rot, preferred_element_type=jnp.float32
        )
        allowed = (seg_block[:, None] == seg_ids[None, :]) & (
            place_block[:, None] >= places[None, :]
        )
        return (jnp.where(allowed[None], scores, MASKED), query_block)

    def attend(block_index):
        scores, query_block = block_scores(block_index * block_rows)
        top_score = jnp.max(scores, axis=-1, keepdims=True)
        exp_scores = jnp.exp(scores - top_score)
        row_total = jnp.sum(exp_scores, axis=-1, keepdims=True)
        soft_weights = (exp_scores / row_total).astype(jnp.bfloat16)
        mixed_block = jnp.einsum(
            "hqk,khd->qhd", soft_weights, values_all, preferred_element_type=jnp.float32
        )
        return (mixed_block, (top_score + jnp.log(row_total))[..., 0])

    mixed_blocks, log_totals = lax.map(attend, jnp.arange(block_count, dtype=jnp.int32))
    mixed_heads = mixed_blocks.reshape(total_rows, head_width).astype(jnp.bfloat16)
    attn_part = jnp.dot(mixed_heads, wide_out, preferred_element_type=jnp.float32)
    resid_one = tokens_float + lax.psum_scatter(
        attn_part.astype(jnp.bfloat16), "mp", scatter_dimension=0, tiled=True
    ).astype(jnp.float32)
    normed_two, unit_two, inverse_two = norm_forward(resid_one, ln2_gain, ln2_bias)
    inputs_two = lax.all_gather(normed_two.astype(jnp.bfloat16), "mp", axis=0, tiled=True)
    prefix = PREFIX0 * jnp.left_shift(jnp.int32(1), granularity[0])
    active_units = jnp.clip(prefix - mp_index * unit_count, 0, unit_count)
    keep_units = (jnp.arange(unit_count, dtype=jnp.int32) < active_units).astype(jnp.float32)
    pre_act = jnp.dot(inputs_two, wide_up, preferred_element_type=jnp.float32)
    hidden_act = (jax.nn.gelu(pre_act, approximate=True) * keep_units).astype(jnp.bfloat16)
    ffn_part = jnp.dot(hidden_act, wide_down, preferred_element_type=jnp.float32)
    output = (
        resid_one
        + lax.psum_scatter(
            ffn_part.astype(jnp.bfloat16), "mp", scatter_dimension=0, tiled=True
        ).astype(jnp.float32)
    ).astype(jnp.bfloat16)
    cot_all = lax.all_gather(cotangent, "mp", axis=0, tiled=True)
    hidden_grad = jnp.einsum("td,sd->ts", cot_all, wide_down, preferred_element_type=jnp.float32)
    pre_grad = (gelu_back(pre_act, hidden_grad) * keep_units).astype(jnp.bfloat16)
    grad_up = jnp.einsum("td,ts->ds", inputs_two, pre_grad, preferred_element_type=jnp.float32)
    grad_down = jnp.einsum("ts,td->sd", hidden_act, cot_all, preferred_element_type=jnp.float32)
    ffn_back_part = jnp.einsum("ts,ds->td", pre_grad, wide_up, preferred_element_type=jnp.float32)
    normed_two_grad = lax.psum_scatter(
        ffn_back_part.astype(jnp.bfloat16), "mp", scatter_dimension=0, tiled=True
    ).astype(jnp.float32)
    resid_grad = cotangent.astype(jnp.float32) + norm_backward(
        normed_two_grad, unit_two, inverse_two, ln2_gain
    )
    gain_two_grad = jnp.sum(normed_two_grad * unit_two, axis=0)
    bias_two_grad = jnp.sum(normed_two_grad, axis=0)
    resid_all = lax.all_gather(resid_grad.astype(jnp.bfloat16), "mp", axis=0, tiled=True)
    grad_out = jnp.einsum("th,td->hd", mixed_heads, resid_all, preferred_element_type=jnp.float32)
    mixed_grad = jnp.einsum(
        "td,hd->th", resid_all, wide_out, preferred_element_type=jnp.float32
    ).astype(jnp.bfloat16)
    mixed_grad = mixed_grad.reshape(total_rows, local_heads, HDIM)

    def attend_back(running, block_index):
        key_sum, value_sum = running
        row_start = block_index * block_rows
        scores, query_block = block_scores(row_start)
        log_block = lax.dynamic_index_in_dim(log_totals, block_index, 0, keepdims=False)
        soft_float = jnp.exp(scores - log_block[..., None])
        grad_block = lax.dynamic_slice_in_dim(mixed_grad, row_start, block_rows, 0)
        prob_grad = jnp.einsum(
            "qhd,khd->hqk", grad_block, values_all, preferred_element_type=jnp.float32
        )
        score_grad = (
            soft_float * (prob_grad - jnp.sum(soft_float * prob_grad, axis=-1, keepdims=True))
        ).astype(jnp.bfloat16)
        query_grad = score_scale * jnp.einsum(
            "hqk,khd->qhd", score_grad, keys_rot, preferred_element_type=jnp.float32
        )
        key_sum = key_sum + score_scale * jnp.einsum(
            "hqk,qhd->khd", score_grad, query_block, preferred_element_type=jnp.float32
        )
        value_sum = value_sum + jnp.einsum(
            "hqk,qhd->khd",
            soft_float.astype(jnp.bfloat16),
            grad_block,
            preferred_element_type=jnp.float32,
        )
        return ((key_sum, value_sum), query_grad)

    zero_heads = jnp.zeros((total_rows, local_heads, HDIM), jnp.float32)
    (key_grad, value_grad), query_grads = lax.scan(
        attend_back, (zero_heads, zero_heads), jnp.arange(block_count, dtype=jnp.int32)
    )
    query_grad_all = query_grads.reshape(total_rows, local_heads, HDIM)
    projected_grad = jnp.stack(
        [
            rotate(query_grad_all, cosine, -sine).reshape(total_rows, head_width),
            rotate(key_grad, cosine, -sine).reshape(total_rows, head_width),
            value_grad.reshape(total_rows, head_width),
        ],
        axis=1,
    ).astype(jnp.bfloat16)
    grad_qkv = jnp.einsum(
        "td,tch->dch", inputs_one, projected_grad, preferred_element_type=jnp.float32
    )
    attn_back_part = jnp.einsum(
        "tch,dch->td", projected_grad, wide_qkv, preferred_element_type=jnp.float32
    )
    normed_one_grad = lax.psum_scatter(
        attn_back_part.astype(jnp.bfloat16), "mp", scatter_dimension=0, tiled=True
    ).astype(jnp.float32)
    input_grad = (
        resid_grad + norm_backward(normed_one_grad, unit_one, inverse_one, ln1_gain)
    ).astype(jnp.bfloat16)
    gain_one_grad = jnp.sum(normed_one_grad * unit_one, axis=0)
    bias_one_grad = jnp.sum(normed_one_grad, axis=0)
    norm_sums = lax.psum((gain_one_grad, bias_one_grad, gain_two_grad, bias_two_grad), ("dp", "mp"))
    grad_qkv_shard, grad_up_shard, grad_out_shard, grad_down_shard = (
        lax.psum_scatter(grad_qkv, "dp", scatter_dimension=0, tiled=True),
        lax.psum_scatter(grad_up, "dp", scatter_dimension=0, tiled=True),
        lax.psum_scatter(grad_out, "dp", scatter_dimension=0, tiled=True),
        lax.psum_scatter(grad_down, "dp", scatter_dimension=0, tiled=True),
    )
    return (
        output,
        input_grad,
        norm_sums[0],
        norm_sums[1],
        grad_qkv_shard,
        grad_out_shard,
        norm_sums[2],
        norm_sums[3],
        grad_up_shard,
        grad_down_shard,
    )


def solution(mesh):
    return jax.shard_map(
        on_device,
        mesh=mesh,
        in_specs=(
            P(("dp", "mp"), None),
            P(("dp", "mp"), None),
            P("dp", None),
            P("dp"),
            P(),
            P(),
            P("dp", None, "mp"),
            P(("mp", "dp"), None),
            P(),
            P(),
            P("dp", "mp"),
            P(("mp", "dp"), None),
        ),
        out_specs=(
            P(("dp", "mp"), None),
            P(("dp", "mp"), None),
            P(),
            P(),
            P("dp", None, "mp"),
            P(("mp", "dp"), None),
            P(),
            P(),
            P("dp", "mp"),
            P(("mp", "dp"), None),
        ),
        check_vma=False,
    )
```

profile of v0, /device:TPU:1, one launch (start us, length us, event | category | flops | bytes accessed | tf_op | source)
XLA Modules:
  0.0 1038.9 jit_solution(4531013267683974176)
XLA Ops:
  10.1 2.4 fusion.62
  14.4 3.2 fusion.76
  17.6 60.6 %all-gather.9.cloned.1.call-done = bf16[1024,1536]{1,0:T(8,128)(2,1)} async-done(((bf16[256,1536]{1,0:T(8,128)(2,1)}), bf16[1024,1536]{1,0:T(8,128)(2,1)}) %all-gather.9.cloned.1.call-update) | async-done | bytes 3145744 | tf_op jit(solution)/shard_map/all_gather | solution.py:107
  78.2 35.0 %all-gather.11.cloned.1.call-done = bf16[1536,3,384]{2,0,1:T(8,128)(2,1)} async-done(((bf16[192,3,384]{2,0,1:T(8,128)(2,1)}), bf16[1536,3,384]{2,0,1:T(8,128)(2,1)}) %all-gather.11.cloned.1.call-update) | async-done | bytes 3538960 | tf_op jit(solution)/shard_map/all_gather | solution.py:89
  113.2 7.0 fusion.49
  124.7 3.0 copy.86
  127.7 3.0 subtract_convert_fusion.2
  131.8 15.6 %while.28 = (s32[]{:T(128)}, bf16[2,512,3,128]{3,1,2,0:T(8,128)(2,1)S(1)}, f32[2,3,512]{2,1,0:T(4,128)S(1)}, s32[2]{0:T(128)S(1)}, s32[1024]{0:T(1024)S(1)}, /*i...) while((s32[]{:T(128)}, ...), condition=%wide.region_8.9_spmd.clone, body=%wide.region_5.8_spmd.clone.sunk | while | flops 825752576 | bytes 23797964 | solution.py:137
  135.1 1.9 fusion.134
  137.0 2.6 fusion.135
  144.8 2.6 fusion.135
  148.3 2.8 copy.56
  152.1 5.0 convolution_convert_fusion.2
  159.1 57.8 %reduce-scatter.9.cloned.1.call-done = bf16[256,1536]{1,0:T(8,128)(2,1)} async-done(((bf16[1024,1536]{1,0:T(8,128)(2,1)}), bf16[256,1536]{1,0:T(8,128)(2,1)}) %reduce-scatter.9.cloned.1.call-update) | async-done | bytes 786448 | tf_op jit(solution)/shard_map/reduce_scatter | solution.py:140
  222.1 60.0 %all-gather.21.cloned.1.call-done = bf16[1024,1536]{1,0:T(8,128)(2,1)} async-done(((bf16[256,1536]{1,0:T(8,128)(2,1)}), bf16[1024,1536]{1,0:T(8,128)(2,1)}) %all-gather.21.cloned.1.call-update) | async-done | bytes 3145744 | tf_op jit(solution)/shard_map/all_gather | solution.py:157
  282.0 39.8 %all-gather.19.cloned.1.call-done = bf16[1536,1536]{1,0:T(8,128)(2,1)} async-done(((bf16[192,1536]{1,0:T(8,128)(2,1)}), bf16[1536,1536]{1,0:T(8,128)(2,1)}) %all-gather.19.cloned.1.call-update) | async-done | bytes 4718608 | tf_op jit(solution)/shard_map/all_gather | solution.py:92
  321.8 9.8 fusion.84
  331.6 31.1 %all-gather.17.cloned.1.call-done = bf16[1536,1536]{1,0:T(8,128)(2,1)} async-done(((bf16[192,1536]{1,0:T(8,128)(2,1)}), bf16[1536,1536]{1,0:T(8,128)(2,1)}) %all-gather.17.cloned.1.call-update) | async-done | bytes 4718608 | tf_op jit(solution)/shard_map/all_gather | solution.py:90
  362.7 65.2 %all-gather.15.cloned.1.call-done = bf16[1024,1536]{1,0:T(8,128)(2,1)} async-done(((bf16[256,1536]{1,0:T(8,128)(2,1)}), bf16[1024,1536]{1,0:T(8,128)(2,1)}) %all-gather.15.cloned.1.call-update) | async-done | bytes 3145744 | tf_op jit(solution)/shard_map/all_gather | solution.py:144
  427.9 13.7 %fusion.46 = (bf16[1024,1536]{1,0:T(8,128)(2,1)S(1)}, f32[1024,1536]{1,0:T(8,128)}) fusion(f32[1024,1536]{1,0:T(8,128)} %fusion.84, f32[1536]{0:T(1024)S(1)} %fusion.77, bf16[1024,1536]{1,0:T(8,128)(2,1)} %all-gather.15.cloned.1.call-done, bf16[1536,1536]{1,0:T(8,128)(2,1)} %all-gather.17.cloned.1.call-done), kind=kOutput, calls=%fused_computation.58 | convolution fusion | flops 4864868352 | bytes 23599104 | tf_op jit(solution)/shard_map/dot_general | solution.py:148
  443.3 6.5 convolution_convert_fusion
  449.8 58.9 %reduce-scatter.13.cloned.1.call-done = bf16[256,1536]{1,0:T(8,128)(2,1)} async-done(((bf16[1024,1536]{1,0:T(8,128)(2,1)}), bf16[256,1536]{1,0:T(8,128)(2,1)}) %reduce-scatter.13.cloned.1.call-update) | async-done | bytes 786448 | tf_op jit(solution)/shard_map/reduce_scatter | solution.py:163
  508.7 2.7 fusion.73
  513.5 63.5 %all-gather.23.cloned.1.call-done = bf16[1024,1536]{1,0:T(8,128)(2,1)} async-done(((bf16[256,1536]{1,0:T(8,128)(2,1)}), bf16[1024,1536]{1,0:T(8,128)(2,1)}) %all-gather.23.cloned.1.call-update) | async-done | bytes 3145744 | tf_op jit(solution)/shard_map/all_gather | solution.py:171
  577.1 4.5 convolution_convert_fusion.3
  581.6 32.5 %while.29 = (s32[]{:T(128)}, f32[1024,3,128]{0,2,1:T(8,128)S(1)}, f32[1024,3,128]{0,2,1:T(8,128)}, f32[2,512,3,128]{3,1,0,2:T(8,128)}, s32[2]{0:T(128)S(1)}, /*i...) while((s32[]{:T(128)}, f32[1024,3,128]{0,2,1:T(8,128)S(1)}, ...), condition=%wide.region_18.19_spmd.clone, body=%wide.region_16.18_spmd.clone.sunk | while | flops 2040593408 | bytes 91812304 | solution.py:206
  587.0 2.2 bitcast_add_fusion.5
  589.3 3.0 multiply_reduce_fusion.3
  592.3 1.9 multiply_convert_fusion.5
  603.3 2.3 bitcast_add_fusion.5
  605.5 3.0 multiply_reduce_fusion.3
  608.6 1.9 multiply_convert_fusion.5
  617.2 3.3 subtract_convert_fusion.1
  624.2 7.8 bitcast_convert_fusion
  632.2 10.3 convolution_convert_fusion.1
  642.5 10.1 fusion.86
  652.7 10.9 %fusion.82 = f32[1536,1536]{1,0:T(8,128)} fusion(bf16[1024,1536]{1,0:T(8,128)(2,1)} %all-gather.21.cloned.1.call-done, f32[1024,1536]{1,0:T(8,128)} %get-tuple-element.298, f32[1536]{0:T(1024)S(1)} %fusion.77), kind=kOutput, calls=%fused_computation.145 | convolution fusion | flops 4847566848 | bytes 18880512 | tf_op jit(solution)/shard_map/ts,td->sd/dot_general | solution.py:161
  664.8 4.7 fusion.85
  669.8 9.1 fusion.47
  679.1 12.0 %reduce-scatter.15.cloned.1.call-done = bf16[256,1536]{1,0:T(8,128)(2,1)} async-done(((bf16[1024,1536]{1,0:T(8,128)(2,1)}), bf16[256,1536]{1,0:T(8,128)(2,1)}) %reduce-scatter.15.cloned.1.call-update) | async-done | bytes 786448 | tf_op jit(solution)/shard_map/reduce_scatter | solution.py:224
  691.0 1.9 fusion.74
  693.0 45.7 %all-reduce = (f32[1536]{0:T(1024)}, f32[1536]{0:T(1024)}, f32[1536]{0:T(1024)}, f32[1536]{0:T(1024)}) all-reduce(f32[1536]{0:T(1024)S(1)} %get-tuple-element.226, f32[1536]{0:T(1024)S(1)} %get-tuple-element.231, f32[1536]{0:T(1024)S(1)} %copy-done.27, f32[1536]{0:T(1024)S(1)} %copy-done.28), channel_id=1, replica_groups=mesh['dp'=8,'mp'=4] {'dp','mp'}, use_global_device_ids=true, to_apply=%region_23.24 | all-reduce | flops 6144 | bytes 49152 | tf_op jit(solution)/shard_map/psum | solution.py:232
  738.7 15.8 %reduce-scatter.11.cloned.1.call-done = bf16[256,1536]{1,0:T(8,128)(2,1)} async-done(((bf16[1024,1536]{1,0:T(8,128)(2,1)}), bf16[256,1536]{1,0:T(8,128)(2,1)}) %reduce-scatter.11.cloned.1.call-update) | async-done | bytes 786448 | tf_op jit(solution)/shard_map/reduce_scatter | solution.py:153
  754.6 3.6 fusion.66
  758.2 77.2 %reduce-scatter.21.cloned.1.call-done = f32[192,1536]{1,0:T(8,128)} async-done(((f32[1536,1536]{1,0:T(8,128)}), f32[192,1536]{1,0:T(8,128)}) %reduce-scatter.21.cloned.1.call-update) | async-done | bytes 1179664 | tf_op jit(solution)/shard_map/reduce_scatter | solution.py:235
  835.3 80.4 %reduce-scatter.23.cloned.1.call-done = f32[192,1536]{1,0:T(8,128)} async-done(((f32[1536,1536]{1,0:T(8,128)}), f32[192,1536]{1,0:T(8,128)}) %reduce-scatter.23.cloned.1.call-update) | async-done | bytes 1179664 | tf_op jit(solution)/shard_map/reduce_scatter | solution.py:237
  915.8 46.3 %reduce-scatter.19.cloned.1.call-done = f32[48,1536]{1,0:T(8,128)} async-done(((f32[384,1536]{1,0:T(8,128)}), f32[48,1536]{1,0:T(8,128)}) %reduce-scatter.19.cloned.1.call-update) | async-done | bytes 294928 | tf_op jit(solution)/shard_map/reduce_scatter | solution.py:236
  962.1 69.9 %reduce-scatter.17.cloned.1.call-done = f32[192,3,384]{2,0,1:T(8,128)} async-done(((f32[1536,3,384]{2,0,1:T(8,128)}), f32[192,3,384]{2,0,1:T(8,128)}) %reduce-scatter.17.cloned.1.call-update) | async-done | bytes 884752 | tf_op jit(solution)/shard_map/reduce_scatter | solution.py:234
  (203 shorter events, 50.9 us)
Async XLA Ops:
  7.2 6.9 copy-start.41
  7.2 71.0 %all-gather.9.cloned.1.call-start = ((), (), s32[]{:S(2)}) async-start(), calls=%async_computation.8 | async-start | bytes 3932160 | tf_op jit(solution)/shard_map/all_gather | solution.py:107
  8.6 9.0 copy-start.29
  10.1 110.1 %copy-start.33 = (f32[256]{0:T(256)}, f32[256]{0:T(256)S(1)}, u32[]{:S(2)}) copy-start(f32[256]{0:T(256)S(1)} %add_rsqrt_fusion.1) | copy-start | bytes 3076
  12.5 100.7 %all-gather.11.cloned.1.call-start = ((), (), s32[]{:S(2)}) async-start(), calls=%async_computation.9 | async-start | bytes 3981312 | tf_op jit(solution)/shard_map/all_gather | solution.py:89
  13.2 138.9 %all-gather.13.cloned.1.call-start = ((), (), s32[]{:S(2)}) async-start(), calls=%async_computation.10 | async-start | bytes 1327104 | tf_op jit(solution)/shard_map/all_gather | solution.py:91
  14.0 202.9 %reduce-scatter.9.cloned.1.call-start = ((), (), s32[]{:S(2)}) async-start(), calls=%async_computation.11 | async-start | bytes 3932160 | tf_op jit(solution)/shard_map/reduce_scatter | solution.py:140
  123.0 4.7 copy-start.13
  123.0 4.6 copy-start.14
  148.3 8.8 copy-start.2
  157.1 59.9 %copy-start = (bf16[256,1536]{1,0:T(8,128)(2,1)S(1)}, bf16[256,1536]{1,0:T(8,128)(2,1)}, u32[]{:S(2)}) copy-start(bf16[256,1536]{1,0:T(8,128)(2,1)} %param.16) | copy-start | bytes 2359300
  157.1 124.9 %all-gather.21.cloned.1.call-start = ((), (), s32[]{:S(2)}) async-start(), calls=%async_computation.16 | async-start | bytes 3932160 | tf_op jit(solution)/shard_map/all_gather | solution.py:157
  157.7 62.3 %copy-start.22 = (f32[1536]{0:T(1024)S(1)}, f32[1536]{0:T(1024)}, u32[]{:S(2)}) copy-start(f32[1536]{0:T(1024)} %param.24) | copy-start | bytes 18436
  157.7 62.3 %copy-start.39 = (f32[1536]{0:T(1024)S(1)}, f32[1536]{0:T(1024)}, u32[]{:S(2)}) copy-start(f32[1536]{0:T(1024)} %param.25) | copy-start | bytes 18436
  157.7 164.1 %all-gather.19.cloned.1.call-start = ((), (), s32[]{:S(2)}) async-start(), calls=%async_computation.14 | async-start | bytes 5308416 | tf_op jit(solution)/shard_map/all_gather | solution.py:92
  158.3 204.4 %all-gather.17.cloned.1.call-start = ((), (), s32[]{:S(2)}) async-start(), calls=%async_computation.13 | async-start | bytes 5308416 | tf_op jit(solution)/shard_map/all_gather | solution.py:90
  159.0 268.8 %all-gather.15.cloned.1.call-start = ((), (), s32[]{:S(2)}) async-start(), calls=%async_computation.12 | async-start | bytes 3932160 | tf_op jit(solution)/shard_map/all_gather | solution.py:144
  216.9 3.1 copy-start.4
  218.4 293.0 %copy-start.25 = (f32[256]{0:T(256)}, f32[256]{0:T(256)S(1)}, u32[]{:S(2)}) copy-start(f32[256]{0:T(256)S(1)} %broadcast_multiply_fusion.4) | copy-start | bytes 3076
  220.0 291.4 %copy-start.31 = (f32[256]{0:T(256)}, f32[256]{0:T(256)S(1)}, u32[]{:S(2)}) copy-start(f32[256]{0:T(256)S(1)} %add_rsqrt_fusion) | copy-start | bytes 3076
  221.3 287.4 %reduce-scatter.13.cloned.1.call-start = ((), (), s32[]{:S(2)}) async-start(), calls=%async_computation.17 | async-start | bytes 3932160 | tf_op jit(solution)/shard_map/reduce_scatter | solution.py:163
  427.9 15.4 %copy-start.40 = (bf16[1536,1536]{1,0:T(8,128)(2,1)S(1)}, bf16[1536,1536]{1,0:T(8,128)(2,1)}, u32[]{:S(2)}) copy-start(bf16[1536,1536]{1,0:T(8,128)(2,1)} %all-gather.17.cloned.1.call-done) | copy-start | bytes 14155780
  449.8 127.3 %all-gather.23.cloned.1.call-start = ((), (), s32[]{:S(2)}) async-start(), calls=%async_computation.18 | async-start | bytes 3932160 | tf_op jit(solution)/shard_map/all_gather | solution.py:171
  508.7 2.7 copy-start.6
  508.7 2.7 copy-start.8
  513.3 177.8 %reduce-scatter.15.cloned.1.call-start = ((), (), s32[]{:S(2)}) async-start(), calls=%async_computation.19 | async-start | bytes 3932160 | tf_op jit(solution)/shard_map/reduce_scatter | solution.py:224
  589.3 3.1 copy-start.16
  603.3 2.3 copy-start.3
  605.5 3.1 copy-start.16
  632.1 122.4 %reduce-scatter.11.cloned.1.call-start = ((), (), s32[]{:S(2)}) async-start(), calls=%async_computation.15 | async-start | bytes 3932160 | tf_op jit(solution)/shard_map/reduce_scatter | solution.py:153
  642.4 192.9 %reduce-scatter.21.cloned.1.call-start = ((), (), s32[]{:S(2)}) async-start(), calls=%async_computation.22 | async-start | bytes 10616832 | tf_op jit(solution)/shard_map/reduce_scatter | solution.py:235
  652.7 263.1 %reduce-scatter.23.cloned.1.call-start = ((), (), s32[]{:S(2)}) async-start(), calls=%async_computation.23 | async-start | bytes 10616832 | tf_op jit(solution)/shard_map/reduce_scatter | solution.py:237
  663.7 298.4 %reduce-scatter.19.cloned.1.call-start = ((), (), s32[]{:S(2)}) async-start(), calls=%async_computation.21 | async-start | bytes 2654208 | tf_op jit(solution)/shard_map/reduce_scatter | solution.py:236
  669.5 362.5 %reduce-scatter.17.cloned.1.call-start = ((), (), s32[]{:S(2)}) async-start(), calls=%async_computation.20 | async-start | bytes 7962624 | tf_op jit(solution)/shard_map/reduce_scatter | solution.py:234
  678.9 12.1 %copy-start.1 = (bf16[256,1536]{1,0:T(8,128)(2,1)S(1)}, bf16[256,1536]{1,0:T(8,128)(2,1)}, u32[]{:S(2)}) copy-start(bf16[256,1536]{1,0:T(8,128)(2,1)} %param.16) | copy-start | bytes 2359300
  678.9 12.1 %copy-start.24 = (f32[1536]{0:T(1024)S(1)}, f32[1536]{0:T(1024)}, u32[]{:S(2)}) copy-start(f32[1536]{0:T(1024)} %param.20) | copy-start | bytes 18436
  678.9 12.1 %copy-start.30 = (f32[256]{0:T(256)S(1)}, f32[256]{0:T(256)}, u32[]{:S(2)}) copy-start(f32[256]{0:T(256)} %copy-done.29) | copy-start | bytes 3076
  678.9 12.1 %copy-start.34 = (f32[256]{0:T(256)S(1)}, f32[256]{0:T(256)}, u32[]{:S(2)}) copy-start(f32[256]{0:T(256)} %copy-done.33) | copy-start | bytes 3076
  678.9 14.1 %copy-start.27 = (f32[1536]{0:T(1024)S(1)}, f32[1536]{0:T(1024)}, u32[]{:S(2)}) copy-start(f32[1536]{0:T(1024)} %get-tuple-element.224) | copy-start | bytes 18436
  678.9 14.1 %copy-start.28 = (f32[1536]{0:T(1024)S(1)}, f32[1536]{0:T(1024)}, u32[]{:S(2)}) copy-start(f32[1536]{0:T(1024)} %get-tuple-element.230) | copy-start | bytes 18436
  678.9 75.6 %copy-start.5 = (bf16[256,1536]{1,0:T(8,128)(2,1)S(1)}, bf16[256,1536]{1,0:T(8,128)(2,1)}, u32[]{:S(2)}) copy-start(bf16[256,1536]{1,0:T(8,128)(2,1)} %reduce-scatter.9.cloned.1.call-done) | copy-start | bytes 2359300
  679.0 75.6 %copy-start.7 = (bf16[256,1536]{1,0:T(8,128)(2,1)S(1)}, bf16[256,1536]{1,0:T(8,128)(2,1)}, u32[]{:S(2)}) copy-start(bf16[256,1536]{1,0:T(8,128)(2,1)} %param.17) | copy-start | bytes 2359300
  679.0 75.6 %copy-start.9 = (bf16[256,1536]{1,0:T(8,128)(2,1)S(1)}, bf16[256,1536]{1,0:T(8,128)(2,1)}, u32[]{:S(2)}) copy-start(bf16[256,1536]{1,0:T(8,128)(2,1)} %reduce-scatter.13.cloned.1.call-done) | copy-start | bytes 2359300
  679.0 75.5 %copy-start.23 = (f32[1536]{0:T(1024)S(1)}, f32[1536]{0:T(1024)}, u32[]{:S(2)}) copy-start(f32[1536]{0:T(1024)} %param.24) | copy-start | bytes 18436
  679.0 75.5 %copy-start.26 = (f32[256]{0:T(256)S(1)}, f32[256]{0:T(256)}, u32[]{:S(2)}) copy-start(f32[256]{0:T(256)} %copy-done.25) | copy-start | bytes 3076
  679.0 75.5 %copy-start.32 = (f32[256]{0:T(256)S(1)}, f32[256]{0:T(256)}, u32[]{:S(2)}) copy-start(f32[256]{0:T(256)} %copy-done.31) | copy-start | bytes 3076
  679.0 75.5 %copy-start.36 = (f32[256]{0:T(256)S(1)}, f32[256]{0:T(256)}, u32[]{:S(2)}) copy-start(f32[256]{0:T(256)} %copy-done.35) | copy-start | bytes 3076
  679.0 75.5 %copy-start.38 = (f32[256]{0:T(256)S(1)}, f32[256]{0:T(256)}, u32[]{:S(2)}) copy-start(f32[256]{0:T(256)} %copy-done.37) | copy-start | bytes 3076
  (17 other events, 24.0 us)
Sparse Core Ops, SparseCore 0:
  12.6 65.5 all-gather.8
  80.1 33.0 all-gather.10
  115.1 24.0 all-gather.12
  157.2 59.6 reduce-scatter.8
  218.3 63.6 all-gather.20
  283.8 38.0 all-gather.18
  323.7 38.9 all-gather.16
  364.8 63.0 all-gather.14
  449.9 58.7 reduce-scatter.12
  513.4 63.6 all-gather.22
  632.2 58.7 reduce-scatter.14
  693.2 61.2 reduce-scatter.10
  758.6 76.7 reduce-scatter.20
  839.3 76.4 reduce-scatter.22
  919.6 42.4 reduce-scatter.18
  966.4 65.4 reduce-scatter.16
where the time goes:
time: 1050 us; the launch traced here: 1040 us
  waiting for transfers between devices  777 us (74%)
  matrix products  124 us (12%)
  blocking collectives  45.7 us (4%)
  other arithmetic  42.5 us (4%)
  local copies, waits for them, and re-layouts  26.8 us (3%)
  between operations  15.6 us (1%)
    reduce_scatter x1, waiting for transfers between devices, on_device(): lax.psum_scatter(grad_down, 'dp', scatter_dimension=0, tiled=True)  80.4 us
    reduce_scatter x1, waiting for transfers between devices, on_device(): lax.psum_scatter(grad_up, 'dp', scatter_dimension=0, tiled=True)  77.2 us
    reduce_scatter x1, waiting for transfers between devices, on_device(): lax.psum_scatter(grad_qkv, 'dp', scatter_dimension=0, tiled=True)  69.9 us
    all_gather x1, waiting for transfers between devices, on_device(): lax.all_gather(normed_two.astype(jnp.bfloat16), 'mp', axis=0, tiled=True)  65.2 us
    all_gather x1, waiting for transfers between devices, on_device(): lax.all_gather(resid_grad.astype(jnp.bfloat16), 'mp', axis=0, tiled=True)  63.5 us
    all_gather x1, waiting for transfers between devices, on_device(): lax.all_gather(normed_one.astype(jnp.bfloat16), 'mp', axis=0, tiled=True)  60.6 us
    all_gather x1, waiting for transfers between devices, on_device(): cot_all = lax.all_gather(cotangent, 'mp', axis=0, tiled=True)  60 us
    reduce_scatter x1, waiting for transfers between devices, on_device(): lax.psum_scatter(ffn_back_part.astype(jnp.bfloat16), 'mp', scatter_dimens...  58.9 us
  transfers between devices with their start and end apart: 16, of which 15 were waited for; matrix products, arithmetic and copies ran while one was open for 10% of the time, Pallas kernels for 0%

commit v1 on v0

v1 whole, which is shorter than its diff:
```python
import functools
import math

import jax
import jax.numpy as jnp
from jax import lax
from jax.experimental import pallas as pl
from jax.experimental.pallas import tpu as pltpu
from jax.sharding import PartitionSpec as P

HDIM = 128
PREFIX0 = 768
WINDOW = 512
EPSILON = 1e-05
MASKED = -1e30
AXES = ("dp", "mp")
F32 = jnp.float32
BF16 = jnp.bfloat16


def norm_forward(values, norm_gain, norm_bias):
    center = values - jnp.mean(values, axis=-1, keepdims=True)
    inverse = lax.rsqrt(jnp.mean(center * center, axis=-1, keepdims=True) + EPSILON)
    normalized = center * inverse
    return (normalized * norm_gain + norm_bias, normalized, inverse)


def norm_backward(upstream, normalized, inverse, norm_gain):
    scaled = upstream * norm_gain
    return inverse * (
        scaled
        - jnp.mean(scaled, axis=-1, keepdims=True)
        - normalized * jnp.mean(scaled * normalized, axis=-1, keepdims=True)
    )


def gelu_back(pre_values, upstream):
    return jax.vjp(lambda pre_value: jax.nn.gelu(pre_value, approximate=True), pre_values)[1](
        upstream
    )[0]


def dot_nt(left, right):
    return lax.dot_general(left, right, (((1,), (1,)), ((), ())), preferred_element_type=F32)


def dot_tn(left, right):
    return lax.dot_general(left, right, (((0,), (0,)), ((), ())), preferred_element_type=F32)


def dot_nn(left, right):
    return lax.dot_general(left, right, (((1,), (0,)), ((), ())), preferred_element_type=F32)


def key_range(block, rows):
    first = max(0, block * rows - (WINDOW - 1)) // rows
    return first * rows, (block + 1) * rows


def attend_kernel(heads, slots, index_ref, proj_ref, cos_ref, sin_ref, start_ref, mixed_ref, q_ref, k_ref, v_ref, lse_ref):
    index = index_ref[0]
    total = proj_ref.shape[0]
    rows = total // slots
    width = heads * HDIM
    for slot in range(slots):
        here = slice(slot * rows, (slot + 1) * rows)
        there = pl.ds(pl.multiple_of((index ^ slot) * rows, rows), rows)
        cosine, sine = cos_ref[here, :], sin_ref[here, :]
        for head in range(heads):
            for part, out in enumerate((q_ref, k_ref)):
                lane = part * width + head * HDIM
                value = proj_ref[here, lane : lane + HDIM]
                value = value * cosine + pltpu.roll(value, HDIM // 2, 1) * sine
                out[head, there, :] = value.astype(BF16)
            lane = 2 * width + head * HDIM
            v_ref[head, there, :] = proj_ref[here, lane : lane + HDIM].astype(BF16)
    for block in range(slots):
        low, high = key_range(block, rows)
        here = slice(block * rows, (block + 1) * rows)
        slot_rows = pl.ds(pl.multiple_of((index ^ block) * rows, rows), rows)
        query_place = block * rows + lax.broadcasted_iota(jnp.int32, (rows, high - low), 0)
        key_place = low + lax.broadcasted_iota(jnp.int32, (rows, high - low), 1)
        allowed = (key_place >= start_ref[slot_rows, :]) & (key_place <= query_place)
        for head in range(heads):
            scores = dot_nt(q_ref[head, here, :], k_ref[head, low:high, :]) * (HDIM**-0.5)
            scores = jnp.where(allowed, scores, MASKED)
            top = jnp.max(scores, axis=-1, keepdims=True)
            weights = jnp.exp(scores - top)
            mass = jnp.sum(weights, axis=-1, keepdims=True)
            weights = (weights / mass).astype(BF16)
            mixed = dot_nn(weights, v_ref[head, low:high, :])
            mixed_ref[slot_rows, head * HDIM : (head + 1) * HDIM] = mixed.astype(BF16)
            lse_ref[head, here, :] = top + jnp.log(mass)


def attend_back_kernel(
    heads, slots, index_ref, grad_ref, q_ref, k_ref, v_ref, lse_ref, cos_ref, sin_ref, start_ref, out_ref, dk_ref, dv_ref
):
    index = index_ref[0]
    total = grad_ref.shape[0]
    rows = total // slots
    width = heads * HDIM
    scale = HDIM**-0.5
    dk_ref[...] = jnp.zeros_like(dk_ref)
    dv_ref[...] = jnp.zeros_like(dv_ref)
    for block in range(slots):
        low, high = key_range(block, rows)
        here = slice(block * rows, (block + 1) * rows)
        slot_rows = pl.ds(pl.multiple_of((index ^ block) * rows, rows), rows)
        query_place = block * rows + lax.broadcasted_iota(jnp.int32, (rows, high - low), 0)
        key_place = low + lax.broadcasted_iota(jnp.int32, (rows, high - low), 1)
        allowed = (key_place >= start_ref[slot_rows, :]) & (key_place <= query_place)
        cosine, sine = cos_ref[slot_rows, :], sin_ref[slot_rows, :]
        for head in range(heads):
            query = q_ref[head, here, :]
            keys = k_ref[head, low:high, :]
            values = v_ref[head, low:high, :]
            grad = grad_ref[slot_rows, head * HDIM : (head + 1) * HDIM]
            scores = jnp.where(allowed, dot_nt(query, keys) * scale, MASKED)
            probs = jnp.exp(scores - lse_ref[head, here, :])
            prob_grad = dot_nt(grad, values)
            mean = jnp.sum(probs * prob_grad, axis=-1, keepdims=True)
            score_grad = (probs * (prob_grad - mean)).astype(BF16)
            query_grad = dot_nn(score_grad, keys) * scale
            query_grad = query_grad * cosine - pltpu.roll(query_grad, HDIM // 2, 1) * sine
            out_ref[slot_rows, head * HDIM : (head + 1) * HDIM] = query_grad.astype(BF16)
            dk_ref[head, low:high, :] += dot_tn(score_grad, query)
            dv_ref[head, low:high, :] += dot_tn(probs.astype(BF16), grad)
    for slot in range(slots):
        here = slice(slot * rows, (slot + 1) * rows)
        there = pl.ds(pl.multiple_of((index ^ slot) * rows, rows), rows)
        cosine, sine = cos_ref[here, :], sin_ref[here, :]
        for head in range(heads):
            key_grad = dk_ref[head, there, :] * scale
            key_grad = key_grad * cosine - pltpu.roll(key_grad, HDIM // 2, 1) * sine
            lane = width + head * HDIM
            out_ref[here, lane : lane + HDIM] = key_grad.astype(BF16)
            lane = 2 * width + head * HDIM
            out_ref[here, lane : lane + HDIM] = dv_ref[head, there, :].astype(BF16)


def vmem():
    return pl.BlockSpec(memory_space=pltpu.VMEM)


def attend(index, proj, cosine, sine, start, heads, slots):
    total = proj.shape[0]
    shape = jax.ShapeDtypeStruct
    return pl.pallas_call(
        functools.partial(attend_kernel, heads, slots),
        in_specs=[pl.BlockSpec(memory_space=pltpu.SMEM)] + [vmem()] * 4,
        out_specs=[vmem()] * 5,
        out_shape=[
            shape((total, heads * HDIM), BF16),
            shape((heads, total, HDIM), BF16),
            shape((heads, total, HDIM), BF16),
            shape((heads, total, HDIM), BF16),
            shape((heads, total, 1), F32),
        ],
        cost_estimate=pl.CostEstimate(flops=3 * 10**9, bytes_accessed=12 * 10**6, transcendentals=2 * 10**6),
        name="attend",
    )(index, proj, cosine, sine, start)


def attend_back(index, grad, q, k, v, lse, cosine, sine, start, heads, slots):
    total = grad.shape[0]
    return pl.pallas_call(
        functools.partial(attend_back_kernel, heads, slots),
        in_specs=[pl.BlockSpec(memory_space=pltpu.SMEM)] + [vmem()] * 8,
        out_specs=vmem(),
        out_shape=jax.ShapeDtypeStruct((total, 3 * heads * HDIM), BF16),
        scratch_shapes=[pltpu.VMEM((heads, total, HDIM), F32)] * 2,
        cost_estimate=pl.CostEstimate(flops=6 * 10**9, bytes_accessed=12 * 10**6, transcendentals=2 * 10**6),
        name="attend_back",
    )(index, grad, q, k, v, lse, cosine, sine, start)


class Layout:
    def __init__(self, dp_count, mp_count):
        self.dp_count, self.mp_count = dp_count, mp_count
        self.planes = dp_count // 2
        self.groups = [[2 * plane + c for plane in range(self.planes)] for c in range(2)]

    def permute(self, value, place):
        pairs = []
        for plane in range(self.planes):
            for c in range(2):
                for p in range(2):
                    for zl in range(2):
                        target = place(plane, c, p, zl)
                        pairs.append((self.number(plane, c, p, zl), self.number(*target)))
        return lax.ppermute(value, AXES, pairs)

    def number(self, plane, c, p, zl):
        return (2 * plane + c) * self.mp_count + 2 * p + zl

    def swap(self, value):
        return self.permute(value, lambda plane, c, p, zl: (plane, p, c, zl))

    def swap_over(self, value):
        return self.permute(value, lambda plane, c, p, zl: (plane, p, 1 - c, zl))

    def swap_over_back(self, value):
        return self.permute(value, lambda plane, c, p, zl: (plane, 1 - p, c, zl))

    def core(self, value):
        return self.permute(value, lambda plane, c, p, zl: (plane, 1 - c, p, zl))

    def pair(self, value):
        return self.permute(value, lambda plane, c, p, zl: (plane, c, p, 1 - zl))

    def gather_weight(self, shard, p):
        one, two = self.swap(shard), self.swap_over(shard)
        both = jnp.where(p == 0, jnp.concatenate([one, two]), jnp.concatenate([two, one]))
        return lax.all_gather(both, "dp", axis=0, tiled=True, axis_index_groups=self.groups)

    def scatter_grad(self, grad, p):
        part = lax.psum_scatter(
            grad.astype(BF16), "dp", scatter_dimension=0, tiled=True, axis_index_groups=self.groups
        )
        half = part.shape[0] // 2
        first, second = part[:half], part[half:]
        mine = jnp.where(p == 0, first, second)
        other = jnp.where(p == 0, second, first)
        return self.swap(mine).astype(F32) + self.swap_over_back(other).astype(F32)


def on_device(
    tokens,
    cotangent,
    lengths,
    granularity,
    ln1_gain,
    ln1_bias,
    w_qkv,
    w_out,
    ln2_gain,
    ln2_bias,
    w_up,
    w_down,
):
    layout = Layout(lax.axis_size("dp"), lax.axis_size("mp"))
    slots = 4
    dp_index, mp_index = lax.axis_index("dp"), lax.axis_index("mp")
    c, p, zl = dp_index % 2, mp_index // 2, mp_index % 2
    index = 2 * c + zl
    rows = tokens.shape[0]
    total = slots * rows
    part_width = w_qkv.shape[2]
    heads = part_width // HDIM
    units = w_up.shape[1]

    facts = jnp.concatenate([lengths[0], granularity])
    facts = jnp.where(p == c, facts, layout.core(facts))
    piece_lengths, piece_gran = facts[:-1], facts[-1]

    wide_qkv = layout.gather_weight(w_qkv.reshape(w_qkv.shape[0], -1), p)
    moved_tokens = layout.swap(tokens)
    moved_cot = layout.swap(cotangent)
    wide_out = layout.gather_weight(w_out, p)
    wide_up = layout.gather_weight(w_up, p)
    wide_down = layout.gather_weight(w_down, p)

    slot_of = jnp.arange(total, dtype=jnp.int32) // rows
    places = (slot_of ^ index) * rows + jnp.arange(total, dtype=jnp.int32) % rows
    seg_ends = jnp.cumsum(piece_lengths)
    starts = seg_ends - piece_lengths
    seg_ids = jnp.sum((places[:, None] >= seg_ends[None, :]).astype(jnp.int32), axis=1)
    member = seg_ids[:, None] == jnp.arange(piece_lengths.shape[0], dtype=jnp.int32)[None, :]
    start = jnp.sum(jnp.where(member, starts[None, :], 0), axis=1)
    half = HDIM // 2
    frequencies = jnp.exp(jnp.arange(half, dtype=F32) * (-2.0 * math.log(10000.0) / HDIM))
    angles = (places - start).astype(F32)[:, None] * frequencies[None, :]
    cosine, sine = jnp.cos(angles), jnp.sin(angles)
    cosine = jnp.concatenate([cosine, cosine], axis=1)
    sine = jnp.concatenate([-sine, sine], axis=1)
    start = start[:, None]
    where = index[None]

    near_tokens = jnp.concatenate([moved_tokens, layout.pair(moved_tokens)]).astype(F32)
    near_one, unit_one, inverse_one = norm_forward(near_tokens, ln1_gain, ln1_bias)
    near_one = near_one.astype(BF16)
    inputs_one = jnp.concatenate([near_one, layout.core(near_one)])
    near_cot = jnp.concatenate([moved_cot, layout.pair(moved_cot)])
    cot_all = jnp.concatenate([near_cot, layout.core(near_cot)])

    projected = dot_nn(inputs_one, wide_qkv)
    mixed, q_all, k_all, v_all, lse = attend(where, projected, cosine, sine, start, heads, slots)

    def chip_sum(part):
        part = part.astype(F32)
        return part[: 2 * rows] + layout.core(part[2 * rows :].astype(BF16)).astype(F32)

    def pair_sum(chip):
        other = layout.pair(chip.astype(BF16)).astype(F32)
        return chip + jnp.concatenate([other[rows:], other[:rows]])

    def pair_own(chip):
        return chip[:rows] + layout.pair(chip[rows:].astype(BF16)).astype(F32)

    resid_one = near_tokens + pair_sum(chip_sum(dot_nn(mixed, wide_out)))
    near_two, unit_two, inverse_two = norm_forward(resid_one, ln2_gain, ln2_bias)
    near_two = near_two.astype(BF16)
    inputs_two = jnp.concatenate([near_two, layout.core(near_two)])

    prefix = PREFIX0 * jnp.left_shift(jnp.int32(1), piece_gran)
    active_units = jnp.clip(prefix - index * units, 0, units)
    keep_units = (jnp.arange(units, dtype=jnp.int32) < active_units).astype(F32)
    pre_act = dot_nn(inputs_two, wide_up)
    hidden_act = (jax.nn.gelu(pre_act, approximate=True) * keep_units).astype(BF16)
    hidden_grad = dot_nt(cot_all, wide_down)
    pre_grad = (gelu_back(pre_act, hidden_grad) * keep_units).astype(BF16)
    near_two_grad = pair_sum(chip_sum(dot_nt(pre_grad, wide_up)))

    output = resid_one[:rows] + pair_own(chip_sum(dot_nn(hidden_act, wide_down)))
    output = layout.swap(output.astype(BF16))
    grad_down = layout.scatter_grad(dot_tn(hidden_act, cot_all), p)
    grad_up = layout.scatter_grad(dot_tn(inputs_two, pre_grad), p)

    resid_grad = near_cot.astype(F32) + norm_backward(near_two_grad, unit_two, inverse_two, ln2_gain)
    gain_two_grad = jnp.sum(near_two_grad[:rows] * unit_two[:rows], axis=0)
    bias_two_grad = jnp.sum(near_two_grad[:rows], axis=0)
    resid_low = resid_grad.astype(BF16)
    resid_all = jnp.concatenate([resid_low, layout.core(resid_low)])
    mixed_grad = dot_nt(resid_all, wide_out).astype(BF16)
    grad_out = layout.scatter_grad(dot_tn(mixed, resid_all), p)
    projected_grad = attend_back(where, mixed_grad, q_all, k_all, v_all, lse, cosine, sine, start, heads, slots)
    own_one_grad = pair_own(chip_sum(dot_nt(projected_grad, wide_qkv)))
    grad_qkv = layout.scatter_grad(dot_tn(inputs_one, projected_grad), p)
    input_grad = resid_grad[:rows] + norm_backward(own_one_grad, unit_one[:rows], inverse_one[:rows], ln1_gain)
    input_grad = layout.swap(input_grad.astype(BF16))
    gain_one_grad = jnp.sum(own_one_grad * unit_one[:rows], axis=0)
    bias_one_grad = jnp.sum(own_one_grad, axis=0)
    norm_sums = lax.psum(jnp.stack([gain_one_grad, bias_one_grad, gain_two_grad, bias_two_grad]), AXES)
    return (
        output,
        input_grad,
        norm_sums[0],
        norm_sums[1],
        grad_qkv.reshape(w_qkv.shape),
        grad_out,
        norm_sums[2],
        norm_sums[3],
        grad_up,
        grad_down,
    )


def solution(mesh):
    return jax.shard_map(
        on_device,
        mesh=mesh,
        in_specs=(
            P(("dp", "mp"), None),
            P(("dp", "mp"), None),
            P("dp", None),
            P("dp"),
            P(),
            P(),
            P("dp", None, "mp"),
            P(("mp", "dp"), None),
            P(),
            P(),
            P("dp", "mp"),
            P(("mp", "dp"), None),
        ),
        out_specs=(
            P(("dp", "mp"), None),
            P(("dp", "mp"), None),
            P(),
            P(),
            P("dp", None, "mp"),
            P(("mp", "dp"), None),
            P(),
            P(),
            P("dp", "mp"),
            P(("mp", "dp"), None),
        ),
        check_vma=False,
    )
```

time: 1050 us -> 615 us (0.59)
  the two profiles are of different devices: /device:TPU:1 before, /device:TPU:0 now
where the time goes in v1:
time: 615 us; the launch traced here: 604 us
  waiting for transfers between devices  228 us (37%)
  starting transfers between devices  124 us (20%)
  matrix products  88.8 us (14%)
  other arithmetic  49.4 us (8%)
  blocking collectives  40 us (7%)
  local copies, waits for them, and re-layouts  32.4 us (5%)
  Pallas kernels  24.7 us (4%)
  between operations  16.6 us (3%)
    ppermute x35, waiting for transfers between devices, permute(): return lax.ppermute(value, AXES, pairs)  227 us
    ppermute x35, starting transfers between devices, permute(): return lax.ppermute(value, AXES, pairs)  124 us
    psum x1, blocking collectives, on_device(): lax.psum(jnp.stack([gain_one_grad, bias_one_grad, gain_two_grad, bias_two...  40 us
    dot_general x4, matrix products, dot_nn(): lax.dot_general(left, right, (((1,), (0,)), ((), ())), preferred_element_...  31.4 us
    dot_general x4, matrix products, dot_tn(): lax.dot_general(left, right, (((0,), (0,)), ((), ())), preferred_element_...  30.2 us
    dot_general x4, matrix products, dot_nt(): lax.dot_general(left, right, (((1,), (1,)), ((), ())), preferred_element_...  27.1 us
    unnamed x69, local copies, waits for them, and re-layouts  17.9 us
    pallas_call x1, Pallas kernels, attend_back(): pl.pallas_call(functools.partial(attend_back_kernel, heads, slots), in_sp...  13.7 us
  transfers between devices with their start and end apart: 43, of which 14 were waited for; matrix products, arithmetic and copies ran while one was open for 21% of the time, Pallas kernels for 4%

profile of v1, /device:TPU:0, one launch (start us, length us, event | category | flops | bytes accessed | tf_op | source)
XLA Modules:
  0.0 603.6 jit_solution(7009420161498936845)
XLA Ops:
  9.1 5.3 collective-permute-start.4
  14.5 9.9 %collective-permute-done.4 = bf16[192,1152]{1,0:T(8,128)(2,1)S(1)} collective-permute-done((bf16[192,1152]{1,0:T(8,128)(2,1)S(1)}, bf16[192,1152]{1,0:T(8,128)(2,1)S(1)}, u32[]{:S(2)}, u32[]{:S(2)}) %collective-permute-start.4) | collective-permute-done | bytes 442400 | tf_op jit(solution)/shard_map/ppermute | solution.py:192
  26.3 14.1 %collective-permute-start.7 = (bf16[48,1536]{1,0:T(8,128)(2,1)S(1)}, bf16[48,1536]{1,0:T(8,128)(2,1)S(1)}, u32[]{:S(2)}, u32[]{:S(2)}) collective-permute-start(bf16[48,1536]{1,0:T(8,128)(2,1)S(1)} %copy-done.28), channel_id=1, source_target_pairs={{0,2},{1,3},{2,6},{3,7},{4,0},{5,1},{6,4},{7,5},{8,10},{9,11},{10,... | collective-permute-start | bytes 442376 | tf_op jit(solution)/shard_map/ppermute | solution.py:192
  40.4 2.7 collective-permute-done.7
  44.7 8.2 %collective-permute-start.12 = (bf16[192,1536]{1,0:T(8,128)(2,1)S(1)}, bf16[192,1536]{1,0:T(8,128)(2,1)S(1)}, u32[]{:S(2)}, u32[]{:S(2)}) collective-permute-start(bf16[192,1536]{1,0:T(8,128)(2,1)S(1)} %copy-done.26), channel_id=1, source_target_pairs={{0,2},{1,3},{2,6},{3,7},{4,0},{5,1},{6,4},{7,5},{8,10},{9,11},{10,... | collective-permute-start | bytes 1769480 | tf_op jit(solution)/shard_map/ppermute | solution.py:192
  53.7 13.1 %collective-permute-done.12 = bf16[192,1536]{1,0:T(8,128)(2,1)S(1)} collective-permute-done((bf16[192,1536]{1,0:T(8,128)(2,1)S(1)}, bf16[192,1536]{1,0:T(8,128)(2,1)S(1)}, u32[]{:S(2)}, u32[]{:S(2)}) %collective-permute-start.12) | collective-permute-done | bytes 589856 | tf_op jit(solution)/shard_map/ppermute | solution.py:192
  68.2 19.3 %collective-permute-start.1 = (bf16[256,1536]{1,0:T(8,128)(2,1)S(1)}, bf16[256,1536]{1,0:T(8,128)(2,1)S(1)}, u32[]{:S(2)}, u32[]{:S(2)}) collective-permute-start(bf16[256,1536]{1,0:T(8,128)(2,1)S(1)} %collective-permute-done), channel_id=1, source_target_pairs={{0,1},{1,0},{2,3},{3,2},{4,5},{5,4},{6,7},{7,6},{8,9},{9,8},{10,11... | collective-permute-start | bytes 2359304 | tf_op jit(solution)/shard_map/ppermute | solution.py:192
  88.2 8.5 %collective-permute-start.5 = (s32[9]{0:T(128)S(1)}, s32[9]{0:T(128)S(1)}, u32[]{:S(2)}, u32[]{:S(2)}) collective-permute-start(s32[9]{0:T(128)S(1)} %pad_add_fusion), channel_id=1, source_target_pairs={{0,4},{1,5},{2,6},{3,7},{4,0},{5,1},{6,2},{7,3},{8,12},{9,13},{10,... | collective-permute-start | bytes 116 | tf_op jit(solution)/shard_map/ppermute | solution.py:192
  96.7 13.6 %collective-permute-done.1 = bf16[256,1536]{1,0:T(8,128)(2,1)S(1)} collective-permute-done((bf16[256,1536]{1,0:T(8,128)(2,1)S(1)}, bf16[256,1536]{1,0:T(8,128)(2,1)S(1)}, u32[]{:S(2)}, u32[]{:S(2)}) %collective-permute-start.1) | collective-permute-done | bytes 786464 | tf_op jit(solution)/shard_map/ppermute | solution.py:192
  113.5 2.8 collective-permute-start.2
  121.1 8.9 %fusion.13.proj_ref = f32[1024,1152]{1,0:T(8,128)} fusion(bf16[1536,1152]{1,0:T(8,128)(2,1)} %all-gather.5.cloned.1.call-done, bf16[512,1536]{1,0:T(8,128)(2,1)} %collective-permute-done.2, bf16[512,1536]{1,0:T(8,128)(2,1)S(1)} %get-tuple-element.70), kind=kOutput, calls=%fused_computation.43 | convolution fusion | flops 3630170112 | bytes 11403264 | tf_op jit(solution)/shard_map/dot_general | solution.py:52
  130.0 11.0 %attend.1 = (bf16[1024,384]{1,0:T(8,128)(2,1)}, bf16[3,1024,128]{2,1,0:T(8,128)(2,1)}, bf16[3,1024,128]{2,1,0:T(8,128)(2,1)}, bf16[3,1024,128]{2,1,0:T(8,128)(2,1)}, f32[3,1024,1]{2,1,0:T(8,128)}) custom-call(s32[1]{0:T(128)} %bitcast.index_ref, f32[1024,1152]{1,0:T(8,128)} %fusion.13.proj_ref, f32[1024,128]{1,0:T(8,128)} %get-tuple-element.90.cos_ref, ...), custom_call_target="tpu_custom_call" | custom-call | flops 3000000000 | bytes 12000000 | tf_op jit(solution)/shard_map/attend/pallas_call | solution.py:149
  141.1 3.3 fusion.45
  144.4 2.9 copy-done
  149.3 4.3 collective-permute-start.14
  153.6 7.4 %collective-permute-start.18 = (bf16[256,1536]{1,0:T(8,128)(2,1)}, bf16[256,1536]{1,0:T(8,128)(2,1)}, u32[]{:S(2)}, u32[]{:S(2)}) collective-permute-start(bf16[256,1536]{1,0:T(8,128)(2,1)} %param.13), channel_id=1, source_target_pairs={{0,0},{1,1},{2,4},{3,5},{4,2},{5,3},{6,6},{7,7},{8,8},{9,9},{10,12... | collective-permute-start | bytes 2359304 | tf_op jit(solution)/shard_map/ppermute | solution.py:192
  161.0 6.4 %collective-permute-done.14 = bf16[192,1536]{1,0:T(8,128)(2,1)S(1)} collective-permute-done((bf16[192,1536]{1,0:T(8,128)(2,1)S(1)}, bf16[192,1536]{1,0:T(8,128)(2,1)S(1)}, u32[]{:S(2)}, u32[]{:S(2)}) %collective-permute-start.14) | collective-permute-done | bytes 589856 | tf_op jit(solution)/shard_map/ppermute | solution.py:192
  168.8 2.5 fusion.14
  171.4 19.3 %collective-permute-start.9 = (bf16[512,1536]{1,0:T(8,128)(2,1)S(1)}, bf16[512,1536]{1,0:T(8,128)(2,1)S(1)}, u32[]{:S(2)}, u32[]{:S(2)}) collective-permute-start(bf16[512,1536]{1,0:T(8,128)(2,1)S(1)} %fusion.14), channel_id=1, source_target_pairs={{0,1},{1,0},{2,3},{3,2},{4,5},{5,4},{6,7},{7,6},{8,9},{9,8},{10,11... | collective-permute-start | bytes 4718600 | tf_op jit(solution)/shard_map/ppermute | solution.py:192
  192.9 53.3 %collective-permute-done.19 = bf16[256,1536]{1,0:T(8,128)(2,1)S(1)} collective-permute-done((bf16[256,1536]{1,0:T(8,128)(2,1)}, bf16[256,1536]{1,0:T(8,128)(2,1)S(1)}, u32[]{:S(2)}, u32[]{:S(2)}) %collective-permute-start.19) | collective-permute-done | bytes 786464 | tf_op jit(solution)/shard_map/ppermute | solution.py:192
  254.2 2.7 constant_dynamic-update-slice_fusion.2
  256.9 9.6 %fusion.12 = f32[1024,1536]{1,0:T(8,128)} fusion(bf16[1536,1536]{1,0:T(8,128)(2,1)} %all-gather.9.cloned.1.call-done, bf16[512,1536]{1,0:T(8,128)(2,1)} %collective-permute-done.10, bf16[512,1536]{1,0:T(8,128)(2,1)} %get-tuple-element.65), kind=kOutput, calls=%fused_computation.42 | convolution fusion | flops 4838129664 | bytes 14155776 | tf_op jit(solution)/shard_map/dot_general | solution.py:52
  266.5 12.0 %fusion.7 = bf16[1024,1536]{1,0:T(8,128)(2,1)S(1)} fusion(f32[1024,1536]{1,0:T(8,128)} %fusion.12, f32[1536]{0:T(1024)S(1)} %fusion.26, bf16[1024,1536]{1,0:T(8,128)(2,1)} %constant_dynamic-update-slice_fusion.2, bf16[1536,1536]{1,0:T(8,128)(2,1)} %all-gather.11.cloned.1.call-done), kind=kOutput, calls=%fused_computation.12 | convolution fusion | flops 4864868352 | bytes 17307648 | tf_op jit(solution)/shard_map/dot_general | solution.py:44
  280.1 5.1 fusion.46
  285.8 3.0 collective-permute-done.21
  289.4 36.7 %collective-permute-done.22 = bf16[512,1536]{1,0:T(8,128)(2,1)S(1)} collective-permute-done((bf16[512,1536]{1,0:T(8,128)(2,1)S(1)}, bf16[512,1536]{1,0:T(8,128)(2,1)S(1)}, u32[]{:S(2)}, u32[]{:S(2)}) %collective-permute-start.22) | collective-permute-done | bytes 1572896 | tf_op jit(solution)/shard_map/ppermute | solution.py:192
  327.5 5.1 fusion.41
  332.6 3.4 collective-permute-done.23
  337.2 2.4 convolution_convert_fusion.3
  339.7 10.4 %convolution_convert_fusion = bf16[1536,1536]{1,0:T(8,128)(2,1)} fusion(bf16[1024,1536]{1,0:T(8,128)(2,1)} %constant_dynamic-update-slice_fusion.2, f32[1024,1536]{1,0:T(8,128)} %fusion.12, f32[1536]{0:T(1024)S(1)} %fusion.26), kind=kOutput, calls=%fused_computation.2 | convolution fusion | flops 4849926144 | bytes 14161920 | tf_op jit(solution)/shard_map/dot_general | solution.py:48
  350.1 9.4 %convolution_convert_fusion.1 = bf16[1536,1536]{1,0:T(8,128)(2,1)} fusion(bf16[1024,1536]{1,0:T(8,128)(2,1)} %copy-done.30, bf16[512,1536]{1,0:T(8,128)(2,1)} %collective-permute-done.10, bf16[512,1536]{1,0:T(8,128)(2,1)} %get-tuple-element.65), kind=kOutput, calls=%fused_computation.3 | convolution fusion | flops 4840488960 | bytes 11010048 | tf_op jit(solution)/shard_map/dot_general | solution.py:48
  359.5 9.6 %fusion.40 = f32[1024,1536]{1,0:T(8,128)S(1)} fusion(bf16[1536,1536]{1,0:T(8,128)(2,1)} %all-gather.11.cloned.1.call-done, f32[1024,1536]{1,0:T(8,128)} %fusion.12, f32[1536]{0:T(1024)S(1)} %fusion.26), kind=kOutput, calls=%fused_computation.134 | convolution fusion | flops 4847566848 | bytes 17307648 | tf_op jit(solution)/shard_map/dot_general | solution.py:52
  373.0 2.7 fusion.20.grad_ref
  375.6 13.7 %attend_back.1 = bf16[1024,1152]{1,0:T(8,128)(2,1)} custom-call(s32[1]{0:T(128)} %bitcast.index_ref, bf16[1024,384]{1,0:T(8,128)(2,1)} %fusion.20.grad_ref, bf16[3,1024,128]{2,1,0:T(8,128)(2,1)} %get-tuple-element.16.q_ref, bf16[3,1024,128]{2,1,0:T(8,128)(2,1)} %get-tuple-element.17.k_ref, bf16[3,1024,128]{2,1,0:T(8,128)(2,1)} %get-tuple-element.18.v_ref, ...), custom_call_target="tpu_custom_call" | custom-call | flops 6000000000 | bytes 12000000 | tf_op jit(solution)/shard_map/attend_back/pallas_call | solution.py:167
  389.3 7.4 %fusion.47 = f32[1024,1536]{1,0:T(8,128)S(1)} fusion(bf16[1024,1152]{1,0:T(8,128)(2,1)} %attend_back.1, bf16[1536,1152]{1,0:T(8,128)(2,1)} %all-gather.5.cloned.1.call-done), kind=kOutput, calls=%fused_computation.141 | convolution fusion | flops 3623878656 | bytes 12189696 | tf_op jit(solution)/shard_map/dot_general | solution.py:44
  396.7 2.6 copy-done.8
  401.1 8.1 %convolution_convert_fusion.2 = bf16[1536,1152]{1,0:T(8,128)(2,1)} fusion(bf16[1024,1152]{1,0:T(8,128)(2,1)S(1)} %copy-done.29, bf16[512,1536]{1,0:T(8,128)(2,1)} %collective-permute-done.2, bf16[512,1536]{1,0:T(8,128)(2,1)S(1)} %copy-done.10), kind=kOutput, calls=%fused_computation.4 | convolution fusion | flops 3631939584 | bytes 9043968 | tf_op jit(solution)/shard_map/dot_general | solution.py:48
  409.2 3.2 slice_add_fusion.2
  412.6 20.0 %collective-permute-done.16 = bf16[256,1536]{1,0:T(8,128)(2,1)S(1)} collective-permute-done((bf16[256,1536]{1,0:T(8,128)(2,1)S(1)}, bf16[256,1536]{1,0:T(8,128)(2,1)S(1)}, u32[]{:S(2)}, u32[]{:S(2)}) %collective-permute-start.16) | collective-permute-done | bytes 786464 | tf_op jit(solution)/shard_map/ppermute | solution.py:192
  434.7 2.8 slice_add_fusion
  442.8 16.7 %collective-permute-start.30 = (bf16[48,1536]{1,0:T(8,128)(2,1)S(1)}, bf16[48,1536]{1,0:T(8,128)(2,1)}, u32[]{:S(2)}, u32[]{:S(2)}) collective-permute-start(bf16[48,1536]{1,0:T(8,128)(2,1)S(1)} %get-tuple-element.86), channel_id=1, source_target_pairs={{0,4},{1,5},{2,0},{3,1},{4,6},{5,7},{6,2},{7,3},{8,12},{9,13},{10,... | collective-permute-start | bytes 442376 | tf_op jit(solution)/shard_map/ppermute | solution.py:192
  459.5 7.3 %collective-permute-done.25 = bf16[256,1536]{1,0:T(8,128)(2,1)} collective-permute-done((bf16[256,1536]{1,0:T(8,128)(2,1)}, bf16[256,1536]{1,0:T(8,128)(2,1)}, u32[]{:S(2)}, u32[]{:S(2)}) %collective-permute-start.25) | collective-permute-done | bytes 786464 | tf_op jit(solution)/shard_map/ppermute | solution.py:192
  466.8 2.8 multiply_reduce_fusion.3
  469.6 3.6 fusion.17
  475.1 40.0 %psum.7 = f32[4,1536]{1,0:T(4,128)S(1)} all-reduce(f32[4,1536]{1,0:T(4,128)S(1)} %pad_maximum_fusion.14), channel_id=1, replica_groups=mesh['dp'=8,'mp'=4] {'dp','mp'}, use_global_device_ids=true, to_apply=%region_15.16 | all-reduce | flops 6144 | bytes 49152 | tf_op jit(solution)/shard_map/psum | solution.py:334
  526.7 34.1 %collective-permute-done.34 = bf16[192,1536]{1,0:T(8,128)(2,1)} collective-permute-done((bf16[192,1536]{1,0:T(8,128)(2,1)S(1)}, bf16[192,1536]{1,0:T(8,128)(2,1)}, u32[]{:S(2)}, u32[]{:S(2)}) %collective-permute-start.34) | collective-permute-done | bytes 589856 | tf_op jit(solution)/shard_map/ppermute | solution.py:192
  566.0 16.9 %collective-permute-done.32 = bf16[192,1536]{1,0:T(8,128)(2,1)} collective-permute-done((bf16[192,1536]{1,0:T(8,128)(2,1)S(1)}, bf16[192,1536]{1,0:T(8,128)(2,1)}, u32[]{:S(2)}, u32[]{:S(2)}) %collective-permute-start.32) | collective-permute-done | bytes 589856 | tf_op jit(solution)/shard_map/ppermute | solution.py:192
  585.4 7.0 %collective-permute-done.28 = bf16[192,1152]{1,0:T(8,128)(2,1)S(1)} collective-permute-done((bf16[192,1152]{1,0:T(8,128)(2,1)S(1)}, bf16[192,1152]{1,0:T(8,128)(2,1)S(1)}, u32[]{:S(2)}, u32[]{:S(2)}) %collective-permute-start.28) | collective-permute-done | bytes 442400 | tf_op jit(solution)/shard_map/ppermute | solution.py:192
  (202 shorter events, 72.0 us)
Async XLA Ops:
  7.2 113.9 %all-gather.5.cloned.1.call-start = ((), (), s32[]{:S(2)}) async-start(), calls=%async_computation.4 | async-start | bytes 4423680 | tf_op jit(solution)/shard_map/all_gather | solution.py:215
  8.4 6.0 collective-permute-start.3
  9.1 15.3 %collective-permute-start.4 = (bf16[192,1152]{1,0:T(8,128)(2,1)S(1)}, bf16[192,1152]{1,0:T(8,128)(2,1)S(1)}, u32[]{:S(2)}, u32[]{:S(2)}) collective-permute-start(bf16[192,1152]{1,0:T(8,128)(2,1)S(1)} %bitcast.36), channel_id=1, source_target_pairs={{0,2},{1,3},{2,6},{3,7},{4,0},{5,1},{6,4},{7,5},{8,10},{9,11},{10,... | collective-permute-start | bytes 1327112 | tf_op jit(solution)/shard_map/ppermute | solution.py:192
  14.4 73.7 %copy-start.21 = (s32[1,8]{1,0:T(1,128)S(1)}, s32[1,8]{1,0:T(1,128)}, u32[]{:S(2)}) copy-start(s32[1,8]{1,0:T(1,128)} %param.14) | copy-start | bytes 100
  25.6 115.5 %all-gather.7.cloned.1.call-start = ((), (), s32[]{:S(2)}) async-start(), calls=%async_computation.5 | async-start | bytes 1474560 | tf_op jit(solution)/shard_map/all_gather | solution.py:215
  25.6 14.8 %collective-permute-start.6 = (bf16[48,1536]{1,0:T(8,128)(2,1)S(1)}, bf16[48,1536]{1,0:T(8,128)(2,1)S(1)}, u32[]{:S(2)}, u32[]{:S(2)}) collective-permute-start(bf16[48,1536]{1,0:T(8,128)(2,1)S(1)} %copy-done.28), channel_id=1, source_target_pairs={{0,0},{1,1},{2,4},{3,5},{4,2},{5,3},{6,6},{7,7},{8,8},{9,9},{10,12... | collective-permute-start | bytes 442376 | tf_op jit(solution)/shard_map/ppermute | solution.py:192
  26.3 16.8 %collective-permute-start.7 = (bf16[48,1536]{1,0:T(8,128)(2,1)S(1)}, bf16[48,1536]{1,0:T(8,128)(2,1)S(1)}, u32[]{:S(2)}, u32[]{:S(2)}) collective-permute-start(bf16[48,1536]{1,0:T(8,128)(2,1)S(1)} %copy-done.28), channel_id=1, source_target_pairs={{0,2},{1,3},{2,6},{3,7},{4,0},{5,1},{6,4},{7,5},{8,10},{9,11},{10,... | collective-permute-start | bytes 442376 | tf_op jit(solution)/shard_map/ppermute | solution.py:192
  43.9 67.2 %copy-start.17 = (f32[1536]{0:T(1024)S(1)}, f32[1536]{0:T(1024)}, u32[]{:S(2)}) copy-start(f32[1536]{0:T(1024)} %param.16) | copy-start | bytes 18436
  44.0 67.2 %copy-start.19 = (f32[1536]{0:T(1024)S(1)}, f32[1536]{0:T(1024)}, u32[]{:S(2)}) copy-start(f32[1536]{0:T(1024)} %param.17) | copy-start | bytes 18436
  44.0 212.9 %all-gather.9.cloned.1.call-start = ((), (), s32[]{:S(2)}) async-start(), calls=%async_computation.6 | async-start | bytes 5898240 | tf_op jit(solution)/shard_map/all_gather | solution.py:215
  44.0 9.6 %collective-permute-start.11 = (bf16[192,1536]{1,0:T(8,128)(2,1)S(1)}, bf16[192,1536]{1,0:T(8,128)(2,1)S(1)}, u32[]{:S(2)}, u32[]{:S(2)}) collective-permute-start(bf16[192,1536]{1,0:T(8,128)(2,1)S(1)} %copy-done.26), channel_id=1, source_target_pairs={{0,0},{1,1},{2,4},{3,5},{4,2},{5,3},{6,6},{7,7},{8,8},{9,9},{10,12... | collective-permute-start | bytes 1769480 | tf_op jit(solution)/shard_map/ppermute | solution.py:192
  44.7 22.0 %collective-permute-start.12 = (bf16[192,1536]{1,0:T(8,128)(2,1)S(1)}, bf16[192,1536]{1,0:T(8,128)(2,1)S(1)}, u32[]{:S(2)}, u32[]{:S(2)}) collective-permute-start(bf16[192,1536]{1,0:T(8,128)(2,1)S(1)} %copy-done.26), channel_id=1, source_target_pairs={{0,2},{1,3},{2,6},{3,7},{4,0},{5,1},{6,4},{7,5},{8,10},{9,11},{10,... | collective-permute-start | bytes 1769480 | tf_op jit(solution)/shard_map/ppermute | solution.py:192
  52.9 15.3 %collective-permute-start = (bf16[256,1536]{1,0:T(8,128)(2,1)S(1)}, bf16[256,1536]{1,0:T(8,128)(2,1)S(1)}, u32[]{:S(2)}, u32[]{:S(2)}) collective-permute-start(bf16[256,1536]{1,0:T(8,128)(2,1)S(1)} %copy-done.25), channel_id=1, source_target_pairs={{0,0},{1,1},{2,4},{3,5},{4,2},{5,3},{6,6},{7,7},{8,8},{9,9},{10,12... | collective-permute-start | bytes 2359304 | tf_op jit(solution)/shard_map/ppermute | solution.py:192
  68.2 198.3 %all-gather.11.cloned.1.call-start = ((), (), s32[]{:S(2)}) async-start(), calls=%async_computation.7 | async-start | bytes 5898240 | tf_op jit(solution)/shard_map/all_gather | solution.py:215
  68.2 42.1 %collective-permute-start.1 = (bf16[256,1536]{1,0:T(8,128)(2,1)S(1)}, bf16[256,1536]{1,0:T(8,128)(2,1)S(1)}, u32[]{:S(2)}, u32[]{:S(2)}) collective-permute-start(bf16[256,1536]{1,0:T(8,128)(2,1)S(1)} %collective-permute-done), channel_id=1, source_target_pairs={{0,1},{1,0},{2,3},{3,2},{4,5},{5,4},{6,7},{7,6},{8,9},{9,8},{10,11... | collective-permute-start | bytes 2359304 | tf_op jit(solution)/shard_map/ppermute | solution.py:192
  88.2 28.1 %collective-permute-start.5 = (s32[9]{0:T(128)S(1)}, s32[9]{0:T(128)S(1)}, u32[]{:S(2)}, u32[]{:S(2)}) collective-permute-start(s32[9]{0:T(128)S(1)} %pad_add_fusion), channel_id=1, source_target_pairs={{0,4},{1,5},{2,6},{3,7},{4,0},{5,1},{6,2},{7,3},{8,12},{9,13},{10,... | collective-permute-start | bytes 116 | tf_op jit(solution)/shard_map/ppermute | solution.py:192
  111.2 327.6 %copy-start.18 = (f32[512]{0:T(512)}, f32[512]{0:T(512)S(1)}, u32[]{:S(2)}) copy-start(f32[512]{0:T(512)S(1)} %add_rsqrt_fusion.1) | copy-start | bytes 6148
  113.5 7.6 %collective-permute-start.2 = (bf16[512,1536]{1,0:T(8,128)(2,1)S(1)}, bf16[512,1536]{1,0:T(8,128)(2,1)}, u32[]{:S(2)}, u32[]{:S(2)}) collective-permute-start(bf16[512,1536]{1,0:T(8,128)(2,1)S(1)} %get-tuple-element.70), channel_id=1, source_target_pairs={{0,4},{1,5},{2,6},{3,7},{4,0},{5,1},{6,2},{7,3},{8,12},{9,13},{10,... | collective-permute-start | bytes 4718600 | tf_op jit(solution)/shard_map/ppermute | solution.py:192
  148.6 20.3 %collective-permute-start.8 = (bf16[512,1536]{1,0:T(8,128)(2,1)}, bf16[512,1536]{1,0:T(8,128)(2,1)S(1)}, u32[]{:S(2)}, u32[]{:S(2)}) collective-permute-start(bf16[512,1536]{1,0:T(8,128)(2,1)} %slice.257), channel_id=1, source_target_pairs={{0,4},{1,5},{2,6},{3,7},{4,0},{5,1},{6,2},{7,3},{8,12},{9,13},{10,... | collective-permute-start | bytes 4718600 | tf_op jit(solution)/shard_map/ppermute | solution.py:192
  148.6 12.4 %collective-permute-start.13 = (bf16[192,1536]{1,0:T(8,128)(2,1)S(1)}, bf16[192,1536]{1,0:T(8,128)(2,1)S(1)}, u32[]{:S(2)}, u32[]{:S(2)}) collective-permute-start(bf16[192,1536]{1,0:T(8,128)(2,1)S(1)} %copy-done.27), channel_id=1, source_target_pairs={{0,0},{1,1},{2,4},{3,5},{4,2},{5,3},{6,6},{7,7},{8,8},{9,9},{10,12... | collective-permute-start | bytes 1769480 | tf_op jit(solution)/shard_map/ppermute | solution.py:192
  149.3 18.1 %collective-permute-start.14 = (bf16[192,1536]{1,0:T(8,128)(2,1)S(1)}, bf16[192,1536]{1,0:T(8,128)(2,1)S(1)}, u32[]{:S(2)}, u32[]{:S(2)}) collective-permute-start(bf16[192,1536]{1,0:T(8,128)(2,1)S(1)} %copy-done.27), channel_id=1, source_target_pairs={{0,2},{1,3},{2,6},{3,7},{4,0},{5,1},{6,4},{7,5},{8,10},{9,11},{10,... | collective-permute-start | bytes 1769480 | tf_op jit(solution)/shard_map/ppermute | solution.py:192
  153.6 37.1 %collective-permute-start.18 = (bf16[256,1536]{1,0:T(8,128)(2,1)}, bf16[256,1536]{1,0:T(8,128)(2,1)}, u32[]{:S(2)}, u32[]{:S(2)}) collective-permute-start(bf16[256,1536]{1,0:T(8,128)(2,1)} %param.13), channel_id=1, source_target_pairs={{0,0},{1,1},{2,4},{3,5},{4,2},{5,3},{6,6},{7,7},{8,8},{9,9},{10,12... | collective-permute-start | bytes 2359304 | tf_op jit(solution)/shard_map/ppermute | solution.py:192
  168.8 270.7 %reduce-scatter.7.cloned.1.call-start = ((), (), s32[]{:S(2)}) async-start(), calls=%async_computation.9 | async-start | bytes 1474560 | tf_op jit(solution)/shard_map/reduce_scatter | solution.py:218
  168.8 80.5 %slice-start = ((s8[6291456]{0:T(1024)(128)(4,1)}), s8[4194304]{0:T(1024)(128)(4,1)S(1)}, s32[]{:S(2)}) async-start(s8[6291456]{0:T(1024)(128)(4,1)} %bitcast.30), calls=%async_computation.12 | async-start | bytes 8388608
  171.4 77.5 %collective-permute-start.9 = (bf16[512,1536]{1,0:T(8,128)(2,1)S(1)}, bf16[512,1536]{1,0:T(8,128)(2,1)S(1)}, u32[]{:S(2)}, u32[]{:S(2)}) collective-permute-start(bf16[512,1536]{1,0:T(8,128)(2,1)S(1)} %fusion.14), channel_id=1, source_target_pairs={{0,1},{1,0},{2,3},{3,2},{4,5},{5,4},{6,7},{7,6},{8,9},{9,8},{10,11... | collective-permute-start | bytes 4718600 | tf_op jit(solution)/shard_map/ppermute | solution.py:192
  190.7 55.5 %collective-permute-start.19 = (bf16[256,1536]{1,0:T(8,128)(2,1)}, bf16[256,1536]{1,0:T(8,128)(2,1)S(1)}, u32[]{:S(2)}, u32[]{:S(2)}) collective-permute-start(bf16[256,1536]{1,0:T(8,128)(2,1)} %collective-permute-done.18), channel_id=1, source_target_pairs={{0,1},{1,0},{2,3},{3,2},{4,5},{5,4},{6,7},{7,6},{8,9},{9,8},{10,11... | collective-permute-start | bytes 2359304 | tf_op jit(solution)/shard_map/ppermute | solution.py:192
  247.2 7.0 %collective-permute-start.20 = (bf16[512,1536]{1,0:T(8,128)(2,1)}, bf16[512,1536]{1,0:T(8,128)(2,1)}, u32[]{:S(2)}, u32[]{:S(2)}) collective-permute-start(bf16[512,1536]{1,0:T(8,128)(2,1)} %get-tuple-element.81), channel_id=1, source_target_pairs={{0,4},{1,5},{2,6},{3,7},{4,0},{5,1},{6,2},{7,3},{8,12},{9,13},{10,... | collective-permute-start | bytes 4718600 | tf_op jit(solution)/shard_map/ppermute | solution.py:192
  252.8 4.0 collective-permute-start.10
  285.3 3.5 collective-permute-start.21
  289.3 36.7 %collective-permute-start.22 = (bf16[512,1536]{1,0:T(8,128)(2,1)S(1)}, bf16[512,1536]{1,0:T(8,128)(2,1)S(1)}, u32[]{:S(2)}, u32[]{:S(2)}) collective-permute-start(bf16[512,1536]{1,0:T(8,128)(2,1)S(1)} %fusion.15), channel_id=1, source_target_pairs={{0,1},{1,0},{2,3},{3,2},{4,5},{5,4},{6,7},{7,6},{8,9},{9,8},{10,11... | collective-permute-start | bytes 4718600 | tf_op jit(solution)/shard_map/ppermute | solution.py:192
  332.6 3.4 collective-permute-start.23
  339.6 176.2 %reduce-scatter.11.cloned.1.call-start = ((), (), s32[]{:S(2)}) async-start(), calls=%async_computation.11 | async-start | bytes 5898240 | tf_op jit(solution)/shard_map/reduce_scatter | solution.py:218
  350.0 171.5 %reduce-scatter.9.cloned.1.call-start = ((), (), s32[]{:S(2)}) async-start(), calls=%async_computation.10 | async-start | bytes 5898240 | tf_op jit(solution)/shard_map/reduce_scatter | solution.py:218
  359.5 203.8 %reduce-scatter.5.cloned.1.call-start = ((), (), s32[]{:S(2)}) async-start(), calls=%async_computation.8 | async-start | bytes 4423680 | tf_op jit(solution)/shard_map/reduce_scatter | solution.py:218
  370.6 38.6 %collective-permute-start.15 = (bf16[512,1536]{1,0:T(8,128)(2,1)}, bf16[512,1536]{1,0:T(8,128)(2,1)}, u32[]{:S(2)}, u32[]{:S(2)}) collective-permute-start(bf16[512,1536]{1,0:T(8,128)(2,1)} %slice.256), channel_id=1, source_target_pairs={{0,4},{1,5},{2,6},{3,7},{4,0},{5,1},{6,2},{7,3},{8,12},{9,13},{10,... | collective-permute-start | bytes 4718600 | tf_op jit(solution)/shard_map/ppermute | solution.py:192
  401.0 33.7 %collective-permute-start.24 = (bf16[512,1536]{1,0:T(8,128)(2,1)}, bf16[512,1536]{1,0:T(8,128)(2,1)}, u32[]{:S(2)}, u32[]{:S(2)}) collective-permute-start(bf16[512,1536]{1,0:T(8,128)(2,1)} %slice.254), channel_id=1, source_target_pairs={{0,4},{1,5},{2,6},{3,7},{4,0},{5,1},{6,2},{7,3},{8,12},{9,13},{10,... | collective-permute-start | bytes 4718600 | tf_op jit(solution)/shard_map/ppermute | solution.py:192
  412.5 20.1 %collective-permute-start.16 = (bf16[256,1536]{1,0:T(8,128)(2,1)S(1)}, bf16[256,1536]{1,0:T(8,128)(2,1)S(1)}, u32[]{:S(2)}, u32[]{:S(2)}) collective-permute-start(bf16[256,1536]{1,0:T(8,128)(2,1)S(1)} %slice.259), channel_id=1, source_target_pairs={{0,1},{1,0},{2,3},{3,2},{4,5},{5,4},{6,7},{7,6},{8,9},{9,8},{10,11... | collective-permute-start | bytes 2359304 | tf_op jit(solution)/shard_map/ppermute | solution.py:192
  433.0 6.4 %collective-permute-start.17 = (bf16[256,1536]{1,0:T(8,128)(2,1)S(1)}, bf16[256,1536]{1,0:T(8,128)(2,1)}, u32[]{:S(2)}, u32[]{:S(2)}) collective-permute-start(bf16[256,1536]{1,0:T(8,128)(2,1)S(1)} %fusion.19), channel_id=1, source_target_pairs={{0,0},{1,1},{2,4},{3,5},{4,2},{5,3},{6,6},{7,7},{8,8},{9,9},{10,12... | collective-permute-start | bytes 2359304 | tf_op jit(solution)/shard_map/ppermute | solution.py:192
  438.5 28.2 %collective-permute-start.25 = (bf16[256,1536]{1,0:T(8,128)(2,1)}, bf16[256,1536]{1,0:T(8,128)(2,1)}, u32[]{:S(2)}, u32[]{:S(2)}) collective-permute-start(bf16[256,1536]{1,0:T(8,128)(2,1)} %slice.258), channel_id=1, source_target_pairs={{0,1},{1,0},{2,3},{3,2},{4,5},{5,4},{6,7},{7,6},{8,9},{9,8},{10,11... | collective-permute-start | bytes 2359304 | tf_op jit(solution)/shard_map/ppermute | solution.py:192
  441.3 78.6 %collective-permute-start.29 = (bf16[48,1536]{1,0:T(8,128)(2,1)}, bf16[48,1536]{1,0:T(8,128)(2,1)S(1)}, u32[]{:S(2)}, u32[]{:S(2)}) collective-permute-start(bf16[48,1536]{1,0:T(8,128)(2,1)} %get-tuple-element.85), channel_id=1, source_target_pairs={{0,0},{1,1},{2,4},{3,5},{4,2},{5,3},{6,6},{7,7},{8,8},{9,9},{10,12... | collective-permute-start | bytes 442376 | tf_op jit(solution)/shard_map/ppermute | solution.py:192
  442.8 77.1 %collective-permute-start.30 = (bf16[48,1536]{1,0:T(8,128)(2,1)S(1)}, bf16[48,1536]{1,0:T(8,128)(2,1)}, u32[]{:S(2)}, u32[]{:S(2)}) collective-permute-start(bf16[48,1536]{1,0:T(8,128)(2,1)S(1)} %get-tuple-element.86), channel_id=1, source_target_pairs={{0,4},{1,5},{2,0},{3,1},{4,6},{5,7},{6,2},{7,3},{8,12},{9,13},{10,... | collective-permute-start | bytes 442376 | tf_op jit(solution)/shard_map/ppermute | solution.py:192
  473.3 48.3 %collective-permute-start.26 = (bf16[256,1536]{1,0:T(8,128)(2,1)}, bf16[256,1536]{1,0:T(8,128)(2,1)S(1)}, u32[]{:S(2)}, u32[]{:S(2)}) collective-permute-start(bf16[256,1536]{1,0:T(8,128)(2,1)} %fusion.17), channel_id=1, source_target_pairs={{0,0},{1,1},{2,4},{3,5},{4,2},{5,3},{6,6},{7,7},{8,8},{9,9},{10,12... | collective-permute-start | bytes 2359304 | tf_op jit(solution)/shard_map/ppermute | solution.py:192
  517.2 9.6 %collective-permute-start.33 = (bf16[192,1536]{1,0:T(8,128)(2,1)S(1)}, bf16[192,1536]{1,0:T(8,128)(2,1)}, u32[]{:S(2)}, u32[]{:S(2)}) collective-permute-start(bf16[192,1536]{1,0:T(8,128)(2,1)S(1)} %get-tuple-element.75), channel_id=1, source_target_pairs={{0,0},{1,1},{2,4},{3,5},{4,2},{5,3},{6,6},{7,7},{8,8},{9,9},{10,12... | collective-permute-start | bytes 1769480 | tf_op jit(solution)/shard_map/ppermute | solution.py:192
  518.6 42.2 %collective-permute-start.34 = (bf16[192,1536]{1,0:T(8,128)(2,1)S(1)}, bf16[192,1536]{1,0:T(8,128)(2,1)}, u32[]{:S(2)}, u32[]{:S(2)}) collective-permute-start(bf16[192,1536]{1,0:T(8,128)(2,1)S(1)} %get-tuple-element.76), channel_id=1, source_target_pairs={{0,4},{1,5},{2,0},{3,1},{4,6},{5,7},{6,2},{7,3},{8,12},{9,13},{10,... | collective-permute-start | bytes 1769480 | tf_op jit(solution)/shard_map/ppermute | solution.py:192
  522.9 43.1 %collective-permute-start.31 = (bf16[192,1536]{1,0:T(8,128)(2,1)S(1)}, bf16[192,1536]{1,0:T(8,128)(2,1)}, u32[]{:S(2)}, u32[]{:S(2)}) collective-permute-start(bf16[192,1536]{1,0:T(8,128)(2,1)S(1)} %get-tuple-element.77), channel_id=1, source_target_pairs={{0,0},{1,1},{2,4},{3,5},{4,2},{5,3},{6,6},{7,7},{8,8},{9,9},{10,12... | collective-permute-start | bytes 1769480 | tf_op jit(solution)/shard_map/ppermute | solution.py:192
  524.4 58.6 %collective-permute-start.32 = (bf16[192,1536]{1,0:T(8,128)(2,1)S(1)}, bf16[192,1536]{1,0:T(8,128)(2,1)}, u32[]{:S(2)}, u32[]{:S(2)}) collective-permute-start(bf16[192,1536]{1,0:T(8,128)(2,1)S(1)} %get-tuple-element.78), channel_id=1, source_target_pairs={{0,4},{1,5},{2,0},{3,1},{4,6},{5,7},{6,2},{7,3},{8,12},{9,13},{10,... | collective-permute-start | bytes 1769480 | tf_op jit(solution)/shard_map/ppermute | solution.py:192
  564.5 20.9 %collective-permute-start.27 = (bf16[192,1152]{1,0:T(8,128)(2,1)S(1)}, bf16[192,1152]{1,0:T(8,128)(2,1)S(1)}, u32[]{:S(2)}, u32[]{:S(2)}) collective-permute-start(bf16[192,1152]{1,0:T(8,128)(2,1)S(1)} %get-tuple-element.79), channel_id=1, source_target_pairs={{0,0},{1,1},{2,4},{3,5},{4,2},{5,3},{6,6},{7,7},{8,8},{9,9},{10,12... | collective-permute-start | bytes 1327112 | tf_op jit(solution)/shard_map/ppermute | solution.py:192
  565.2 27.1 %collective-permute-start.28 = (bf16[192,1152]{1,0:T(8,128)(2,1)S(1)}, bf16[192,1152]{1,0:T(8,128)(2,1)S(1)}, u32[]{:S(2)}, u32[]{:S(2)}) collective-permute-start(bf16[192,1152]{1,0:T(8,128)(2,1)S(1)} %get-tuple-element.80), channel_id=1, source_target_pairs={{0,4},{1,5},{2,0},{3,1},{4,6},{5,7},{6,2},{7,3},{8,12},{9,13},{10,... | collective-permute-start | bytes 1327112 | tf_op jit(solution)/shard_map/ppermute | solution.py:192
  (29 other events, 297.5 us)
Sparse Core Ops, SparseCore 0:
  25.7 58.6 all-gather.4
  86.8 27.7 all-gather.6
  116.9 57.1 all-gather.8
  176.4 69.0 all-gather.10
  339.7 28.0 reduce-scatter.6
  370.7 57.0 reduce-scatter.10
  430.8 57.6 reduce-scatter.8
  491.5 47.9 reduce-scatter.4

commit v2 on v1

--- a/solution.py
+++ b/solution.py
@@ -200,8 +200,31 @@
     def swap_over(self, value):
         return self.permute(value, lambda plane, c, p, zl: (plane, p, 1 - c, zl))
 
-    def swap_over_back(self, value):
-        return self.permute(value, lambda plane, c, p, zl: (plane, 1 - p, c, zl))
+    def send_shard(self, shard):
+        return self.swap(shard), self.swap_over(shard)
+
+    def line_up(self, shards, p):
+        one, two = shards
+        return jnp.where(p == 0, jnp.concatenate([one, two]), jnp.concatenate([two, one]))
+
+    def sum_all(self, value):
+        value = value + self.core(value)
+        value = value + self.pair(value)
+        value = value + self.permute(value, lambda plane, c, p, zl: (plane, c, 1 - p, zl))
+        step = 1
+        while step < self.planes:
+            value = value + self.plane_step(value, step)
+            step *= 2
+        return value
+
+    def flip(self, value, into):
+        pairs = []
+        for plane in range(self.planes):
+            for c in range(2):
+                for zl in range(2):
+                    near, far = self.number(plane, c, c, zl), self.number(plane, c, 1 - c, zl)
+                    pairs.append((far, near) if into else (near, far))
+        return lax.ppermute(value, AXES, pairs)
 
     def core(self, value):
         return self.permute(value, lambda plane, c, p, zl: (plane, 1 - c, p, zl))
@@ -209,20 +232,99 @@
     def pair(self, value):
         return self.permute(value, lambda plane, c, p, zl: (plane, c, p, 1 - zl))
 
-    def gather_weight(self, shard, p):
-        one, two = self.swap(shard), self.swap_over(shard)
-        both = jnp.where(p == 0, jnp.concatenate([one, two]), jnp.concatenate([two, one]))
-        return lax.all_gather(both, "dp", axis=0, tiled=True, axis_index_groups=self.groups)
-
-    def scatter_grad(self, grad, p):
-        part = lax.psum_scatter(
-            grad.astype(BF16), "dp", scatter_dimension=0, tiled=True, axis_index_groups=self.groups
+    def plane_step(self, value, flip):
+        return self.permute(value, lambda plane, c, p, zl: (plane ^ flip, c, p, zl))
+
+    def both(self, shard, other, c):
+        return jnp.where(c == 0, jnp.concatenate([shard, other]), jnp.concatenate([other, shard]))
+
+    def gather(self, block):
+        return lax.all_gather(block, "dp", axis=0, tiled=True, axis_index_groups=self.groups)
+
+    def gather_near(self, block):
+        if self.planes != 4:
+            return (self.gather(block),)
+        return block, self.plane_step(block, 1), self.plane_step(block, 2)
+
+    def far_sends(self, pieces):
+        if self.planes != 4:
+            return ()
+        half = pieces[0].shape[0] // 2
+        return pieces[1][:half], pieces[2][half:]
+
+    def gather_far(self, pieces, sends):
+        if self.planes != 4:
+            return pieces
+        return *pieces, self.plane_step(sends[0], 2), self.plane_step(sends[1], 1)
+
+    def assemble(self, pieces, plane):
+        if self.planes != 4:
+            return pieces[0]
+        block, across, along, far_one, far_two = pieces
+        rows = block.shape[0]
+        whole = jnp.zeros((4 * rows, block.shape[1]), block.dtype)
+        put = lambda whole, piece, place: lax.dynamic_update_slice(whole, piece, (place, 0))
+        whole = put(whole, block, plane * rows)
+        whole = put(whole, across, (plane ^ 1) * rows)
+        whole = put(whole, along, (plane ^ 2) * rows)
+        whole = put(whole, far_one, (plane ^ 3) * rows)
+        return put(whole, far_two, (plane ^ 3) * rows + rows // 2)
+
+    def scatter(self, grad):
+        return lax.psum_scatter(grad, "dp", scatter_dimension=0, tiled=True, axis_index_groups=self.groups)
+
+    def near_sends(self, grad, plane):
+        if self.planes != 4:
+            return ()
+        rows = grad.shape[0] // 4
+        half = rows // 2
+        take = lambda place: lax.dynamic_slice(grad, (place, 0), (half, grad.shape[1]))
+        return take((plane ^ 3) * rows), take((plane ^ 3) * rows + half)
+
+    def scatter_near(self, grad, sends):
+        if self.planes != 4:
+            return self.scatter(grad)
+        return self.plane_step(sends[0], 1), self.plane_step(sends[1], 2)
+
+    def later_sends(self, grad, got, plane):
+        if self.planes != 4:
+            return ()
+        rows = grad.shape[0] // 4
+        half = rows // 2
+        take = lambda place, count: lax.dynamic_slice(grad, (place, 0), (count, grad.shape[1]))
+        add = lambda left, right: (left.astype(F32) + right.astype(F32)).astype(BF16)
+        to_across = jnp.concatenate(
+            [take((plane ^ 1) * rows, half), add(take((plane ^ 1) * rows + half, half), got[1])]
         )
-        half = part.shape[0] // 2
-        first, second = part[:half], part[half:]
-        mine = jnp.where(p == 0, first, second)
-        other = jnp.where(p == 0, second, first)
-        return self.swap(mine).astype(F32) + self.swap_over_back(other).astype(F32)
+        to_along = jnp.concatenate(
+            [add(take((plane ^ 2) * rows, half), got[0]), take((plane ^ 2) * rows + half, half)]
+        )
+        return to_across, to_along
+
+    def scatter_far(self, grad, got, sends, plane):
+        if self.planes != 4:
+            return got
+        rows = grad.shape[0] // 4
+        mine = lax.dynamic_slice(grad, (plane * rows, 0), (rows, grad.shape[1]))
+        return mine, self.plane_step(sends[0], 1), self.plane_step(sends[1], 2)
+
+    def scatter_sum(self, parts):
+        if self.planes != 4:
+            return parts
+        return sum([part.astype(F32) for part in parts]).astype(BF16)
+
+    def own_shards(self, part, received, c):
+        whole = part.astype(F32) + received.astype(F32)
+        first, second = jnp.split(whole, 2)
+        return jnp.where(c == 0, first, second), jnp.where(c == 0, second, first)
+
+
+def hold(*values):
+    return lax.optimization_barrier(values)
+
+
+def after(value, *others):
+    return lax.optimization_barrier((value, others))[0]
 
 
 def on_device(
@@ -243,6 +345,7 @@
     slots = 4
     dp_index, mp_index = lax.axis_index("dp"), lax.axis_index("mp")
     c, p, zl = dp_index % 2, mp_index // 2, mp_index % 2
+    plane = dp_index // 2
     index = 2 * c + zl
     rows = tokens.shape[0]
     total = slots * rows
@@ -251,15 +354,19 @@
     units = w_up.shape[1]
 
     facts = jnp.concatenate([lengths[0], granularity])
-    facts = jnp.where(p == c, facts, layout.core(facts))
+    other_facts = layout.core(facts)
+    facts = jnp.where(p == c, facts, other_facts)
     piece_lengths, piece_gran = facts[:-1], facts[-1]
 
-    wide_qkv = layout.gather_weight(w_qkv.reshape(w_qkv.shape[0], -1), p)
-    moved_tokens = layout.swap(tokens)
-    moved_cot = layout.swap(cotangent)
-    wide_out = layout.gather_weight(w_out, p)
-    wide_up = layout.gather_weight(w_up, p)
-    wide_down = layout.gather_weight(w_down, p)
+    depth = w_qkv.shape[0]
+    w_qkv_flat, _ = hold(w_qkv.reshape(depth, -1), other_facts)
+    sent_qkv = layout.send_shard(w_qkv_flat)
+    block_qkv = layout.line_up(sent_qkv, p)
+    wide_qkv = layout.gather(block_qkv)
+    moved_tokens = layout.swap(after(tokens, block_qkv))
+    sent_out = layout.send_shard(after(w_out, block_qkv))
+    other_down = layout.core(after(w_down, block_qkv))
+    both_down = layout.both(w_down, other_down, c)
 
     slot_of = jnp.arange(total, dtype=jnp.int32) // rows
     places = (slot_of ^ index) * rows + jnp.arange(total, dtype=jnp.int32) % rows
@@ -277,61 +384,133 @@
     start = start[:, None]
     where = index[None]
 
-    near_tokens = jnp.concatenate([moved_tokens, layout.pair(moved_tokens)]).astype(F32)
+    moved_tokens, cosine, sine, start, both_down = hold(moved_tokens, cosine, sine, start, both_down)
+    pair_tokens = layout.pair(moved_tokens)
+    block_out = layout.line_up(after(sent_out, moved_tokens), p)
+    wide_out = layout.gather(block_out)
+    pair_tokens, block_out = hold(pair_tokens, block_out)
+    near_tokens = jnp.concatenate([moved_tokens, pair_tokens]).astype(F32)
     near_one, unit_one, inverse_one = norm_forward(near_tokens, ln1_gain, ln1_bias)
-    near_one = near_one.astype(BF16)
+    near_one, w_up = hold(near_one.astype(BF16), w_up)
+    sent_up = layout.send_shard(w_up)
     inputs_one = jnp.concatenate([near_one, layout.core(near_one)])
-    near_cot = jnp.concatenate([moved_cot, layout.pair(moved_cot)])
-    cot_all = jnp.concatenate([near_cot, layout.core(near_cot)])
-
     projected = dot_nn(inputs_one, wide_qkv)
+    projected, sent_up, both_down = hold(projected, sent_up, both_down)
+    block_up, projected, both_down = hold(layout.line_up(sent_up, p), projected, both_down)
+    pieces_up = layout.gather_near(block_up)
+    flip_down = layout.flip(both_down, False)
     mixed, q_all, k_all, v_all, lse = attend(where, projected, cosine, sine, start, heads, slots)
-
-    def chip_sum(part):
-        part = part.astype(F32)
-        return part[: 2 * rows] + layout.core(part[2 * rows :].astype(BF16)).astype(F32)
-
-    def pair_sum(chip):
-        other = layout.pair(chip.astype(BF16)).astype(F32)
-        return chip + jnp.concatenate([other[rows:], other[:rows]])
-
-    def pair_own(chip):
-        return chip[:rows] + layout.pair(chip[rows:].astype(BF16)).astype(F32)
-
-    resid_one = near_tokens + pair_sum(chip_sum(dot_nn(mixed, wide_out)))
+    attn_part = dot_nn(mixed, wide_out)
+    attn_send = attn_part[2 * rows :].astype(BF16)
+    attn_send, pieces_up, flip_down = hold(attn_send, pieces_up, flip_down)
+
+    attn_got = layout.core(attn_send)
+    block_down = jnp.where(p == c, both_down, flip_down)
+    sends_up = layout.far_sends(pieces_up)
+    attn_got, block_down, sends_up = hold(attn_got, block_down, sends_up)
+    wide_down = layout.gather(block_down)
+    attn_chip = attn_part[: 2 * rows] + attn_got.astype(F32)
+    attn_low, sends_up, cotangent = hold(attn_chip.astype(BF16), sends_up, cotangent)
+    attn_other = layout.pair(attn_low)
+    pieces_up = layout.gather_far(pieces_up, sends_up)
+    moved_cot = layout.swap(cotangent)
+    attn_other, pieces_up, moved_cot = hold(attn_other, pieces_up, moved_cot)
+
+    def pair_order(other):
+        other = other.astype(F32)
+        return jnp.concatenate([other[rows:], other[:rows]])
+
+    resid_one = near_tokens + attn_chip + pair_order(attn_other)
     near_two, unit_two, inverse_two = norm_forward(resid_one, ln2_gain, ln2_bias)
-    near_two = near_two.astype(BF16)
+    near_two, pieces_up, moved_cot = hold(near_two.astype(BF16), pieces_up, moved_cot)
+    pair_cot = layout.pair(moved_cot)
     inputs_two = jnp.concatenate([near_two, layout.core(near_two)])
+    wide_up = layout.assemble(pieces_up, plane)
 
     prefix = PREFIX0 * jnp.left_shift(jnp.int32(1), piece_gran)
     active_units = jnp.clip(prefix - index * units, 0, units)
     keep_units = (jnp.arange(units, dtype=jnp.int32) < active_units).astype(F32)
     pre_act = dot_nn(inputs_two, wide_up)
     hidden_act = (jax.nn.gelu(pre_act, approximate=True) * keep_units).astype(BF16)
+    hidden_act, pair_cot = hold(hidden_act, pair_cot)
+    near_cot = jnp.concatenate([moved_cot, pair_cot])
+    cot_all = jnp.concatenate([near_cot, layout.core(near_cot)])
+    grad_down_part = dot_tn(hidden_act, cot_all).astype(BF16)
+    grad_down_sum = layout.scatter(grad_down_part)
+    wide_down = after(wide_down, grad_down_part)
     hidden_grad = dot_nt(cot_all, wide_down)
     pre_grad = (gelu_back(pre_act, hidden_grad) * keep_units).astype(BF16)
-    near_two_grad = pair_sum(chip_sum(dot_nt(pre_grad, wide_up)))
-
-    output = resid_one[:rows] + pair_own(chip_sum(dot_nn(hidden_act, wide_down)))
-    output = layout.swap(output.astype(BF16))
-    grad_down = layout.scatter_grad(dot_tn(hidden_act, cot_all), p)
-    grad_up = layout.scatter_grad(dot_tn(inputs_two, pre_grad), p)
+    ffn_part = dot_nt(pre_grad, wide_up)
+    (ffn_send,) = hold(ffn_part[2 * rows :].astype(BF16))
+    (ffn_got,) = hold(layout.core(ffn_send))
+    ffn_chip = ffn_part[: 2 * rows] + ffn_got.astype(F32)
+    ffn_low, pre_grad, hidden_act = hold(ffn_chip.astype(BF16), pre_grad, hidden_act)
+    ffn_other = layout.pair(ffn_low)
+    grad_up_part = dot_tn(inputs_two, pre_grad).astype(BF16)
+    grad_up_sum = layout.scatter(grad_up_part)
+    out_part = dot_nn(hidden_act, wide_down)
+    out_send = out_part[2 * rows :].astype(BF16)
+    ffn_other, out_send, grad_up_part = hold(ffn_other, out_send, grad_up_part)
+    near_two_grad = ffn_chip + pair_order(ffn_other)
 
     resid_grad = near_cot.astype(F32) + norm_backward(near_two_grad, unit_two, inverse_two, ln2_gain)
     gain_two_grad = jnp.sum(near_two_grad[:rows] * unit_two[:rows], axis=0)
     bias_two_grad = jnp.sum(near_two_grad[:rows], axis=0)
     resid_low = resid_grad.astype(BF16)
+    resid_low, out_send, down_sum = hold(resid_low, out_send, grad_down_sum)
+    down_flip = layout.flip(down_sum, True)
+    out_got = layout.core(out_send)
     resid_all = jnp.concatenate([resid_low, layout.core(resid_low)])
     mixed_grad = dot_nt(resid_all, wide_out).astype(BF16)
-    grad_out = layout.scatter_grad(dot_tn(mixed, resid_all), p)
-    projected_grad = attend_back(where, mixed_grad, q_all, k_all, v_all, lse, cosine, sine, start, heads, slots)
-    own_one_grad = pair_own(chip_sum(dot_nt(projected_grad, wide_qkv)))
-    grad_qkv = layout.scatter_grad(dot_tn(inputs_one, projected_grad), p)
-    input_grad = resid_grad[:rows] + norm_backward(own_one_grad, unit_one[:rows], inverse_one[:rows], ln1_gain)
-    input_grad = layout.swap(input_grad.astype(BF16))
+    grad_out_part = dot_tn(mixed, resid_all).astype(BF16)
+    grad_out_sum = layout.scatter(grad_out_part)
+    projected_grad = attend_back(
+        where, after(mixed_grad, grad_out_part), q_all, k_all, v_all, lse, cosine, sine, start, heads, slots
+    )
+    grad_qkv_part = dot_tn(inputs_one, projected_grad).astype(BF16)
+    near_qkv = layout.near_sends(grad_qkv_part, plane)
+    out_chip = out_part[: 2 * rows] + after(out_got, near_qkv).astype(F32)
+    near_qkv, down_flip, out_send, projected_grad = hold(near_qkv, down_flip, out_chip[rows:].astype(BF16), projected_grad)
+
+    got_qkv = layout.scatter_near(grad_qkv_part, near_qkv)
+    out_other = layout.pair(out_send)
+    one_part = dot_nt(projected_grad, wide_qkv)
+    one_send = one_part[2 * rows :].astype(BF16)
+    one_send, got_qkv, out_other = hold(one_send, got_qkv, out_other)
+    one_got = layout.core(one_send)
+    later_qkv = layout.later_sends(grad_qkv_part, got_qkv, plane)
+    one_got, later_qkv = hold(one_got, later_qkv)
+    one_chip = one_part[: 2 * rows] + one_got.astype(F32)
+    output = resid_one[:rows] + out_chip[:rows] + out_other.astype(F32)
+    one_send, later_qkv, up_sum, output = hold(one_chip[rows:].astype(BF16), later_qkv, grad_up_sum, output.astype(BF16))
+    one_other = layout.pair(one_send)
+    qkv_parts = layout.scatter_far(grad_qkv_part, got_qkv, later_qkv, plane)
+    up_flip = layout.flip(up_sum, True)
+    down_own, down_other = layout.own_shards(down_sum, down_flip, c)
+    one_other, qkv_parts, up_flip, output, down_other = hold(one_other, qkv_parts, up_flip, output, down_other)
+
+    own_one_grad = one_chip[:rows] + one_other.astype(F32)
     gain_one_grad = jnp.sum(own_one_grad * unit_one[:rows], axis=0)
     bias_one_grad = jnp.sum(own_one_grad, axis=0)
-    norm_sums = lax.psum(jnp.stack([gain_one_grad, bias_one_grad, gain_two_grad, bias_two_grad]), AXES)
+    norm_parts = jnp.stack([gain_one_grad, bias_one_grad, gain_two_grad, bias_two_grad])
+    input_grad = resid_grad[:rows] + norm_backward(own_one_grad, unit_one[:rows], inverse_one[:rows], ln1_gain)
+    qkv_sum = layout.scatter_sum(qkv_parts)
+    one_sum = jnp.concatenate([qkv_sum, grad_out_sum.reshape(qkv_sum.shape[0], -1)], axis=1)
+    input_grad, norm_parts, one_sum, output = hold(input_grad.astype(BF16), norm_parts, one_sum, output)
+    one_flip = layout.flip(one_sum, True)
+    moved_input = layout.swap(input_grad)
+    moved_output = layout.swap(output)
+    norm_sums = layout.sum_all(norm_parts)
+    up_own, up_other = layout.own_shards(up_sum, up_flip, c)
+    one_flip, norm_sums, up_own, up_other = hold(one_flip, norm_sums, up_own, up_other)
+    one_own, one_other = layout.own_shards(one_sum, one_flip, c)
+    down_got, up_got, one_got = layout.core(down_other), layout.core(up_other), layout.core(one_other)
+    grad_down = jnp.where(p == c, down_own, down_got)
+    grad_up = jnp.where(p == c, up_own, up_got)
+    grad_one = jnp.where(p == c, one_own, one_got)
+    grad_qkv = grad_one[:, : 3 * part_width]
+    grad_out = grad_one[:, 3 * part_width :].reshape(w_out.shape)
+    output, input_grad = moved_output, moved_input
     return (
         output,
         input_grad,

time: 615 us -> 519 us (0.84)
  the two profiles are of different devices: /device:TPU:0 before, /device:TPU:1 now
where the time goes in v2:
time: 519 us; the launch traced here: 510 us
  waiting for transfers between devices  191 us (37%)
  starting transfers between devices  96 us (18%)
  matrix products  80 us (15%)
  other arithmetic  53.8 us (10%)
  local copies, waits for them, and re-layouts  48.1 us (9%)
  Pallas kernels  23.9 us (5%)
  between operations  16.9 us (3%)
    ppermute x42, waiting for transfers between devices, permute(): return lax.ppermute(value, AXES, pairs)  184 us
    ppermute x42, starting transfers between devices, permute(): return lax.ppermute(value, AXES, pairs)  81.9 us
    dot_general x4, matrix products, dot_nn(): lax.dot_general(left, right, (((1,), (0,)), ((), ())), preferred_element_...  28.4 us
    dot_general x4, matrix products, dot_nt(): lax.dot_general(left, right, (((1,), (1,)), ((), ())), preferred_element_...  27.8 us
    dot_general x4, matrix products, dot_tn(): lax.dot_general(left, right, (((0,), (0,)), ((), ())), preferred_element_...  23.8 us
    unnamed x108, local copies, waits for them, and re-layouts  21 us
    ppermute x4, starting transfers between devices, flip(): return lax.ppermute(value, AXES, pairs)  13.1 us
    pallas_call x1, Pallas kernels, attend_back(): pl.pallas_call(functools.partial(attend_back_kernel, heads, slots), in_sp...  13.1 us
  transfers between devices with their start and end apart: 52, of which 28 were waited for; matrix products, arithmetic and copies ran while one was open for 29% of the time, Pallas kernels for 5%

profile of v2, /device:TPU:1, one launch (start us, length us, event | category | flops | bytes accessed | tf_op | source)
XLA Modules:
  0.0 510.2 jit_solution(12632044986501469931)
XLA Ops:
  10.4 5.6 %collective-permute-start.1 = (bf16[192,1152]{1,0:T(8,128)(2,1)S(1)}, bf16[192,1152]{1,0:T(8,128)(2,1)S(1)}, u32[]{:S(2)}, u32[]{:S(2)}) collective-permute-start(bf16[192,1152]{1,0:T(8,128)(2,1)S(1)} %bitcast.44), channel_id=1, source_target_pairs={{0,0},{1,1},{2,4},{3,5},{4,2},{5,3},{6,6},{7,7},{8,8},{9,9},{10,12... | collective-permute-start | bytes 1327112 | tf_op jit(solution)/shard_map/ppermute | solution.py:192
  16.0 16.3 %collective-permute-done.2 = bf16[192,1152]{1,0:T(8,128)(2,1)S(1)} collective-permute-done((bf16[192,1152]{1,0:T(8,128)(2,1)S(1)}, bf16[192,1152]{1,0:T(8,128)(2,1)S(1)}, u32[]{:S(2)}, u32[]{:S(2)}) %collective-permute-start.2) | collective-permute-done | bytes 442400 | tf_op jit(solution)/shard_map/ppermute | solution.py:192
  42.1 16.1 %collective-permute-done.3 = bf16[256,1536]{1,0:T(8,128)(2,1)S(1)} collective-permute-done((bf16[256,1536]{1,0:T(8,128)(2,1)S(1)}, bf16[256,1536]{1,0:T(8,128)(2,1)S(1)}, u32[]{:S(2)}, u32[]{:S(2)}) %collective-permute-start.3) | collective-permute-done | bytes 786464 | tf_op jit(solution)/shard_map/ppermute | solution.py:192
  58.2 3.4 collective-permute-start.6
  63.5 6.8 %collective-permute-done.6 = bf16[48,1536]{1,0:T(8,128)(2,1)S(1)} collective-permute-done((bf16[48,1536]{1,0:T(8,128)(2,1)S(1)}, bf16[48,1536]{1,0:T(8,128)(2,1)S(1)}, u32[]{:S(2)}, u32[]{:S(2)}) %collective-permute-start.6) | collective-permute-done | bytes 147488 | tf_op jit(solution)/shard_map/ppermute | solution.py:192
  76.4 3.9 collective-permute-start.9
  81.6 2.7 constant_dynamic-update-slice_fusion
  84.3 9.4 %fusion.36.proj_ref = f32[1024,1152]{1,0:T(8,128)} fusion(bf16[1024,1536]{1,0:T(8,128)(2,1)} %constant_dynamic-update-slice_fusion, bf16[1536,1152]{1,0:T(8,128)(2,1)} %all-gather.4.cloned.1.call-done), kind=kOutput, calls=%fused_computation.147 | convolution fusion | flops 3623878656 | bytes 11403264 | tf_op jit(solution)/shard_map/dot_general | solution.py:52
  93.6 9.3 %collective-permute-done.10 = bf16[192,1536]{1,0:T(8,128)(2,1)} collective-permute-done((bf16[192,1536]{1,0:T(8,128)(2,1)}, bf16[192,1536]{1,0:T(8,128)(2,1)}, u32[]{:S(2)}, u32[]{:S(2)}) %collective-permute-start.10) | collective-permute-done | bytes 589856 | tf_op jit(solution)/shard_map/ppermute | solution.py:192
  112.1 10.8 %attend.1 = (bf16[1024,384]{1,0:T(8,128)(2,1)}, bf16[3,1024,128]{2,1,0:T(8,128)(2,1)}, bf16[3,1024,128]{2,1,0:T(8,128)(2,1)}, bf16[3,1024,128]{2,1,0:T(8,128)(2,1)}, f32[3,1024,1]{2,1,0:T(8,128)}) custom-call(s32[1]{0:T(128)} %bitcast.4.index_ref, f32[1024,1152]{1,0:T(8,128)} %fusion.36.proj_ref, f32[1024,128]{1,0:T(8,128)} %get-tuple-element.124.cos_ref, ...), custom_call_target="tpu_custom_call" | custom-call | flops 3000000000 | bytes 12000000 | tf_op jit(solution)/shard_map/attend/pallas_call | solution.py:149
  122.9 3.3 fusion.37
  126.2 2.6 copy-done
  130.2 7.5 %collective-permute-done.13 = bf16[384,1536]{1,0:T(8,128)(2,1)} collective-permute-done((bf16[384,1536]{1,0:T(8,128)(2,1)}, bf16[384,1536]{1,0:T(8,128)(2,1)}, u32[]{:S(2)}, u32[]{:S(2)}) %collective-permute-start.13) | collective-permute-done | bytes 1179680 | tf_op jit(solution)/shard_map/ppermute | solution.py:227
  143.6 2.4 broadcast_select_fusion
  147.2 3.5 fusion.12
  151.9 4.3 collective-permute-start.18
  159.6 8.5 %collective-permute-done.16 = bf16[192,1536]{1,0:T(8,128)(2,1)} collective-permute-done((bf16[192,1536]{1,0:T(8,128)(2,1)}, bf16[192,1536]{1,0:T(8,128)(2,1)}, u32[]{:S(2)}, u32[]{:S(2)}) %collective-permute-start.16) | collective-permute-done | bytes 589856 | tf_op jit(solution)/shard_map/ppermute | solution.py:192
  168.8 26.0 %collective-permute-done.18 = bf16[256,1536]{1,0:T(8,128)(2,1)} collective-permute-done((bf16[256,1536]{1,0:T(8,128)(2,1)}, bf16[256,1536]{1,0:T(8,128)(2,1)}, u32[]{:S(2)}, u32[]{:S(2)}) %collective-permute-start.18) | collective-permute-done | bytes 786464 | tf_op jit(solution)/shard_map/ppermute | solution.py:192
  195.8 2.6 fusion.32
  209.8 7.8 %multiply_convert_fusion = (bf16[1024,1536]{1,0:T(8,128)(2,1)S(1)}, f32[1024,1536]{1,0:T(8,128)}) fusion(f32[1536]{0:T(1024)S(1)} %fusion.23, bf16[1024,1536]{1,0:T(8,128)(2,1)S(1)} %constant_dynamic-update-slice_fusion.2, bf16[1536,1536]{1,0:T(8,128)(2,1)S(1)} %constant_dynamic-update-slice_fusion.11), kind=kOutput, calls=%fused_computation.13 | convolution fusion | flops 4847566848 | bytes 17307648 | tf_op jit(solution)/shard_map/dot_general | solution.py:52
  222.1 3.0 collective-permute-done.21
  226.9 7.0 %convolution_convert_fusion.2 = bf16[1536,1536]{1,0:T(8,128)(2,1)} fusion(bf16[1024,1536]{1,0:T(8,128)(2,1)S(1)} %get-tuple-element.161, bf16[1024,1536]{1,0:T(8,128)(2,1)S(1)} %constant_dynamic-update-slice_fusion.6), kind=kOutput, calls=%fused_computation.4 | convolution fusion | flops 4834197504 | bytes 11010048 | tf_op jit(solution)/shard_map/dot_general | solution.py:48
  234.1 11.8 %fusion.7 = bf16[1024,1536]{1,0:T(8,128)(2,1)S(1)} fusion(f32[1024,1536]{1,0:T(8,128)} %get-tuple-element.277, f32[1536]{0:T(1024)S(1)} %fusion.23, bf16[1024,1536]{1,0:T(8,128)(2,1)} %copy-done.35, bf16[1536,1536]{1,0:T(8,128)(2,1)} %all-gather.8.cloned.1.call-done), kind=kOutput, calls=%fused_computation.12 | convolution fusion | flops 4864868352 | bytes 17307648 | tf_op jit(solution)/shard_map/dot_general | solution.py:44
  246.0 7.1 %fusion.38 = f32[1024,1536]{1,0:T(8,128)S(1)} fusion(bf16[1024,1536]{1,0:T(8,128)(2,1)S(1)} %fusion.7, bf16[1536,1536]{1,0:T(8,128)(2,1)} %copy-done.17), kind=kOutput, calls=%fused_computation.149 | convolution fusion | flops 4831838208 | bytes 14155776 | tf_op jit(solution)/shard_map/dot_general | solution.py:44
  253.8 3.0 collective-permute-done.22
  259.8 6.8 %convolution_convert_fusion.1 = bf16[1536,1536]{1,0:T(8,128)(2,1)} fusion(bf16[1024,1536]{1,0:T(8,128)(2,1)S(1)} %copy-done.28, bf16[1024,1536]{1,0:T(8,128)(2,1)S(1)} %fusion.7), kind=kOutput, calls=%fused_computation.3 | convolution fusion | flops 4834197504 | bytes 11010048 | tf_op jit(solution)/shard_map/dot_general | solution.py:48
  266.7 8.0 %fusion.39 = f32[1024,1536]{1,0:T(8,128)S(1)} fusion(bf16[1024,1536]{1,0:T(8,128)(2,1)} %copy-done.47, bf16[1536,1536]{1,0:T(8,128)(2,1)} %all-gather.8.cloned.1.call-done), kind=kOutput, calls=%fused_computation.150 | convolution fusion | flops 4831838208 | bytes 14155776 | tf_op jit(solution)/shard_map/dot_general | solution.py:52
  277.9 24.8 %collective-permute-done.23 = bf16[512,1536]{1,0:T(8,128)(2,1)S(1)} collective-permute-done((bf16[512,1536]{1,0:T(8,128)(2,1)}, bf16[512,1536]{1,0:T(8,128)(2,1)S(1)}, u32[]{:S(2)}, u32[]{:S(2)}) %collective-permute-start.23) | collective-permute-done | bytes 1572896 | tf_op jit(solution)/shard_map/ppermute | solution.py:192
  305.8 3.1 fusion.31
  312.4 3.8 collective-permute-start.25
  319.5 2.4 convolution_convert_fusion.3
  321.9 4.6 convolution_convert_fusion.4.grad_ref
  326.6 13.1 %attend_back.1 = bf16[1024,1152]{1,0:T(8,128)(2,1)} custom-call(s32[1]{0:T(128)} %bitcast.4.index_ref, bf16[1024,384]{1,0:T(8,128)(2,1)} %convolution_convert_fusion.4.grad_ref, bf16[3,1024,128]{2,1,0:T(8,128)(2,1)} %get-tuple-element.167.q_ref, bf16[3,1024,128]{2,1,0:T(8,128)(2,1)} %get-tuple-element.168.k_ref, ...), custom_call_target="tpu_custom_call" | custom-call | flops 6000000000 | bytes 12000000 | tf_op jit(solution)/shard_map/attend_back/pallas_call | solution.py:167
  339.7 7.6 %convolution_convert_fusion = bf16[1536,1152]{1,0:T(8,128)(2,1)S(1)} fusion(bf16[1024,1536]{1,0:T(8,128)(2,1)} %constant_dynamic-update-slice_fusion, bf16[1024,1152]{1,0:T(8,128)(2,1)} %attend_back.1), kind=kOutput, calls=%fused_computation.2 | convolution fusion | flops 3625648128 | bytes 9043968 | tf_op jit(solution)/shard_map/dot_general | solution.py:48
  347.5 3.0 slice_add_fusion.1
  353.4 4.2 fusion.40
  357.9 3.9 collective-permute-done.27
  362.7 7.4 %collective-permute-done.29 = bf16[256,1536]{1,0:T(8,128)(2,1)S(1)} collective-permute-done((bf16[256,1536]{1,0:T(8,128)(2,1)S(1)}, bf16[256,1536]{1,0:T(8,128)(2,1)S(1)}, u32[]{:S(2)}, u32[]{:S(2)}) %collective-permute-start.29) | collective-permute-done | bytes 786464 | tf_op jit(solution)/shard_map/ppermute | solution.py:192
  380.1 4.6 collective-permute-start.34
  389.9 26.2 %collective-permute-done.31 = bf16[256,1536]{1,0:T(8,128)(2,1)} collective-permute-done((bf16[256,1536]{1,0:T(8,128)(2,1)}, bf16[256,1536]{1,0:T(8,128)(2,1)}, u32[]{:S(2)}, u32[]{:S(2)}) %collective-permute-start.31) | collective-permute-done | bytes 786464 | tf_op jit(solution)/shard_map/ppermute | solution.py:192
  416.2 2.9 multiply_reduce_fusion.3
  425.1 2.7 collective-permute-done.39
  428.9 3.2 collective-permute-start.37
  432.1 5.0 collective-permute-start.35
  445.8 33.4 %collective-permute-start.43 = (f32[192,1536]{1,0:T(8,128)S(1)}, f32[192,1536]{1,0:T(8,128)S(1)}, u32[]{:S(2)}, u32[]{:S(2)}) collective-permute-start(f32[192,1536]{1,0:T(8,128)S(1)} %slice_select_fusion), channel_id=1, source_target_pairs={{0,4},{1,5},{2,6},{3,7},{4,0},{5,1},{6,2},{7,3},{8,12},{9,13},{10,... | collective-permute-start | bytes 3538952 | tf_op jit(solution)/shard_map/ppermute | solution.py:192
  479.2 7.2 %collective-permute-done.35 = bf16[256,1536]{1,0:T(8,128)(2,1)S(1)} collective-permute-done((bf16[256,1536]{1,0:T(8,128)(2,1)S(1)}, bf16[256,1536]{1,0:T(8,128)(2,1)S(1)}, u32[]{:S(2)}, u32[]{:S(2)}) %collective-permute-start.35) | collective-permute-done | bytes 786464 | tf_op jit(solution)/shard_map/ppermute | solution.py:192
  486.4 8.4 %collective-permute-done.36 = bf16[256,1536]{1,0:T(8,128)(2,1)S(1)} collective-permute-done((bf16[256,1536]{1,0:T(8,128)(2,1)S(1)}, bf16[256,1536]{1,0:T(8,128)(2,1)S(1)}, u32[]{:S(2)}, u32[]{:S(2)}) %collective-permute-start.36) | collective-permute-done | bytes 786464 | tf_op jit(solution)/shard_map/ppermute | solution.py:192
  499.0 2.4 broadcast_select_fusion.1
  (285 shorter events, 120.1 us)
Async XLA Ops:
  7.2 77.1 %all-gather.4.cloned.1.call-start = ((), (), s32[]{:S(2)}) async-start(), calls=%async_computation.3 | async-start | bytes 4423680 | tf_op jit(solution)/shard_map/all_gather | solution.py:242
  9.9 22.5 %collective-permute-start.2 = (bf16[192,1152]{1,0:T(8,128)(2,1)S(1)}, bf16[192,1152]{1,0:T(8,128)(2,1)S(1)}, u32[]{:S(2)}, u32[]{:S(2)}) collective-permute-start(bf16[192,1152]{1,0:T(8,128)(2,1)S(1)} %bitcast.43), channel_id=1, source_target_pairs={{0,2},{1,3},{2,6},{3,7},{4,0},{5,1},{6,4},{7,5},{8,10},{9,11},{10,... | collective-permute-start | bytes 1327112 | tf_op jit(solution)/shard_map/ppermute | solution.py:192
  10.4 23.2 %collective-permute-start.1 = (bf16[192,1152]{1,0:T(8,128)(2,1)S(1)}, bf16[192,1152]{1,0:T(8,128)(2,1)S(1)}, u32[]{:S(2)}, u32[]{:S(2)}) collective-permute-start(bf16[192,1152]{1,0:T(8,128)(2,1)S(1)} %bitcast.44), channel_id=1, source_target_pairs={{0,0},{1,1},{2,4},{3,5},{4,2},{5,3},{6,6},{7,7},{8,8},{9,9},{10,12... | collective-permute-start | bytes 1327112 | tf_op jit(solution)/shard_map/ppermute | solution.py:192
  34.8 88.1 %all-gather.6.cloned.1.call-start = ((), (), s32[]{:S(2)}) async-start(), calls=%async_computation.4 | async-start | bytes 1474560 | tf_op jit(solution)/shard_map/all_gather | solution.py:242
  35.3 5.4 %collective-permute-start.4 = (bf16[192,1536]{1,0:T(8,128)(2,1)S(1)}, bf16[192,1536]{1,0:T(8,128)(2,1)S(1)}, u32[]{:S(2)}, u32[]{:S(2)}) collective-permute-start(bf16[192,1536]{1,0:T(8,128)(2,1)S(1)} %copy-done.34), channel_id=1, source_target_pairs={{0,4},{1,5},{2,6},{3,7},{4,0},{5,1},{6,2},{7,3},{8,12},{9,13},{10,... | collective-permute-start | bytes 1769480 | tf_op jit(solution)/shard_map/ppermute | solution.py:192
  35.4 22.7 %collective-permute-start.3 = (bf16[256,1536]{1,0:T(8,128)(2,1)S(1)}, bf16[256,1536]{1,0:T(8,128)(2,1)S(1)}, u32[]{:S(2)}, u32[]{:S(2)}) collective-permute-start(bf16[256,1536]{1,0:T(8,128)(2,1)S(1)} %copy-done.45), channel_id=1, source_target_pairs={{0,0},{1,1},{2,4},{3,5},{4,2},{5,3},{6,6},{7,7},{8,8},{9,9},{10,12... | collective-permute-start | bytes 2359304 | tf_op jit(solution)/shard_map/ppermute | solution.py:192
  58.2 14.4 %collective-permute-start.5 = (bf16[256,1536]{1,0:T(8,128)(2,1)S(1)}, bf16[256,1536]{1,0:T(8,128)(2,1)S(1)}, u32[]{:S(2)}, u32[]{:S(2)}) collective-permute-start(bf16[256,1536]{1,0:T(8,128)(2,1)S(1)} %collective-permute-done.3), channel_id=1, source_target_pairs={{0,1},{1,0},{2,3},{3,2},{4,5},{5,4},{6,7},{7,6},{8,9},{9,8},{10,11... | collective-permute-start | bytes 2359304 | tf_op jit(solution)/shard_map/ppermute | solution.py:192
  58.2 5.3 %collective-permute-start.7 = (bf16[48,1536]{1,0:T(8,128)(2,1)S(1)}, bf16[48,1536]{1,0:T(8,128)(2,1)S(1)}, u32[]{:S(2)}, u32[]{:S(2)}) collective-permute-start(bf16[48,1536]{1,0:T(8,128)(2,1)S(1)} %copy-done.46), channel_id=1, source_target_pairs={{0,2},{1,3},{2,6},{3,7},{4,0},{5,1},{6,4},{7,5},{8,10},{9,11},{10,... | collective-permute-start | bytes 442376 | tf_op jit(solution)/shard_map/ppermute | solution.py:192
  58.2 12.1 %collective-permute-start.6 = (bf16[48,1536]{1,0:T(8,128)(2,1)S(1)}, bf16[48,1536]{1,0:T(8,128)(2,1)S(1)}, u32[]{:S(2)}, u32[]{:S(2)}) collective-permute-start(bf16[48,1536]{1,0:T(8,128)(2,1)S(1)} %copy-done.46), channel_id=1, source_target_pairs={{0,0},{1,1},{2,4},{3,5},{4,2},{5,3},{6,6},{7,7},{8,8},{9,9},{10,12... | collective-permute-start | bytes 442376 | tf_op jit(solution)/shard_map/ppermute | solution.py:192
  75.7 5.9 %collective-permute-start.8 = (bf16[512,1536]{1,0:T(8,128)(2,1)S(1)}, bf16[512,1536]{1,0:T(8,128)(2,1)}, u32[]{:S(2)}, u32[]{:S(2)}) collective-permute-start(bf16[512,1536]{1,0:T(8,128)(2,1)S(1)} %get-tuple-element.116), channel_id=1, source_target_pairs={{0,4},{1,5},{2,6},{3,7},{4,0},{5,1},{6,2},{7,3},{8,12},{9,13},{10,... | collective-permute-start | bytes 4718600 | tf_op jit(solution)/shard_map/ppermute | solution.py:192
  75.8 158.4 %all-gather.8.cloned.1.call-start = ((), (), s32[]{:S(2)}) async-start(), calls=%async_computation.5 | async-start | bytes 5898240 | tf_op jit(solution)/shard_map/all_gather | solution.py:242
  75.8 27.1 %collective-permute-start.10 = (bf16[192,1536]{1,0:T(8,128)(2,1)}, bf16[192,1536]{1,0:T(8,128)(2,1)}, u32[]{:S(2)}, u32[]{:S(2)}) collective-permute-start(bf16[192,1536]{1,0:T(8,128)(2,1)} %param.22), channel_id=1, source_target_pairs={{0,2},{1,3},{2,6},{3,7},{4,0},{5,1},{6,4},{7,5},{8,10},{9,11},{10,... | collective-permute-start | bytes 1769480 | tf_op jit(solution)/shard_map/ppermute | solution.py:192
  76.4 28.4 %collective-permute-start.9 = (bf16[192,1536]{1,0:T(8,128)(2,1)}, bf16[192,1536]{1,0:T(8,128)(2,1)}, u32[]{:S(2)}, u32[]{:S(2)}) collective-permute-start(bf16[192,1536]{1,0:T(8,128)(2,1)} %param.22), channel_id=1, source_target_pairs={{0,0},{1,1},{2,4},{3,5},{4,2},{5,3},{6,6},{7,7},{8,8},{9,9},{10,12... | collective-permute-start | bytes 1769480 | tf_op jit(solution)/shard_map/ppermute | solution.py:192
  106.9 30.8 %collective-permute-start.13 = (bf16[384,1536]{1,0:T(8,128)(2,1)}, bf16[384,1536]{1,0:T(8,128)(2,1)}, u32[]{:S(2)}, u32[]{:S(2)}) collective-permute-start(bf16[384,1536]{1,0:T(8,128)(2,1)} %maximum_select_fusion), channel_id=1, source_target_pairs={{0,2},{1,3},{6,4},{7,5},{8,10},{9,11},{14,12},{15,13},{16,18},{17,... | collective-permute-start | bytes 3538952 | tf_op jit(solution)/shard_map/ppermute | solution.py:227
  108.5 30.1 %collective-permute-start.12 = (bf16[384,1536]{1,0:T(8,128)(2,1)S(1)}, bf16[384,1536]{1,0:T(8,128)(2,1)}, u32[]{:S(2)}, u32[]{:S(2)}) collective-permute-start(bf16[384,1536]{1,0:T(8,128)(2,1)S(1)} %maximum_select_fusion.1), channel_id=1, source_target_pairs={{0,16},{1,17},{2,18},{3,19},{4,20},{5,21},{6,22},{7,23},{8,24},{9,... | collective-permute-start | bytes 3538952 | tf_op jit(solution)/shard_map/ppermute | solution.py:192
  109.8 28.8 %collective-permute-start.11 = (bf16[384,1536]{1,0:T(8,128)(2,1)S(1)}, bf16[384,1536]{1,0:T(8,128)(2,1)}, u32[]{:S(2)}, u32[]{:S(2)}) collective-permute-start(bf16[384,1536]{1,0:T(8,128)(2,1)S(1)} %maximum_select_fusion.1), channel_id=1, source_target_pairs={{0,8},{1,9},{2,10},{3,11},{4,12},{5,13},{6,14},{7,15},{8,0},{9,1},... | collective-permute-start | bytes 3538952 | tf_op jit(solution)/shard_map/ppermute | solution.py:192
  138.6 7.4 %collective-permute-start.14 = (bf16[512,1536]{1,0:T(8,128)(2,1)}, bf16[512,1536]{1,0:T(8,128)(2,1)S(1)}, u32[]{:S(2)}, u32[]{:S(2)}) collective-permute-start(bf16[512,1536]{1,0:T(8,128)(2,1)} %slice.215), channel_id=1, source_target_pairs={{0,4},{1,5},{2,6},{3,7},{4,0},{5,1},{6,2},{7,3},{8,12},{9,13},{10,... | collective-permute-start | bytes 4718600 | tf_op jit(solution)/shard_map/ppermute | solution.py:192
  150.7 44.8 %collective-permute-start.15 = (bf16[512,1536]{1,0:T(8,128)(2,1)}, bf16[512,1536]{1,0:T(8,128)(2,1)S(1)}, u32[]{:S(2)}, u32[]{:S(2)}) collective-permute-start(bf16[512,1536]{1,0:T(8,128)(2,1)} %fusion.12), channel_id=1, source_target_pairs={{0,1},{1,0},{2,3},{3,2},{4,5},{5,4},{6,7},{7,6},{8,9},{9,8},{10,11... | collective-permute-start | bytes 4718600 | tf_op jit(solution)/shard_map/ppermute | solution.py:192
  151.9 43.0 %collective-permute-start.18 = (bf16[256,1536]{1,0:T(8,128)(2,1)}, bf16[256,1536]{1,0:T(8,128)(2,1)}, u32[]{:S(2)}, u32[]{:S(2)}) collective-permute-start(bf16[256,1536]{1,0:T(8,128)(2,1)} %param.13), channel_id=1, source_target_pairs={{0,0},{1,1},{2,4},{3,5},{4,2},{5,3},{6,6},{7,7},{8,8},{9,9},{10,12... | collective-permute-start | bytes 2359304 | tf_op jit(solution)/shard_map/ppermute | solution.py:192
  156.2 11.8 %collective-permute-start.16 = (bf16[192,1536]{1,0:T(8,128)(2,1)}, bf16[192,1536]{1,0:T(8,128)(2,1)}, u32[]{:S(2)}, u32[]{:S(2)}) collective-permute-start(bf16[192,1536]{1,0:T(8,128)(2,1)} %slice.108), channel_id=1, source_target_pairs={{0,16},{1,17},{2,18},{3,19},{4,20},{5,21},{6,22},{7,23},{8,24},{9,... | collective-permute-start | bytes 1769480 | tf_op jit(solution)/shard_map/ppermute | solution.py:192
  157.4 11.4 %collective-permute-start.17 = (bf16[192,1536]{1,0:T(8,128)(2,1)}, bf16[192,1536]{1,0:T(8,128)(2,1)}, u32[]{:S(2)}, u32[]{:S(2)}) collective-permute-start(bf16[192,1536]{1,0:T(8,128)(2,1)} %slice.109), channel_id=1, source_target_pairs={{0,8},{1,9},{2,10},{3,11},{4,12},{5,13},{6,14},{7,15},{8,0},{9,1},... | collective-permute-start | bytes 1769480 | tf_op jit(solution)/shard_map/ppermute | solution.py:192
  159.0 149.9 %reduce-scatter.4.cloned.1.call-start = ((), (), s32[]{:S(2)}) async-start(), calls=%async_computation.6 | async-start | bytes 5898240 | tf_op jit(solution)/shard_map/reduce_scatter | solution.py:274
  200.1 19.8 %collective-permute-start.20 = (bf16[256,1536]{1,0:T(8,128)(2,1)}, bf16[256,1536]{1,0:T(8,128)(2,1)S(1)}, u32[]{:S(2)}, u32[]{:S(2)}) collective-permute-start(bf16[256,1536]{1,0:T(8,128)(2,1)} %collective-permute-done.18), channel_id=1, source_target_pairs={{0,1},{1,0},{2,3},{3,2},{4,5},{5,4},{6,7},{7,6},{8,9},{9,8},{10,11... | collective-permute-start | bytes 2359304 | tf_op jit(solution)/shard_map/ppermute | solution.py:192
  202.1 7.4 %collective-permute-start.19 = (bf16[512,1536]{1,0:T(8,128)(2,1)S(1)}, bf16[512,1536]{1,0:T(8,128)(2,1)S(1)}, u32[]{:S(2)}, u32[]{:S(2)}) collective-permute-start(bf16[512,1536]{1,0:T(8,128)(2,1)S(1)} %get-tuple-element.150), channel_id=1, source_target_pairs={{0,4},{1,5},{2,6},{3,7},{4,0},{5,1},{6,2},{7,3},{8,12},{9,13},{10,... | collective-permute-start | bytes 4718600 | tf_op jit(solution)/shard_map/ppermute | solution.py:192
  221.2 3.9 collective-permute-start.21
  233.9 144.7 %reduce-scatter.6.cloned.1.call-start = ((), (), s32[]{:S(2)}) async-start(), calls=%async_computation.7 | async-start | bytes 5898240 | tf_op jit(solution)/shard_map/reduce_scatter | solution.py:274
  253.3 3.6 collective-permute-start.22
  266.6 122.1 %reduce-scatter.8.cloned.1.call-start = ((), (), s32[]{:S(2)}) async-start(), calls=%async_computation.8 | async-start | bytes 1474560 | tf_op jit(solution)/shard_map/reduce_scatter | solution.py:274
  266.7 36.0 %collective-permute-start.23 = (bf16[512,1536]{1,0:T(8,128)(2,1)}, bf16[512,1536]{1,0:T(8,128)(2,1)S(1)}, u32[]{:S(2)}, u32[]{:S(2)}) collective-permute-start(bf16[512,1536]{1,0:T(8,128)(2,1)} %fusion.13), channel_id=1, source_target_pairs={{0,1},{1,0},{2,3},{3,2},{4,5},{5,4},{6,7},{7,6},{8,9},{9,8},{10,11... | collective-permute-start | bytes 4718600 | tf_op jit(solution)/shard_map/ppermute | solution.py:192
  308.8 7.5 %collective-permute-start.24 = (bf16[512,1536]{1,0:T(8,128)(2,1)}, bf16[512,1536]{1,0:T(8,128)(2,1)}, u32[]{:S(2)}, u32[]{:S(2)}) collective-permute-start(bf16[512,1536]{1,0:T(8,128)(2,1)} %get-tuple-element.165), channel_id=1, source_target_pairs={{0,4},{1,5},{2,6},{3,7},{4,0},{5,1},{6,2},{7,3},{8,12},{9,13},{10,... | collective-permute-start | bytes 4718600 | tf_op jit(solution)/shard_map/ppermute | solution.py:192
  312.4 38.2 %collective-permute-start.25 = (bf16[384,1536]{1,0:T(8,128)(2,1)}, bf16[384,1536]{1,0:T(8,128)(2,1)S(1)}, u32[]{:S(2)}, u32[]{:S(2)}) collective-permute-start(bf16[384,1536]{1,0:T(8,128)(2,1)} %reduce-scatter.4.cloned.1.call-done), channel_id=1, source_target_pairs={{2,0},{3,1},{4,6},{5,7},{10,8},{11,9},{12,14},{13,15},{18,16},{19,... | collective-permute-start | bytes 3538952 | tf_op jit(solution)/shard_map/ppermute | solution.py:227
  316.2 31.3 %collective-permute-start.26 = (bf16[512,1536]{1,0:T(8,128)(2,1)}, bf16[512,1536]{1,0:T(8,128)(2,1)}, u32[]{:S(2)}, u32[]{:S(2)}) collective-permute-start(bf16[512,1536]{1,0:T(8,128)(2,1)} %slice.213), channel_id=1, source_target_pairs={{0,4},{1,5},{2,6},{3,7},{4,0},{5,1},{6,2},{7,3},{8,12},{9,13},{10,... | collective-permute-start | bytes 4718600 | tf_op jit(solution)/shard_map/ppermute | solution.py:192
  350.6 11.2 %collective-permute-start.27 = (bf16[192,1152]{1,0:T(8,128)(2,1)S(1)}, bf16[192,1152]{1,0:T(8,128)(2,1)S(1)}, u32[]{:S(2)}, u32[]{:S(2)}) collective-permute-start(bf16[192,1152]{1,0:T(8,128)(2,1)S(1)} %get-tuple-element.175), channel_id=1, source_target_pairs={{0,8},{1,9},{2,10},{3,11},{4,12},{5,13},{6,14},{7,15},{8,0},{9,1},... | collective-permute-start | bytes 1327112 | tf_op jit(solution)/shard_map/ppermute | solution.py:192
  351.8 10.9 %collective-permute-start.28 = (bf16[192,1152]{1,0:T(8,128)(2,1)S(1)}, bf16[192,1152]{1,0:T(8,128)(2,1)S(1)}, u32[]{:S(2)}, u32[]{:S(2)}) collective-permute-start(bf16[192,1152]{1,0:T(8,128)(2,1)S(1)} %get-tuple-element.176), channel_id=1, source_target_pairs={{0,16},{1,17},{2,18},{3,19},{4,20},{5,21},{6,22},{7,23},{8,24},{9,... | collective-permute-start | bytes 1327112 | tf_op jit(solution)/shard_map/ppermute | solution.py:192
  352.1 18.0 %collective-permute-start.29 = (bf16[256,1536]{1,0:T(8,128)(2,1)S(1)}, bf16[256,1536]{1,0:T(8,128)(2,1)S(1)}, u32[]{:S(2)}, u32[]{:S(2)}) collective-permute-start(bf16[256,1536]{1,0:T(8,128)(2,1)S(1)} %slice.217), channel_id=1, source_target_pairs={{0,1},{1,0},{2,3},{3,2},{4,5},{5,4},{6,7},{7,6},{8,9},{9,8},{10,11... | collective-permute-start | bytes 2359304 | tf_op jit(solution)/shard_map/ppermute | solution.py:192
  370.1 5.4 %collective-permute-start.30 = (bf16[512,1536]{1,0:T(8,128)(2,1)S(1)}, bf16[512,1536]{1,0:T(8,128)(2,1)S(1)}, u32[]{:S(2)}, u32[]{:S(2)}) collective-permute-start(bf16[512,1536]{1,0:T(8,128)(2,1)S(1)} %slice.212), channel_id=1, source_target_pairs={{0,4},{1,5},{2,6},{3,7},{4,0},{5,1},{6,2},{7,3},{8,12},{9,13},{10,... | collective-permute-start | bytes 4718600 | tf_op jit(solution)/shard_map/ppermute | solution.py:192
  378.6 37.5 %collective-permute-start.32 = (bf16[384,1152]{1,0:T(8,128)(2,1)}, bf16[384,1152]{1,0:T(8,128)(2,1)}, u32[]{:S(2)}, u32[]{:S(2)}) collective-permute-start(bf16[384,1152]{1,0:T(8,128)(2,1)} %pad_maximum_fusion.2), channel_id=1, source_target_pairs={{0,8},{1,9},{2,10},{3,11},{4,12},{5,13},{6,14},{7,15},{8,0},{9,1},... | collective-permute-start | bytes 2654216 | tf_op jit(solution)/shard_map/ppermute | solution.py:192
  379.8 36.4 %collective-permute-start.33 = (bf16[384,1152]{1,0:T(8,128)(2,1)}, bf16[384,1152]{1,0:T(8,128)(2,1)}, u32[]{:S(2)}, u32[]{:S(2)}) collective-permute-start(bf16[384,1152]{1,0:T(8,128)(2,1)} %pad_maximum_fusion.3), channel_id=1, source_target_pairs={{0,16},{1,17},{2,18},{3,19},{4,20},{5,21},{6,22},{7,23},{8,24},{9,... | collective-permute-start | bytes 2654216 | tf_op jit(solution)/shard_map/ppermute | solution.py:192
  380.1 36.0 %collective-permute-start.34 = (bf16[384,1536]{1,0:T(8,128)(2,1)}, bf16[384,1536]{1,0:T(8,128)(2,1)}, u32[]{:S(2)}, u32[]{:S(2)}) collective-permute-start(bf16[384,1536]{1,0:T(8,128)(2,1)} %reduce-scatter.6.cloned.1.call-done), channel_id=1, source_target_pairs={{2,0},{3,1},{4,6},{5,7},{10,8},{11,9},{12,14},{13,15},{18,16},{19,... | collective-permute-start | bytes 3538952 | tf_op jit(solution)/shard_map/ppermute | solution.py:227
  386.3 29.8 %collective-permute-start.31 = (bf16[256,1536]{1,0:T(8,128)(2,1)}, bf16[256,1536]{1,0:T(8,128)(2,1)}, u32[]{:S(2)}, u32[]{:S(2)}) collective-permute-start(bf16[256,1536]{1,0:T(8,128)(2,1)} %slice.216), channel_id=1, source_target_pairs={{0,1},{1,0},{2,3},{3,2},{4,5},{5,4},{6,7},{7,6},{8,9},{9,8},{10,11... | collective-permute-start | bytes 2359304 | tf_op jit(solution)/shard_map/ppermute | solution.py:192
  427.7 11.5 %collective-permute-start.40 = (f32[4,1536]{1,0:T(4,128)S(1)}, f32[4,1536]{1,0:T(4,128)S(1)}, u32[]{:S(2)}, u32[]{:S(2)}) collective-permute-start(f32[4,1536]{1,0:T(4,128)S(1)} %add.250), channel_id=1, source_target_pairs={{0,2},{1,3},{2,0},{3,1},{4,6},{5,7},{6,4},{7,5},{8,10},{9,11},{10,... | collective-permute-start | bytes 73736 | tf_op jit(solution)/shard_map/ppermute | solution.py:192
  428.9 16.4 %collective-permute-start.37 = (bf16[384,1536]{1,0:T(8,128)(2,1)S(1)}, bf16[384,1536]{1,0:T(8,128)(2,1)S(1)}, u32[]{:S(2)}, u32[]{:S(2)}) collective-permute-start(bf16[384,1536]{1,0:T(8,128)(2,1)S(1)} %pad_maximum_fusion.1), channel_id=1, source_target_pairs={{2,0},{3,1},{4,6},{5,7},{10,8},{11,9},{12,14},{13,15},{18,16},{19,... | collective-permute-start | bytes 3538952 | tf_op jit(solution)/shard_map/ppermute | solution.py:227
  432.1 54.3 %collective-permute-start.35 = (bf16[256,1536]{1,0:T(8,128)(2,1)S(1)}, bf16[256,1536]{1,0:T(8,128)(2,1)S(1)}, u32[]{:S(2)}, u32[]{:S(2)}) collective-permute-start(bf16[256,1536]{1,0:T(8,128)(2,1)S(1)} %copy-done.26), channel_id=1, source_target_pairs={{0,0},{1,1},{2,4},{3,5},{4,2},{5,3},{6,6},{7,7},{8,8},{9,9},{10,12... | collective-permute-start | bytes 2359304 | tf_op jit(solution)/shard_map/ppermute | solution.py:192
  437.1 57.7 %collective-permute-start.36 = (bf16[256,1536]{1,0:T(8,128)(2,1)S(1)}, bf16[256,1536]{1,0:T(8,128)(2,1)S(1)}, u32[]{:S(2)}, u32[]{:S(2)}) collective-permute-start(bf16[256,1536]{1,0:T(8,128)(2,1)S(1)} %fusion.17), channel_id=1, source_target_pairs={{0,0},{1,1},{2,4},{3,5},{4,2},{5,3},{6,6},{7,7},{8,8},{9,9},{10,12... | collective-permute-start | bytes 2359304 | tf_op jit(solution)/shard_map/ppermute | solution.py:192
  439.2 3.0 collective-permute-start.41
  444.6 51.0 %collective-permute-start.45 = (f32[192,1536]{1,0:T(8,128)S(1)}, f32[192,1536]{1,0:T(8,128)S(1)}, u32[]{:S(2)}, u32[]{:S(2)}) collective-permute-start(f32[192,1536]{1,0:T(8,128)S(1)} %copy-done.25), channel_id=1, source_target_pairs={{0,4},{1,5},{2,6},{3,7},{4,0},{5,1},{6,2},{7,3},{8,12},{9,13},{10,... | collective-permute-start | bytes 3538952 | tf_op jit(solution)/shard_map/ppermute | solution.py:192
  445.8 51.0 %collective-permute-start.43 = (f32[192,1536]{1,0:T(8,128)S(1)}, f32[192,1536]{1,0:T(8,128)S(1)}, u32[]{:S(2)}, u32[]{:S(2)}) collective-permute-start(f32[192,1536]{1,0:T(8,128)S(1)} %slice_select_fusion), channel_id=1, source_target_pairs={{0,4},{1,5},{2,6},{3,7},{4,0},{5,1},{6,2},{7,3},{8,12},{9,13},{10,... | collective-permute-start | bytes 3538952 | tf_op jit(solution)/shard_map/ppermute | solution.py:192
  494.8 4.2 collective-permute-start.44
  (56 other events, 772.3 us)
Sparse Core Ops, SparseCore 0:
  34.9 48.9 all-gather.3
  86.3 29.4 all-gather.5
  159.1 58.7 all-gather.7
  234.0 56.2 reduce-scatter.3
  293.1 57.0 reduce-scatter.5
  353.6 28.5 reduce-scatter.7

commit v3 on v2

--- a/solution.py
+++ b/solution.py
@@ -207,15 +207,20 @@
         one, two = shards
         return jnp.where(p == 0, jnp.concatenate([one, two]), jnp.concatenate([two, one]))
 
-    def sum_all(self, value):
+    def sum_quad(self, value):
         value = value + self.core(value)
-        value = value + self.pair(value)
+        return value + self.pair(value)
+
+    def sum_quads(self, value):
         value = value + self.permute(value, lambda plane, c, p, zl: (plane, c, 1 - p, zl))
         step = 1
         while step < self.planes:
             value = value + self.plane_step(value, step)
             step *= 2
         return value
+
+    def swap_over_back(self, value):
+        return self.permute(value, lambda plane, c, p, zl: (plane, 1 - p, c, zl))
 
     def flip(self, value, into):
         pairs = []
@@ -454,8 +459,6 @@
     near_two_grad = ffn_chip + pair_order(ffn_other)
 
     resid_grad = near_cot.astype(F32) + norm_backward(near_two_grad, unit_two, inverse_two, ln2_gain)
-    gain_two_grad = jnp.sum(near_two_grad[:rows] * unit_two[:rows], axis=0)
-    bias_two_grad = jnp.sum(near_two_grad[:rows], axis=0)
     resid_low = resid_grad.astype(BF16)
     resid_low, out_send, down_sum = hold(resid_low, out_send, grad_down_sum)
     down_flip = layout.flip(down_sum, True)
@@ -464,52 +467,60 @@
     mixed_grad = dot_nt(resid_all, wide_out).astype(BF16)
     grad_out_part = dot_tn(mixed, resid_all).astype(BF16)
     grad_out_sum = layout.scatter(grad_out_part)
+    out_got = after(out_got, grad_out_part)
+    out_send = (out_part[rows : 2 * rows] + out_got[rows:].astype(F32)).astype(BF16)
+    out_other = layout.pair(out_send)
     projected_grad = attend_back(
-        where, after(mixed_grad, grad_out_part), q_all, k_all, v_all, lse, cosine, sine, start, heads, slots
+        where, after(mixed_grad, out_send), q_all, k_all, v_all, lse, cosine, sine, start, heads, slots
     )
     grad_qkv_part = dot_tn(inputs_one, projected_grad).astype(BF16)
     near_qkv = layout.near_sends(grad_qkv_part, plane)
-    out_chip = out_part[: 2 * rows] + after(out_got, near_qkv).astype(F32)
-    near_qkv, down_flip, out_send, projected_grad = hold(near_qkv, down_flip, out_chip[rows:].astype(BF16), projected_grad)
+    near_qkv, down_flip, out_other, projected_grad = hold(near_qkv, down_flip, out_other, projected_grad)
 
     got_qkv = layout.scatter_near(grad_qkv_part, near_qkv)
-    out_other = layout.pair(out_send)
     one_part = dot_nt(projected_grad, wide_qkv)
-    one_send = one_part[2 * rows :].astype(BF16)
-    one_send, got_qkv, out_other = hold(one_send, got_qkv, out_other)
-    one_got = layout.core(one_send)
+    output = resid_one[:rows] + out_part[:rows] + out_got[:rows].astype(F32) + out_other.astype(F32)
+    one_send, got_qkv, output = hold(one_part[2 * rows :].astype(BF16), got_qkv, output.astype(BF16))
+    (one_got,) = hold(layout.core(one_send))
+    one_send = (one_part[rows : 2 * rows] + one_got[rows:].astype(F32)).astype(BF16)
+    one_send, got_qkv, output, near_two_grad, up_sum = hold(one_send, got_qkv, output, near_two_grad, grad_up_sum)
+    one_other = layout.pair(one_send)
     later_qkv = layout.later_sends(grad_qkv_part, got_qkv, plane)
-    one_got, later_qkv = hold(one_got, later_qkv)
-    one_chip = one_part[: 2 * rows] + one_got.astype(F32)
-    output = resid_one[:rows] + out_chip[:rows] + out_other.astype(F32)
-    one_send, later_qkv, up_sum, output = hold(one_chip[rows:].astype(BF16), later_qkv, grad_up_sum, output.astype(BF16))
-    one_other = layout.pair(one_send)
     qkv_parts = layout.scatter_far(grad_qkv_part, got_qkv, later_qkv, plane)
     up_flip = layout.flip(up_sum, True)
-    down_own, down_other = layout.own_shards(down_sum, down_flip, c)
-    one_other, qkv_parts, up_flip, output, down_other = hold(one_other, qkv_parts, up_flip, output, down_other)
-
-    own_one_grad = one_chip[:rows] + one_other.astype(F32)
-    gain_one_grad = jnp.sum(own_one_grad * unit_one[:rows], axis=0)
-    bias_one_grad = jnp.sum(own_one_grad, axis=0)
-    norm_parts = jnp.stack([gain_one_grad, bias_one_grad, gain_two_grad, bias_two_grad])
+    moved_output = layout.swap(output)
+    one_other, qkv_parts, up_flip, moved_output, near_two_grad = hold(
+        one_other, qkv_parts, up_flip, moved_output, near_two_grad
+    )
+
+    own_one_grad = one_part[:rows] + one_got[:rows].astype(F32) + one_other.astype(F32)
+    norm_parts = [
+        jnp.sum(own_one_grad * unit_one[:rows], axis=0),
+        jnp.sum(own_one_grad, axis=0),
+        jnp.sum(near_two_grad[:rows] * unit_two[:rows], axis=0),
+        jnp.sum(near_two_grad[:rows], axis=0),
+    ]
     input_grad = resid_grad[:rows] + norm_backward(own_one_grad, unit_one[:rows], inverse_one[:rows], ln1_gain)
+    input_grad, norm_parts, qkv_parts = hold(input_grad.astype(BF16), jnp.stack(norm_parts), qkv_parts)
+    moved_input = layout.swap(input_grad)
+    norm_parts = layout.sum_quad(norm_parts)
     qkv_sum = layout.scatter_sum(qkv_parts)
     one_sum = jnp.concatenate([qkv_sum, grad_out_sum.reshape(qkv_sum.shape[0], -1)], axis=1)
-    input_grad, norm_parts, one_sum, output = hold(input_grad.astype(BF16), norm_parts, one_sum, output)
-    one_flip = layout.flip(one_sum, True)
-    moved_input = layout.swap(input_grad)
-    moved_output = layout.swap(output)
-    norm_sums = layout.sum_all(norm_parts)
+    norm_parts, one_sum, moved_input = hold(norm_parts, one_sum, moved_input)
+    down_own, down_other = layout.own_shards(down_sum, down_flip, c)
+    first, second = jnp.split(one_sum, 2)
+    one_own = layout.swap(jnp.where(p == 0, first, second))
+    one_far = layout.swap_over_back(jnp.where(p == 0, second, first))
+    norm_sums = layout.sum_quads(norm_parts)
     up_own, up_other = layout.own_shards(up_sum, up_flip, c)
-    one_flip, norm_sums, up_own, up_other = hold(one_flip, norm_sums, up_own, up_other)
-    one_own, one_other = layout.own_shards(one_sum, one_flip, c)
-    down_got, up_got, one_got = layout.core(down_other), layout.core(up_other), layout.core(one_other)
+    down_got, up_got = layout.core(down_other), layout.core(up_other)
     grad_down = jnp.where(p == c, down_own, down_got)
     grad_up = jnp.where(p == c, up_own, up_got)
-    grad_one = jnp.where(p == c, one_own, one_got)
-    grad_qkv = grad_one[:, : 3 * part_width]
-    grad_out = grad_one[:, 3 * part_width :].reshape(w_out.shape)
+    one_own, one_far, norm_sums, grad_down, grad_up = hold(one_own, one_far, norm_sums, grad_down, grad_up)
+    lanes = lambda part: slice(part * part_width, (part + 1) * part_width)
+    total_of = lambda part: one_own[:, lanes(part)].astype(F32) + one_far[:, lanes(part)].astype(F32)
+    grad_qkv = jnp.stack([total_of(0), total_of(1), total_of(2)], axis=1)
+    grad_out = total_of(3).reshape(w_out.shape)
     output, input_grad = moved_output, moved_input
     return (
         output,

time: 519 us -> 505 us (0.973)
  starting transfers between devices: 96 us -> 78.9 us
  local copies, waits for them, and re-layouts: 48.1 us -> 60 us
  waiting for transfers between devices: 191 us -> 180 us
  other arithmetic: 53.8 us -> 59.3 us
    ppermute x42 -> x43, starting transfers between devices: 81.9 us -> 63.8 us  [permute(): return lax.ppermute(value, AXES, pairs)]
    ppermute x42 -> x43, waiting for transfers between devices: 184 us -> 171 us  [permute(): return lax.ppermute(value, AXES, pairs)]
    unnamed x108 -> x100, local copies, waits for them, and re-layouts: 21 us -> 31.1 us
    convert_element_type x0 -> x2, other arithmetic: none -> 5.48 us  [the longest x1 2.82 us: on_device(): (out_part[rows:2 * rows] + out_got[rows:].astype(F32)).astype(BF16)]
    ppermute x4 -> x3, starting transfers between devices: 13.1 us -> 14.5 us  [flip(): return lax.ppermute(value, AXES, pairs)]
  transfers between devices with their start and end apart: 52 -> 52, of which waited for: 28 -> 28; matrix products, arithmetic and copies ran while one was open for 29% -> 33% of each run, Pallas kernels for 5% -> 5%
where the time goes in v3:
time: 505 us; the launch traced here: 496 us
  waiting for transfers between devices  180 us (36%)
  starting transfers between devices  78.9 us (16%)
  matrix products  77 us (15%)
  local copies, waits for them, and re-layouts  60 us (12%)
  other arithmetic  59.3 us (12%)
  Pallas kernels  23.7 us (5%)
  between operations  16.7 us (3%)
    ppermute x43, waiting for transfers between devices, permute(): return lax.ppermute(value, AXES, pairs)  171 us
    ppermute x43, starting transfers between devices, permute(): return lax.ppermute(value, AXES, pairs)  63.8 us
    unnamed x100, local copies, waits for them, and re-layouts  31.1 us
    dot_general x4, matrix products, dot_nt(): lax.dot_general(left, right, (((1,), (1,)), ((), ())), preferred_element_...  27.8 us
    dot_general x4, matrix products, dot_nn(): lax.dot_general(left, right, (((1,), (0,)), ((), ())), preferred_element_...  25.5 us
    dot_general x4, matrix products, dot_tn(): lax.dot_general(left, right, (((0,), (0,)), ((), ())), preferred_element_...  23.6 us
    ppermute x3, starting transfers between devices, flip(): return lax.ppermute(value, AXES, pairs)  14.5 us
    pallas_call x1, Pallas kernels, attend_back(): pl.pallas_call(functools.partial(attend_back_kernel, heads, slots), in_sp...  13 us
  transfers between devices with their start and end apart: 52, of which 28 were waited for; matrix products, arithmetic and copies ran while one was open for 33% of the time, Pallas kernels for 5%

profile of v3, /device:TPU:1, one launch (start us, length us, event | category | flops | bytes accessed | tf_op | source)
XLA Modules:
  0.0 495.6 jit_solution(11155581517614017141)
XLA Ops:
  10.4 5.6 %collective-permute-start.1 = (bf16[192,1152]{1,0:T(8,128)(2,1)S(1)}, bf16[192,1152]{1,0:T(8,128)(2,1)S(1)}, u32[]{:S(2)}, u32[]{:S(2)}) collective-permute-start(bf16[192,1152]{1,0:T(8,128)(2,1)S(1)} %bitcast.42), channel_id=1, source_target_pairs={{0,0},{1,1},{2,4},{3,5},{4,2},{5,3},{6,6},{7,7},{8,8},{9,9},{10,12... | collective-permute-start | bytes 1327112 | tf_op jit(solution)/shard_map/ppermute | solution.py:192
  16.0 16.3 %collective-permute-done.2 = bf16[192,1152]{1,0:T(8,128)(2,1)S(1)} collective-permute-done((bf16[192,1152]{1,0:T(8,128)(2,1)S(1)}, bf16[192,1152]{1,0:T(8,128)(2,1)S(1)}, u32[]{:S(2)}, u32[]{:S(2)}) %collective-permute-start.2) | collective-permute-done | bytes 442400 | tf_op jit(solution)/shard_map/ppermute | solution.py:192
  42.0 16.1 %collective-permute-done.3 = bf16[256,1536]{1,0:T(8,128)(2,1)S(1)} collective-permute-done((bf16[256,1536]{1,0:T(8,128)(2,1)S(1)}, bf16[256,1536]{1,0:T(8,128)(2,1)S(1)}, u32[]{:S(2)}, u32[]{:S(2)}) %collective-permute-start.3) | collective-permute-done | bytes 786464 | tf_op jit(solution)/shard_map/ppermute | solution.py:192
  58.2 3.4 collective-permute-start.6
  63.5 6.8 %collective-permute-done.6 = bf16[48,1536]{1,0:T(8,128)(2,1)S(1)} collective-permute-done((bf16[48,1536]{1,0:T(8,128)(2,1)S(1)}, bf16[48,1536]{1,0:T(8,128)(2,1)S(1)}, u32[]{:S(2)}, u32[]{:S(2)}) %collective-permute-start.6) | collective-permute-done | bytes 147488 | tf_op jit(solution)/shard_map/ppermute | solution.py:192
  76.4 3.9 collective-permute-start.9
  81.6 2.6 constant_dynamic-update-slice_fusion
  84.2 9.4 %fusion.40.proj_ref = f32[1024,1152]{1,0:T(8,128)} fusion(bf16[1024,1536]{1,0:T(8,128)(2,1)} %constant_dynamic-update-slice_fusion, bf16[1536,1152]{1,0:T(8,128)(2,1)} %all-gather.4.cloned.1.call-done), kind=kOutput, calls=%fused_computation.150 | convolution fusion | flops 3623878656 | bytes 11403264 | tf_op jit(solution)/shard_map/dot_general | solution.py:52
  93.6 9.5 %collective-permute-done.10 = bf16[192,1536]{1,0:T(8,128)(2,1)} collective-permute-done((bf16[192,1536]{1,0:T(8,128)(2,1)}, bf16[192,1536]{1,0:T(8,128)(2,1)}, u32[]{:S(2)}, u32[]{:S(2)}) %collective-permute-start.10) | collective-permute-done | bytes 589856 | tf_op jit(solution)/shard_map/ppermute | solution.py:192
  112.3 10.7 %attend.1 = (bf16[1024,384]{1,0:T(8,128)(2,1)}, bf16[3,1024,128]{2,1,0:T(8,128)(2,1)}, bf16[3,1024,128]{2,1,0:T(8,128)(2,1)}, bf16[3,1024,128]{2,1,0:T(8,128)(2,1)}, f32[3,1024,1]{2,1,0:T(8,128)}) custom-call(s32[1]{0:T(128)} %bitcast.4.index_ref, f32[1024,1152]{1,0:T(8,128)} %fusion.40.proj_ref, f32[1024,128]{1,0:T(8,128)} %get-tuple-element.127.cos_ref, ...), custom_call_target="tpu_custom_call" | custom-call | flops 3000000000 | bytes 12000000 | tf_op jit(solution)/shard_map/attend/pallas_call | solution.py:149
  123.0 3.3 fusion.41
  130.3 7.4 %collective-permute-done.13 = bf16[384,1536]{1,0:T(8,128)(2,1)} collective-permute-done((bf16[384,1536]{1,0:T(8,128)(2,1)}, bf16[384,1536]{1,0:T(8,128)(2,1)}, u32[]{:S(2)}, u32[]{:S(2)}) %collective-permute-start.13) | collective-permute-done | bytes 1179680 | tf_op jit(solution)/shard_map/ppermute | solution.py:232
  147.2 3.5 fusion.12
  151.9 4.4 collective-permute-start.18
  159.3 8.9 %collective-permute-done.16 = bf16[192,1536]{1,0:T(8,128)(2,1)} collective-permute-done((bf16[192,1536]{1,0:T(8,128)(2,1)}, bf16[192,1536]{1,0:T(8,128)(2,1)}, u32[]{:S(2)}, u32[]{:S(2)}) %collective-permute-start.16) | collective-permute-done | bytes 589856 | tf_op jit(solution)/shard_map/ppermute | solution.py:192
  168.8 26.0 %collective-permute-done.18 = bf16[256,1536]{1,0:T(8,128)(2,1)} collective-permute-done((bf16[256,1536]{1,0:T(8,128)(2,1)}, bf16[256,1536]{1,0:T(8,128)(2,1)}, u32[]{:S(2)}, u32[]{:S(2)}) %collective-permute-start.18) | collective-permute-done | bytes 786464 | tf_op jit(solution)/shard_map/ppermute | solution.py:192
  209.9 7.8 %multiply_convert_fusion = (bf16[1024,1536]{1,0:T(8,128)(2,1)S(1)}, f32[1024,1536]{1,0:T(8,128)}) fusion(f32[1536]{0:T(1024)S(1)} %fusion.27, bf16[1024,1536]{1,0:T(8,128)(2,1)S(1)} %constant_dynamic-update-slice_fusion.2, bf16[1536,1536]{1,0:T(8,128)(2,1)S(1)} %constant_dynamic-update-slice_fusion.11), kind=kOutput, calls=%fused_computation.13 | convolution fusion | flops 4847566848 | bytes 17307648 | tf_op jit(solution)/shard_map/dot_general | solution.py:52
  222.2 3.0 collective-permute-done.21
  227.0 6.9 %convolution_convert_fusion.2 = bf16[1536,1536]{1,0:T(8,128)(2,1)} fusion(bf16[1024,1536]{1,0:T(8,128)(2,1)S(1)} %get-tuple-element.164, bf16[1024,1536]{1,0:T(8,128)(2,1)S(1)} %constant_dynamic-update-slice_fusion.6), kind=kOutput, calls=%fused_computation.4 | convolution fusion | flops 4834197504 | bytes 11010048 | tf_op jit(solution)/shard_map/dot_general | solution.py:48
  234.2 11.8 %fusion.7 = bf16[1024,1536]{1,0:T(8,128)(2,1)S(1)} fusion(f32[1024,1536]{1,0:T(8,128)} %get-tuple-element.258, f32[1536]{0:T(1024)S(1)} %fusion.27, bf16[1024,1536]{1,0:T(8,128)(2,1)} %copy-done.32, bf16[1536,1536]{1,0:T(8,128)(2,1)} %all-gather.8.cloned.1.call-done), kind=kOutput, calls=%fused_computation.12 | convolution fusion | flops 4864868352 | bytes 17307648 | tf_op jit(solution)/shard_map/dot_general | solution.py:44
  246.1 7.1 %fusion.42 = f32[1024,1536]{1,0:T(8,128)S(1)} fusion(bf16[1024,1536]{1,0:T(8,128)(2,1)S(1)} %fusion.7, bf16[1536,1536]{1,0:T(8,128)(2,1)} %copy-done.15), kind=kOutput, calls=%fused_computation.152 | convolution fusion | flops 4831838208 | bytes 14155776 | tf_op jit(solution)/shard_map/dot_general | solution.py:44
  254.0 3.0 collective-permute-done.22
  260.1 5.0 %fusion.43 = f32[1024,1536]{1,0:T(8,128)S(1)} fusion(bf16[1024,1536]{1,0:T(8,128)(2,1)S(1)} %copy-done.45, bf16[1536,1536]{1,0:T(8,128)(2,1)S(1)} %copy-done.40), kind=kOutput, calls=%fused_computation.153 | convolution fusion | flops 4831838208 | bytes 14155776 | tf_op jit(solution)/shard_map/dot_general | solution.py:52
  265.1 2.6 copy-done.18
  270.2 7.0 %convolution_convert_fusion.1 = bf16[1536,1536]{1,0:T(8,128)(2,1)} fusion(bf16[1024,1536]{1,0:T(8,128)(2,1)S(1)} %copy-done.27, bf16[1024,1536]{1,0:T(8,128)(2,1)S(1)} %fusion.7), kind=kOutput, calls=%fused_computation.3 | convolution fusion | flops 4834197504 | bytes 11010048 | tf_op jit(solution)/shard_map/dot_general | solution.py:48
  277.3 17.4 %collective-permute-done.23 = bf16[512,1536]{1,0:T(8,128)(2,1)} collective-permute-done((bf16[512,1536]{1,0:T(8,128)(2,1)}, bf16[512,1536]{1,0:T(8,128)(2,1)}, u32[]{:S(2)}, u32[]{:S(2)}) %collective-permute-start.23) | collective-permute-done | bytes 1572896 | tf_op jit(solution)/shard_map/ppermute | solution.py:192
  296.5 3.1 multiply_reduce_fusion.2
  301.3 3.1 fusion.35
  305.5 5.0 collective-permute-start.26
  317.8 2.8 fusion.21
  322.0 4.6 convolution_convert_fusion.4.grad_ref
  326.6 13.0 %attend_back.1 = bf16[1024,1152]{1,0:T(8,128)(2,1)} custom-call(s32[1]{0:T(128)} %bitcast.4.index_ref, bf16[1024,384]{1,0:T(8,128)(2,1)} %convolution_convert_fusion.4.grad_ref, bf16[3,1024,128]{2,1,0:T(8,128)(2,1)} %get-tuple-element.172.q_ref, bf16[3,1024,128]{2,1,0:T(8,128)(2,1)} %get-tuple-element.173.k_ref, ...), custom_call_target="tpu_custom_call" | custom-call | flops 6000000000 | bytes 12000000 | tf_op jit(solution)/shard_map/attend_back/pallas_call | solution.py:167
  339.6 7.3 %convolution_convert_fusion = bf16[1536,1152]{1,0:T(8,128)(2,1)S(1)} fusion(bf16[1024,1536]{1,0:T(8,128)(2,1)} %constant_dynamic-update-slice_fusion, bf16[1024,1152]{1,0:T(8,128)(2,1)} %attend_back.1), kind=kOutput, calls=%fused_computation.2 | convolution fusion | flops 3625648128 | bytes 9043968 | tf_op jit(solution)/shard_map/dot_general | solution.py:48
  352.0 4.2 fusion.44
  357.6 2.9 copy-done.2
  360.5 3.2 fusion.19
  369.1 2.7 fusion.20
  371.8 4.9 collective-permute-start.35
  381.6 7.8 %collective-permute-start.34 = (bf16[384,1536]{1,0:T(8,128)(2,1)}, bf16[384,1536]{1,0:T(8,128)(2,1)}, u32[]{:S(2)}, u32[]{:S(2)}) collective-permute-start(bf16[384,1536]{1,0:T(8,128)(2,1)} %reduce-scatter.6.cloned.1.call-done), channel_id=1, source_target_pairs={{2,0},{3,1},{4,6},{5,7},{10,8},{11,9},{12,14},{13,15},{18,16},{19,... | collective-permute-start | bytes 3538952 | tf_op jit(solution)/shard_map/ppermute | solution.py:232
  397.9 3.5 collective-permute-done.31
  402.3 9.2 %collective-permute-done.33 = bf16[384,1152]{1,0:T(8,128)(2,1)} collective-permute-done((bf16[384,1152]{1,0:T(8,128)(2,1)}, bf16[384,1152]{1,0:T(8,128)(2,1)}, u32[]{:S(2)}, u32[]{:S(2)}) %collective-permute-start.33) | collective-permute-done | bytes 884768 | tf_op jit(solution)/shard_map/ppermute | solution.py:192
  413.3 2.8 multiply_reduce_fusion.3
  416.7 13.2 %collective-permute-start.36 = (f32[4,1536]{1,0:T(4,128)S(1)}, f32[4,1536]{1,0:T(4,128)S(1)}, u32[]{:S(2)}, u32[]{:S(2)}) collective-permute-start(f32[4,1536]{1,0:T(4,128)S(1)} %pad_maximum_fusion.7), channel_id=1, source_target_pairs={{0,4},{1,5},{2,6},{3,7},{4,0},{5,1},{6,2},{7,3},{8,12},{9,13},{10,... | collective-permute-start | bytes 73736 | tf_op jit(solution)/shard_map/ppermute | solution.py:192
  437.6 3.7 collective-permute-done.37
  441.3 9.9 %collective-permute-done.38 = bf16[256,1536]{1,0:T(8,128)(2,1)S(1)} collective-permute-done((bf16[256,1536]{1,0:T(8,128)(2,1)S(1)}, bf16[256,1536]{1,0:T(8,128)(2,1)S(1)}, u32[]{:S(2)}, u32[]{:S(2)}) %collective-permute-start.38) | collective-permute-done | bytes 786464 | tf_op jit(solution)/shard_map/ppermute | solution.py:192
  451.2 3.6 collective-permute-done.41
  455.3 3.2 collective-permute-start.39
  462.9 20.2 %collective-permute-done.39 = bf16[192,1536]{1,0:T(8,128)(2,1)S(1)} collective-permute-done((bf16[192,1536]{1,0:T(8,128)(2,1)S(1)}, bf16[192,1536]{1,0:T(8,128)(2,1)S(1)}, u32[]{:S(2)}, u32[]{:S(2)}) %collective-permute-start.39) | collective-permute-done | bytes 589856 | tf_op jit(solution)/shard_map/ppermute | solution.py:192
  (271 shorter events, 135.6 us)
Async XLA Ops:
  7.2 77.0 %all-gather.4.cloned.1.call-start = ((), (), s32[]{:S(2)}) async-start(), calls=%async_computation.3 | async-start | bytes 4423680 | tf_op jit(solution)/shard_map/all_gather | solution.py:247
  9.9 22.5 %collective-permute-start.2 = (bf16[192,1152]{1,0:T(8,128)(2,1)S(1)}, bf16[192,1152]{1,0:T(8,128)(2,1)S(1)}, u32[]{:S(2)}, u32[]{:S(2)}) collective-permute-start(bf16[192,1152]{1,0:T(8,128)(2,1)S(1)} %bitcast.41), channel_id=1, source_target_pairs={{0,2},{1,3},{2,6},{3,7},{4,0},{5,1},{6,4},{7,5},{8,10},{9,11},{10,... | collective-permute-start | bytes 1327112 | tf_op jit(solution)/shard_map/ppermute | solution.py:192
  10.4 23.2 %collective-permute-start.1 = (bf16[192,1152]{1,0:T(8,128)(2,1)S(1)}, bf16[192,1152]{1,0:T(8,128)(2,1)S(1)}, u32[]{:S(2)}, u32[]{:S(2)}) collective-permute-start(bf16[192,1152]{1,0:T(8,128)(2,1)S(1)} %bitcast.42), channel_id=1, source_target_pairs={{0,0},{1,1},{2,4},{3,5},{4,2},{5,3},{6,6},{7,7},{8,8},{9,9},{10,12... | collective-permute-start | bytes 1327112 | tf_op jit(solution)/shard_map/ppermute | solution.py:192
  34.8 88.2 %all-gather.6.cloned.1.call-start = ((), (), s32[]{:S(2)}) async-start(), calls=%async_computation.4 | async-start | bytes 1474560 | tf_op jit(solution)/shard_map/all_gather | solution.py:247
  35.3 5.3 %collective-permute-start.4 = (bf16[192,1536]{1,0:T(8,128)(2,1)S(1)}, bf16[192,1536]{1,0:T(8,128)(2,1)S(1)}, u32[]{:S(2)}, u32[]{:S(2)}) collective-permute-start(bf16[192,1536]{1,0:T(8,128)(2,1)S(1)} %copy-done.29), channel_id=1, source_target_pairs={{0,4},{1,5},{2,6},{3,7},{4,0},{5,1},{6,2},{7,3},{8,12},{9,13},{10,... | collective-permute-start | bytes 1769480 | tf_op jit(solution)/shard_map/ppermute | solution.py:192
  35.4 22.7 %collective-permute-start.3 = (bf16[256,1536]{1,0:T(8,128)(2,1)S(1)}, bf16[256,1536]{1,0:T(8,128)(2,1)S(1)}, u32[]{:S(2)}, u32[]{:S(2)}) collective-permute-start(bf16[256,1536]{1,0:T(8,128)(2,1)S(1)} %copy-done.42), channel_id=1, source_target_pairs={{0,0},{1,1},{2,4},{3,5},{4,2},{5,3},{6,6},{7,7},{8,8},{9,9},{10,12... | collective-permute-start | bytes 2359304 | tf_op jit(solution)/shard_map/ppermute | solution.py:192
  58.1 14.4 %collective-permute-start.5 = (bf16[256,1536]{1,0:T(8,128)(2,1)S(1)}, bf16[256,1536]{1,0:T(8,128)(2,1)S(1)}, u32[]{:S(2)}, u32[]{:S(2)}) collective-permute-start(bf16[256,1536]{1,0:T(8,128)(2,1)S(1)} %collective-permute-done.3), channel_id=1, source_target_pairs={{0,1},{1,0},{2,3},{3,2},{4,5},{5,4},{6,7},{7,6},{8,9},{9,8},{10,11... | collective-permute-start | bytes 2359304 | tf_op jit(solution)/shard_map/ppermute | solution.py:192
  58.2 5.3 %collective-permute-start.7 = (bf16[48,1536]{1,0:T(8,128)(2,1)S(1)}, bf16[48,1536]{1,0:T(8,128)(2,1)S(1)}, u32[]{:S(2)}, u32[]{:S(2)}) collective-permute-start(bf16[48,1536]{1,0:T(8,128)(2,1)S(1)} %copy-done.43), channel_id=1, source_target_pairs={{0,2},{1,3},{2,6},{3,7},{4,0},{5,1},{6,4},{7,5},{8,10},{9,11},{10,... | collective-permute-start | bytes 442376 | tf_op jit(solution)/shard_map/ppermute | solution.py:192
  58.2 12.1 %collective-permute-start.6 = (bf16[48,1536]{1,0:T(8,128)(2,1)S(1)}, bf16[48,1536]{1,0:T(8,128)(2,1)S(1)}, u32[]{:S(2)}, u32[]{:S(2)}) collective-permute-start(bf16[48,1536]{1,0:T(8,128)(2,1)S(1)} %copy-done.43), channel_id=1, source_target_pairs={{0,0},{1,1},{2,4},{3,5},{4,2},{5,3},{6,6},{7,7},{8,8},{9,9},{10,12... | collective-permute-start | bytes 442376 | tf_op jit(solution)/shard_map/ppermute | solution.py:192
  75.8 5.8 %collective-permute-start.8 = (bf16[512,1536]{1,0:T(8,128)(2,1)S(1)}, bf16[512,1536]{1,0:T(8,128)(2,1)}, u32[]{:S(2)}, u32[]{:S(2)}) collective-permute-start(bf16[512,1536]{1,0:T(8,128)(2,1)S(1)} %get-tuple-element.119), channel_id=1, source_target_pairs={{0,4},{1,5},{2,6},{3,7},{4,0},{5,1},{6,2},{7,3},{8,12},{9,13},{10,... | collective-permute-start | bytes 4718600 | tf_op jit(solution)/shard_map/ppermute | solution.py:192
  75.8 158.4 %all-gather.8.cloned.1.call-start = ((), (), s32[]{:S(2)}) async-start(), calls=%async_computation.5 | async-start | bytes 5898240 | tf_op jit(solution)/shard_map/all_gather | solution.py:247
  75.8 27.2 %collective-permute-start.10 = (bf16[192,1536]{1,0:T(8,128)(2,1)}, bf16[192,1536]{1,0:T(8,128)(2,1)}, u32[]{:S(2)}, u32[]{:S(2)}) collective-permute-start(bf16[192,1536]{1,0:T(8,128)(2,1)} %param.22), channel_id=1, source_target_pairs={{0,2},{1,3},{2,6},{3,7},{4,0},{5,1},{6,4},{7,5},{8,10},{9,11},{10,... | collective-permute-start | bytes 1769480 | tf_op jit(solution)/shard_map/ppermute | solution.py:192
  76.4 28.4 %collective-permute-start.9 = (bf16[192,1536]{1,0:T(8,128)(2,1)}, bf16[192,1536]{1,0:T(8,128)(2,1)}, u32[]{:S(2)}, u32[]{:S(2)}) collective-permute-start(bf16[192,1536]{1,0:T(8,128)(2,1)} %param.22), channel_id=1, source_target_pairs={{0,0},{1,1},{2,4},{3,5},{4,2},{5,3},{6,6},{7,7},{8,8},{9,9},{10,12... | collective-permute-start | bytes 1769480 | tf_op jit(solution)/shard_map/ppermute | solution.py:192
  106.9 30.8 %collective-permute-start.13 = (bf16[384,1536]{1,0:T(8,128)(2,1)}, bf16[384,1536]{1,0:T(8,128)(2,1)}, u32[]{:S(2)}, u32[]{:S(2)}) collective-permute-start(bf16[384,1536]{1,0:T(8,128)(2,1)} %maximum_select_fusion), channel_id=1, source_target_pairs={{0,2},{1,3},{6,4},{7,5},{8,10},{9,11},{14,12},{15,13},{16,18},{17,... | collective-permute-start | bytes 3538952 | tf_op jit(solution)/shard_map/ppermute | solution.py:232
  108.7 30.0 %collective-permute-start.12 = (bf16[384,1536]{1,0:T(8,128)(2,1)S(1)}, bf16[384,1536]{1,0:T(8,128)(2,1)}, u32[]{:S(2)}, u32[]{:S(2)}) collective-permute-start(bf16[384,1536]{1,0:T(8,128)(2,1)S(1)} %maximum_select_fusion.1), channel_id=1, source_target_pairs={{0,16},{1,17},{2,18},{3,19},{4,20},{5,21},{6,22},{7,23},{8,24},{9,... | collective-permute-start | bytes 3538952 | tf_op jit(solution)/shard_map/ppermute | solution.py:192
  110.0 28.6 %collective-permute-start.11 = (bf16[384,1536]{1,0:T(8,128)(2,1)S(1)}, bf16[384,1536]{1,0:T(8,128)(2,1)}, u32[]{:S(2)}, u32[]{:S(2)}) collective-permute-start(bf16[384,1536]{1,0:T(8,128)(2,1)S(1)} %maximum_select_fusion.1), channel_id=1, source_target_pairs={{0,8},{1,9},{2,10},{3,11},{4,12},{5,13},{6,14},{7,15},{8,0},{9,1},... | collective-permute-start | bytes 3538952 | tf_op jit(solution)/shard_map/ppermute | solution.py:192
  138.6 7.4 %collective-permute-start.14 = (bf16[512,1536]{1,0:T(8,128)(2,1)}, bf16[512,1536]{1,0:T(8,128)(2,1)S(1)}, u32[]{:S(2)}, u32[]{:S(2)}) collective-permute-start(bf16[512,1536]{1,0:T(8,128)(2,1)} %slice.250), channel_id=1, source_target_pairs={{0,4},{1,5},{2,6},{3,7},{4,0},{5,1},{6,2},{7,3},{8,12},{9,13},{10,... | collective-permute-start | bytes 4718600 | tf_op jit(solution)/shard_map/ppermute | solution.py:192
  150.7 44.8 %collective-permute-start.15 = (bf16[512,1536]{1,0:T(8,128)(2,1)}, bf16[512,1536]{1,0:T(8,128)(2,1)S(1)}, u32[]{:S(2)}, u32[]{:S(2)}) collective-permute-start(bf16[512,1536]{1,0:T(8,128)(2,1)} %fusion.12), channel_id=1, source_target_pairs={{0,1},{1,0},{2,3},{3,2},{4,5},{5,4},{6,7},{7,6},{8,9},{9,8},{10,11... | collective-permute-start | bytes 4718600 | tf_op jit(solution)/shard_map/ppermute | solution.py:192
  151.9 43.0 %collective-permute-start.18 = (bf16[256,1536]{1,0:T(8,128)(2,1)}, bf16[256,1536]{1,0:T(8,128)(2,1)}, u32[]{:S(2)}, u32[]{:S(2)}) collective-permute-start(bf16[256,1536]{1,0:T(8,128)(2,1)} %param.13), channel_id=1, source_target_pairs={{0,0},{1,1},{2,4},{3,5},{4,2},{5,3},{6,6},{7,7},{8,8},{9,9},{10,12... | collective-permute-start | bytes 2359304 | tf_op jit(solution)/shard_map/ppermute | solution.py:192
  156.3 11.9 %collective-permute-start.16 = (bf16[192,1536]{1,0:T(8,128)(2,1)}, bf16[192,1536]{1,0:T(8,128)(2,1)}, u32[]{:S(2)}, u32[]{:S(2)}) collective-permute-start(bf16[192,1536]{1,0:T(8,128)(2,1)} %slice.130), channel_id=1, source_target_pairs={{0,16},{1,17},{2,18},{3,19},{4,20},{5,21},{6,22},{7,23},{8,24},{9,... | collective-permute-start | bytes 1769480 | tf_op jit(solution)/shard_map/ppermute | solution.py:192
  157.4 11.4 %collective-permute-start.17 = (bf16[192,1536]{1,0:T(8,128)(2,1)}, bf16[192,1536]{1,0:T(8,128)(2,1)}, u32[]{:S(2)}, u32[]{:S(2)}) collective-permute-start(bf16[192,1536]{1,0:T(8,128)(2,1)} %slice.131), channel_id=1, source_target_pairs={{0,8},{1,9},{2,10},{3,11},{4,12},{5,13},{6,14},{7,15},{8,0},{9,1},... | collective-permute-start | bytes 1769480 | tf_op jit(solution)/shard_map/ppermute | solution.py:192
  159.0 145.3 %reduce-scatter.4.cloned.1.call-start = ((), (), s32[]{:S(2)}) async-start(), calls=%async_computation.6 | async-start | bytes 5898240 | tf_op jit(solution)/shard_map/reduce_scatter | solution.py:279
  200.1 20.0 %collective-permute-start.20 = (bf16[256,1536]{1,0:T(8,128)(2,1)}, bf16[256,1536]{1,0:T(8,128)(2,1)S(1)}, u32[]{:S(2)}, u32[]{:S(2)}) collective-permute-start(bf16[256,1536]{1,0:T(8,128)(2,1)} %collective-permute-done.18), channel_id=1, source_target_pairs={{0,1},{1,0},{2,3},{3,2},{4,5},{5,4},{6,7},{7,6},{8,9},{9,8},{10,11... | collective-permute-start | bytes 2359304 | tf_op jit(solution)/shard_map/ppermute | solution.py:192
  202.2 7.4 %collective-permute-start.19 = (bf16[512,1536]{1,0:T(8,128)(2,1)S(1)}, bf16[512,1536]{1,0:T(8,128)(2,1)S(1)}, u32[]{:S(2)}, u32[]{:S(2)}) collective-permute-start(bf16[512,1536]{1,0:T(8,128)(2,1)S(1)} %get-tuple-element.153), channel_id=1, source_target_pairs={{0,4},{1,5},{2,6},{3,7},{4,0},{5,1},{6,2},{7,3},{8,12},{9,13},{10,... | collective-permute-start | bytes 4718600 | tf_op jit(solution)/shard_map/ppermute | solution.py:192
  221.4 3.8 collective-permute-start.21
  233.9 137.8 %reduce-scatter.6.cloned.1.call-start = ((), (), s32[]{:S(2)}) async-start(), calls=%async_computation.7 | async-start | bytes 5898240 | tf_op jit(solution)/shard_map/reduce_scatter | solution.py:279
  258.8 35.9 %collective-permute-start.23 = (bf16[512,1536]{1,0:T(8,128)(2,1)}, bf16[512,1536]{1,0:T(8,128)(2,1)}, u32[]{:S(2)}, u32[]{:S(2)}) collective-permute-start(bf16[512,1536]{1,0:T(8,128)(2,1)} %fusion.13), channel_id=1, source_target_pairs={{0,1},{1,0},{2,3},{3,2},{4,5},{5,4},{6,7},{7,6},{8,9},{9,8},{10,11... | collective-permute-start | bytes 4718600 | tf_op jit(solution)/shard_map/ppermute | solution.py:192
  277.2 119.5 %reduce-scatter.8.cloned.1.call-start = ((), (), s32[]{:S(2)}) async-start(), calls=%async_computation.8 | async-start | bytes 1474560 | tf_op jit(solution)/shard_map/reduce_scatter | solution.py:279
  304.4 7.6 %collective-permute-start.24 = (bf16[512,1536]{1,0:T(8,128)(2,1)}, bf16[512,1536]{1,0:T(8,128)(2,1)}, u32[]{:S(2)}, u32[]{:S(2)}) collective-permute-start(bf16[512,1536]{1,0:T(8,128)(2,1)} %get-tuple-element.168), channel_id=1, source_target_pairs={{0,4},{1,5},{2,6},{3,7},{4,0},{5,1},{6,2},{7,3},{8,12},{9,13},{10,... | collective-permute-start | bytes 4718600 | tf_op jit(solution)/shard_map/ppermute | solution.py:192
  305.5 12.3 %collective-permute-start.25 = (bf16[512,1536]{1,0:T(8,128)(2,1)}, bf16[512,1536]{1,0:T(8,128)(2,1)}, u32[]{:S(2)}, u32[]{:S(2)}) collective-permute-start(bf16[512,1536]{1,0:T(8,128)(2,1)} %slice.248), channel_id=1, source_target_pairs={{0,4},{1,5},{2,6},{3,7},{4,0},{5,1},{6,2},{7,3},{8,12},{9,13},{10,... | collective-permute-start | bytes 4718600 | tf_op jit(solution)/shard_map/ppermute | solution.py:192
  305.5 44.3 %collective-permute-start.26 = (bf16[384,1536]{1,0:T(8,128)(2,1)}, bf16[384,1536]{1,0:T(8,128)(2,1)}, u32[]{:S(2)}, u32[]{:S(2)}) collective-permute-start(bf16[384,1536]{1,0:T(8,128)(2,1)} %reduce-scatter.4.cloned.1.call-done), channel_id=1, source_target_pairs={{2,0},{3,1},{4,6},{5,7},{10,8},{11,9},{12,14},{13,15},{18,16},{19,... | collective-permute-start | bytes 3538952 | tf_op jit(solution)/shard_map/ppermute | solution.py:232
  320.6 29.8 %collective-permute-start.27 = (bf16[256,1536]{1,0:T(8,128)(2,1)}, bf16[256,1536]{1,0:T(8,128)(2,1)}, u32[]{:S(2)}, u32[]{:S(2)}) collective-permute-start(bf16[256,1536]{1,0:T(8,128)(2,1)} %fusion.21), channel_id=1, source_target_pairs={{0,1},{1,0},{2,3},{3,2},{4,5},{5,4},{6,7},{7,6},{8,9},{9,8},{10,11... | collective-permute-start | bytes 2359304 | tf_op jit(solution)/shard_map/ppermute | solution.py:192
  350.4 13.3 %collective-permute-start.28 = (bf16[192,1152]{1,0:T(8,128)(2,1)S(1)}, bf16[192,1152]{1,0:T(8,128)(2,1)S(1)}, u32[]{:S(2)}, u32[]{:S(2)}) collective-permute-start(bf16[192,1152]{1,0:T(8,128)(2,1)S(1)} %get-tuple-element.178), channel_id=1, source_target_pairs={{0,8},{1,9},{2,10},{3,11},{4,12},{5,13},{6,14},{7,15},{8,0},{9,1},... | collective-permute-start | bytes 1327112 | tf_op jit(solution)/shard_map/ppermute | solution.py:192
  351.8 12.7 %collective-permute-start.29 = (bf16[192,1152]{1,0:T(8,128)(2,1)S(1)}, bf16[192,1152]{1,0:T(8,128)(2,1)S(1)}, u32[]{:S(2)}, u32[]{:S(2)}) collective-permute-start(bf16[192,1152]{1,0:T(8,128)(2,1)S(1)} %get-tuple-element.179), channel_id=1, source_target_pairs={{0,16},{1,17},{2,18},{3,19},{4,20},{5,21},{6,22},{7,23},{8,24},{9,... | collective-permute-start | bytes 1327112 | tf_op jit(solution)/shard_map/ppermute | solution.py:192
  365.3 3.8 collective-permute-start.30
  371.7 29.6 %collective-permute-start.31 = (bf16[256,1536]{1,0:T(8,128)(2,1)}, bf16[256,1536]{1,0:T(8,128)(2,1)}, u32[]{:S(2)}, u32[]{:S(2)}) collective-permute-start(bf16[256,1536]{1,0:T(8,128)(2,1)} %fusion.20), channel_id=1, source_target_pairs={{0,1},{1,0},{2,3},{3,2},{4,5},{5,4},{6,7},{7,6},{8,9},{9,8},{10,11... | collective-permute-start | bytes 2359304 | tf_op jit(solution)/shard_map/ppermute | solution.py:192
  371.8 30.6 %collective-permute-start.35 = (bf16[256,1536]{1,0:T(8,128)(2,1)}, bf16[256,1536]{1,0:T(8,128)(2,1)}, u32[]{:S(2)}, u32[]{:S(2)}) collective-permute-start(bf16[256,1536]{1,0:T(8,128)(2,1)} %fusion.19), channel_id=1, source_target_pairs={{0,0},{1,1},{2,4},{3,5},{4,2},{5,3},{6,6},{7,7},{8,8},{9,9},{10,12... | collective-permute-start | bytes 2359304 | tf_op jit(solution)/shard_map/ppermute | solution.py:192
  380.4 21.9 %collective-permute-start.32 = (bf16[384,1152]{1,0:T(8,128)(2,1)}, bf16[384,1152]{1,0:T(8,128)(2,1)}, u32[]{:S(2)}, u32[]{:S(2)}) collective-permute-start(bf16[384,1152]{1,0:T(8,128)(2,1)} %pad_maximum_fusion.2), channel_id=1, source_target_pairs={{0,8},{1,9},{2,10},{3,11},{4,12},{5,13},{6,14},{7,15},{8,0},{9,1},... | collective-permute-start | bytes 2654216 | tf_op jit(solution)/shard_map/ppermute | solution.py:192
  381.6 30.0 %collective-permute-start.34 = (bf16[384,1536]{1,0:T(8,128)(2,1)}, bf16[384,1536]{1,0:T(8,128)(2,1)}, u32[]{:S(2)}, u32[]{:S(2)}) collective-permute-start(bf16[384,1536]{1,0:T(8,128)(2,1)} %reduce-scatter.6.cloned.1.call-done), channel_id=1, source_target_pairs={{2,0},{3,1},{4,6},{5,7},{10,8},{11,9},{12,14},{13,15},{18,16},{19,... | collective-permute-start | bytes 3538952 | tf_op jit(solution)/shard_map/ppermute | solution.py:232
  390.3 21.2 %collective-permute-start.33 = (bf16[384,1152]{1,0:T(8,128)(2,1)}, bf16[384,1152]{1,0:T(8,128)(2,1)}, u32[]{:S(2)}, u32[]{:S(2)}) collective-permute-start(bf16[384,1152]{1,0:T(8,128)(2,1)} %pad_maximum_fusion.3), channel_id=1, source_target_pairs={{0,16},{1,17},{2,18},{3,19},{4,20},{5,21},{6,22},{7,23},{8,24},{9,... | collective-permute-start | bytes 2654216 | tf_op jit(solution)/shard_map/ppermute | solution.py:192
  401.4 58.6 %collective-permute-start.44 = (f32[192,1536]{1,0:T(8,128)}, f32[192,1536]{1,0:T(8,128)S(1)}, u32[]{:S(2)}, u32[]{:S(2)}) collective-permute-start(f32[192,1536]{1,0:T(8,128)} %slice_select_fusion.1), channel_id=1, source_target_pairs={{0,4},{1,5},{2,6},{3,7},{4,0},{5,1},{6,2},{7,3},{8,12},{9,13},{10,... | collective-permute-start | bytes 3538952 | tf_op jit(solution)/shard_map/ppermute | solution.py:192
  416.7 19.1 %collective-permute-start.36 = (f32[4,1536]{1,0:T(4,128)S(1)}, f32[4,1536]{1,0:T(4,128)S(1)}, u32[]{:S(2)}, u32[]{:S(2)}) collective-permute-start(f32[4,1536]{1,0:T(4,128)S(1)} %pad_maximum_fusion.7), channel_id=1, source_target_pairs={{0,4},{1,5},{2,6},{3,7},{4,0},{5,1},{6,2},{7,3},{8,12},{9,13},{10,... | collective-permute-start | bytes 73736 | tf_op jit(solution)/shard_map/ppermute | solution.py:192
  429.9 21.3 %collective-permute-start.38 = (bf16[256,1536]{1,0:T(8,128)(2,1)S(1)}, bf16[256,1536]{1,0:T(8,128)(2,1)S(1)}, u32[]{:S(2)}, u32[]{:S(2)}) collective-permute-start(bf16[256,1536]{1,0:T(8,128)(2,1)S(1)} %fusion.16), channel_id=1, source_target_pairs={{0,0},{1,1},{2,4},{3,5},{4,2},{5,3},{6,6},{7,7},{8,8},{9,9},{10,12... | collective-permute-start | bytes 2359304 | tf_op jit(solution)/shard_map/ppermute | solution.py:192
  433.9 27.7 %collective-permute-start.45 = (f32[192,1536]{1,0:T(8,128)S(1)}, f32[192,1536]{1,0:T(8,128)S(1)}, u32[]{:S(2)}, u32[]{:S(2)}) collective-permute-start(f32[192,1536]{1,0:T(8,128)S(1)} %slice_select_fusion), channel_id=1, source_target_pairs={{0,4},{1,5},{2,6},{3,7},{4,0},{5,1},{6,2},{7,3},{8,12},{9,13},{10,... | collective-permute-start | bytes 3538952 | tf_op jit(solution)/shard_map/ppermute | solution.py:192
  435.8 5.4 %collective-permute-start.37 = (f32[4,1536]{1,0:T(4,128)S(1)}, f32[4,1536]{1,0:T(4,128)S(1)}, u32[]{:S(2)}, u32[]{:S(2)}) collective-permute-start(f32[4,1536]{1,0:T(4,128)S(1)} %add.263), channel_id=1, source_target_pairs={{0,1},{1,0},{2,3},{3,2},{4,5},{5,4},{6,7},{7,6},{8,9},{9,8},{10,11... | collective-permute-start | bytes 73736 | tf_op jit(solution)/shard_map/ppermute | solution.py:192
  454.8 3.7 collective-permute-start.42
  455.2 7.6 %collective-permute-start.40 = (bf16[192,1536]{1,0:T(8,128)(2,1)S(1)}, bf16[192,1536]{1,0:T(8,128)(2,1)S(1)}, u32[]{:S(2)}, u32[]{:S(2)}) collective-permute-start(bf16[192,1536]{1,0:T(8,128)(2,1)S(1)} %get-tuple-element.248), channel_id=1, source_target_pairs={{0,4},{1,5},{2,0},{3,1},{4,6},{5,7},{6,2},{7,3},{8,12},{9,13},{10,... | collective-permute-start | bytes 1769480 | tf_op jit(solution)/shard_map/ppermute | solution.py:192
  455.3 27.8 %collective-permute-start.39 = (bf16[192,1536]{1,0:T(8,128)(2,1)S(1)}, bf16[192,1536]{1,0:T(8,128)(2,1)S(1)}, u32[]{:S(2)}, u32[]{:S(2)}) collective-permute-start(bf16[192,1536]{1,0:T(8,128)(2,1)S(1)} %get-tuple-element.249), channel_id=1, source_target_pairs={{0,0},{1,1},{2,4},{3,5},{4,2},{5,3},{6,6},{7,7},{8,8},{9,9},{10,12... | collective-permute-start | bytes 1769480 | tf_op jit(solution)/shard_map/ppermute | solution.py:192
  (52 other events, 773.4 us)
Sparse Core Ops, SparseCore 0:
  34.9 48.9 all-gather.3
  86.3 29.3 all-gather.5
  159.1 58.8 all-gather.7
  234.1 56.3 reduce-scatter.3
  293.3 57.0 reduce-scatter.5
  365.6 31.0 reduce-scatter.7

commit v4 on v3

--- a/solution.py
+++ b/solution.py
@@ -409,17 +409,15 @@
     attn_send = attn_part[2 * rows :].astype(BF16)
     attn_send, pieces_up, flip_down = hold(attn_send, pieces_up, flip_down)
 
-    attn_got = layout.core(attn_send)
+    attn_got, pieces_up, flip_down = hold(layout.core(attn_send), pieces_up, flip_down)
+    attn_chip = attn_part[: 2 * rows] + attn_got.astype(F32)
+    attn_low, pieces_up, flip_down, cotangent = hold(attn_chip.astype(BF16), pieces_up, flip_down, cotangent)
+    attn_other = layout.pair(attn_low)
     block_down = jnp.where(p == c, both_down, flip_down)
-    sends_up = layout.far_sends(pieces_up)
-    attn_got, block_down, sends_up = hold(attn_got, block_down, sends_up)
     wide_down = layout.gather(block_down)
-    attn_chip = attn_part[: 2 * rows] + attn_got.astype(F32)
-    attn_low, sends_up, cotangent = hold(attn_chip.astype(BF16), sends_up, cotangent)
-    attn_other = layout.pair(attn_low)
-    pieces_up = layout.gather_far(pieces_up, sends_up)
+    pieces_up = layout.gather_far(pieces_up, layout.far_sends(pieces_up))
     moved_cot = layout.swap(cotangent)
-    attn_other, pieces_up, moved_cot = hold(attn_other, pieces_up, moved_cot)
+    attn_other, pieces_up, moved_cot, block_down = hold(attn_other, pieces_up, moved_cot, block_down)
 
     def pair_order(other):
         other = other.astype(F32)

time: 505 us -> 498 us (0.986)
  local copies, waits for them, and re-layouts: 60 us -> 54.5 us
  transfers between devices with their start and end apart: 52 -> 52, of which waited for: 28 -> 30; matrix products, arithmetic and copies ran while one was open for 33% -> 33% of each run, Pallas kernels for 5% -> 5%
where the time goes in v4:
time: 498 us; the launch traced here: 489 us
  waiting for transfers between devices  180 us (36%)
  starting transfers between devices  79.6 us (16%)
  matrix products  76.8 us (15%)
  other arithmetic  56.9 us (11%)
  local copies, waits for them, and re-layouts  54.5 us (11%)
  Pallas kernels  23.7 us (5%)
  between operations  16.8 us (3%)
    ppermute x43, waiting for transfers between devices, permute(): return lax.ppermute(value, AXES, pairs)  167 us
    ppermute x43, starting transfers between devices, permute(): return lax.ppermute(value, AXES, pairs)  65.2 us
    dot_general x4, matrix products, dot_nt(): lax.dot_general(left, right, (((1,), (1,)), ((), ())), preferred_element_...  27.7 us
    unnamed x100, local copies, waits for them, and re-layouts  26.8 us
    dot_general x4, matrix products, dot_nn(): lax.dot_general(left, right, (((1,), (0,)), ((), ())), preferred_element_...  25.5 us
    dot_general x4, matrix products, dot_tn(): lax.dot_general(left, right, (((0,), (0,)), ((), ())), preferred_element_...  23.6 us
    ppermute x3, starting transfers between devices, flip(): return lax.ppermute(value, AXES, pairs)  13.7 us
    pallas_call x1, Pallas kernels, attend_back(): pl.pallas_call(functools.partial(attend_back_kernel, heads, slots), in_sp...  13 us
  transfers between devices with their start and end apart: 52, of which 30 were waited for; matrix products, arithmetic and copies ran while one was open for 33% of the time, Pallas kernels for 5%

profile of v4, /device:TPU:1, one launch (start us, length us, event | category | flops | bytes accessed | tf_op | source)
XLA Modules:
  0.0 488.6 jit_solution(15658442174639578388)
XLA Ops:
  10.4 5.6 %collective-permute-start.1 = (bf16[192,1152]{1,0:T(8,128)(2,1)S(1)}, bf16[192,1152]{1,0:T(8,128)(2,1)S(1)}, u32[]{:S(2)}, u32[]{:S(2)}) collective-permute-start(bf16[192,1152]{1,0:T(8,128)(2,1)S(1)} %bitcast.42), channel_id=1, source_target_pairs={{0,0},{1,1},{2,4},{3,5},{4,2},{5,3},{6,6},{7,7},{8,8},{9,9},{10,12... | collective-permute-start | bytes 1327112 | tf_op jit(solution)/shard_map/ppermute | solution.py:192
  16.0 16.3 %collective-permute-done.2 = bf16[192,1152]{1,0:T(8,128)(2,1)S(1)} collective-permute-done((bf16[192,1152]{1,0:T(8,128)(2,1)S(1)}, bf16[192,1152]{1,0:T(8,128)(2,1)S(1)}, u32[]{:S(2)}, u32[]{:S(2)}) %collective-permute-start.2) | collective-permute-done | bytes 442400 | tf_op jit(solution)/shard_map/ppermute | solution.py:192
  42.0 16.1 %collective-permute-done.3 = bf16[256,1536]{1,0:T(8,128)(2,1)S(1)} collective-permute-done((bf16[256,1536]{1,0:T(8,128)(2,1)S(1)}, bf16[256,1536]{1,0:T(8,128)(2,1)S(1)}, u32[]{:S(2)}, u32[]{:S(2)}) %collective-permute-start.3) | collective-permute-done | bytes 786464 | tf_op jit(solution)/shard_map/ppermute | solution.py:192
  58.2 3.4 collective-permute-start.6
  63.5 6.8 %collective-permute-done.6 = bf16[48,1536]{1,0:T(8,128)(2,1)S(1)} collective-permute-done((bf16[48,1536]{1,0:T(8,128)(2,1)S(1)}, bf16[48,1536]{1,0:T(8,128)(2,1)S(1)}, u32[]{:S(2)}, u32[]{:S(2)}) %collective-permute-start.6) | collective-permute-done | bytes 147488 | tf_op jit(solution)/shard_map/ppermute | solution.py:192
  76.4 3.9 collective-permute-start.9
  81.6 2.6 constant_dynamic-update-slice_fusion
  84.2 9.4 %fusion.40.proj_ref = f32[1024,1152]{1,0:T(8,128)} fusion(bf16[1024,1536]{1,0:T(8,128)(2,1)} %constant_dynamic-update-slice_fusion, bf16[1536,1152]{1,0:T(8,128)(2,1)} %all-gather.4.cloned.1.call-done), kind=kOutput, calls=%fused_computation.150 | convolution fusion | flops 3623878656 | bytes 11403264 | tf_op jit(solution)/shard_map/dot_general | solution.py:52
  93.6 9.5 %collective-permute-done.10 = bf16[192,1536]{1,0:T(8,128)(2,1)} collective-permute-done((bf16[192,1536]{1,0:T(8,128)(2,1)}, bf16[192,1536]{1,0:T(8,128)(2,1)}, u32[]{:S(2)}, u32[]{:S(2)}) %collective-permute-start.10) | collective-permute-done | bytes 589856 | tf_op jit(solution)/shard_map/ppermute | solution.py:192
  112.3 10.7 %attend.1 = (bf16[1024,384]{1,0:T(8,128)(2,1)}, bf16[3,1024,128]{2,1,0:T(8,128)(2,1)}, bf16[3,1024,128]{2,1,0:T(8,128)(2,1)}, bf16[3,1024,128]{2,1,0:T(8,128)(2,1)}, f32[3,1024,1]{2,1,0:T(8,128)}) custom-call(s32[1]{0:T(128)} %bitcast.4.index_ref, f32[1024,1152]{1,0:T(8,128)} %fusion.40.proj_ref, f32[1024,128]{1,0:T(8,128)} %get-tuple-element.130.cos_ref, ...), custom_call_target="tpu_custom_call" | custom-call | flops 3000000000 | bytes 12000000 | tf_op jit(solution)/shard_map/attend/pallas_call | solution.py:149
  123.0 3.3 fusion.41
  126.5 11.2 %collective-permute-done.13 = bf16[384,1536]{1,0:T(8,128)(2,1)} collective-permute-done((bf16[384,1536]{1,0:T(8,128)(2,1)}, bf16[384,1536]{1,0:T(8,128)(2,1)}, u32[]{:S(2)}, u32[]{:S(2)}) %collective-permute-start.13) | collective-permute-done | bytes 1179680 | tf_op jit(solution)/shard_map/ppermute | solution.py:232
  139.7 3.0 collective-permute-done.14
  145.6 4.7 collective-permute-start.18
  159.6 7.7 %collective-permute-done.17 = bf16[192,1536]{1,0:T(8,128)(2,1)} collective-permute-done((bf16[192,1536]{1,0:T(8,128)(2,1)}, bf16[192,1536]{1,0:T(8,128)(2,1)}, u32[]{:S(2)}, u32[]{:S(2)}) %collective-permute-start.17) | collective-permute-done | bytes 589856 | tf_op jit(solution)/shard_map/ppermute | solution.py:192
  168.3 20.3 %collective-permute-done.18 = bf16[256,1536]{1,0:T(8,128)(2,1)} collective-permute-done((bf16[256,1536]{1,0:T(8,128)(2,1)}, bf16[256,1536]{1,0:T(8,128)(2,1)}, u32[]{:S(2)}, u32[]{:S(2)}) %collective-permute-start.18) | collective-permute-done | bytes 786464 | tf_op jit(solution)/shard_map/ppermute | solution.py:192
  192.8 3.1 collective-permute-start.20
  203.6 7.8 %multiply_convert_fusion = (bf16[1024,1536]{1,0:T(8,128)(2,1)S(1)}, f32[1024,1536]{1,0:T(8,128)}) fusion(f32[1536]{0:T(1024)S(1)} %fusion.27, bf16[1024,1536]{1,0:T(8,128)(2,1)S(1)} %constant_dynamic-update-slice_fusion.2, bf16[1536,1536]{1,0:T(8,128)(2,1)S(1)} %constant_dynamic-update-slice_fusion.11), kind=kOutput, calls=%fused_computation.13 | convolution fusion | flops 4847566848 | bytes 17307648 | tf_op jit(solution)/shard_map/dot_general | solution.py:52
  215.9 3.0 collective-permute-done.21
  220.8 6.9 %convolution_convert_fusion.2 = bf16[1536,1536]{1,0:T(8,128)(2,1)} fusion(bf16[1024,1536]{1,0:T(8,128)(2,1)S(1)} %get-tuple-element.170, bf16[1024,1536]{1,0:T(8,128)(2,1)S(1)} %constant_dynamic-update-slice_fusion.6), kind=kOutput, calls=%fused_computation.4 | convolution fusion | flops 4834197504 | bytes 11010048 | tf_op jit(solution)/shard_map/dot_general | solution.py:48
  228.0 11.8 %fusion.7 = bf16[1024,1536]{1,0:T(8,128)(2,1)S(1)} fusion(f32[1024,1536]{1,0:T(8,128)} %get-tuple-element.264, f32[1536]{0:T(1024)S(1)} %fusion.27, bf16[1024,1536]{1,0:T(8,128)(2,1)} %copy-done.32, bf16[1536,1536]{1,0:T(8,128)(2,1)} %all-gather.8.cloned.1.call-done), kind=kOutput, calls=%fused_computation.12 | convolution fusion | flops 4864868352 | bytes 17307648 | tf_op jit(solution)/shard_map/dot_general | solution.py:44
  239.8 7.0 %fusion.42 = f32[1024,1536]{1,0:T(8,128)S(1)} fusion(bf16[1024,1536]{1,0:T(8,128)(2,1)S(1)} %fusion.7, bf16[1536,1536]{1,0:T(8,128)(2,1)} %copy-done.15), kind=kOutput, calls=%fused_computation.152 | convolution fusion | flops 4831838208 | bytes 14155776 | tf_op jit(solution)/shard_map/dot_general | solution.py:44
  247.5 3.0 collective-permute-done.22
  253.6 5.0 %fusion.43 = f32[1024,1536]{1,0:T(8,128)S(1)} fusion(bf16[1024,1536]{1,0:T(8,128)(2,1)S(1)} %copy-done.45, bf16[1536,1536]{1,0:T(8,128)(2,1)S(1)} %copy-done.40), kind=kOutput, calls=%fused_computation.153 | convolution fusion | flops 4831838208 | bytes 14155776 | tf_op jit(solution)/shard_map/dot_general | solution.py:52
  258.6 2.6 copy-done.18
  263.7 7.0 %convolution_convert_fusion.1 = bf16[1536,1536]{1,0:T(8,128)(2,1)} fusion(bf16[1024,1536]{1,0:T(8,128)(2,1)S(1)} %copy-done.27, bf16[1024,1536]{1,0:T(8,128)(2,1)S(1)} %fusion.7), kind=kOutput, calls=%fused_computation.3 | convolution fusion | flops 4834197504 | bytes 11010048 | tf_op jit(solution)/shard_map/dot_general | solution.py:48
  270.8 17.4 %collective-permute-done.23 = bf16[512,1536]{1,0:T(8,128)(2,1)} collective-permute-done((bf16[512,1536]{1,0:T(8,128)(2,1)}, bf16[512,1536]{1,0:T(8,128)(2,1)}, u32[]{:S(2)}, u32[]{:S(2)}) %collective-permute-start.23) | collective-permute-done | bytes 1572896 | tf_op jit(solution)/shard_map/ppermute | solution.py:192
  290.0 3.1 multiply_reduce_fusion.2
  294.7 3.1 fusion.35
  299.0 4.2 collective-permute-start.26
  310.5 2.8 fusion.21
  314.7 4.6 convolution_convert_fusion.4.grad_ref
  319.3 13.0 %attend_back.1 = bf16[1024,1152]{1,0:T(8,128)(2,1)} custom-call(s32[1]{0:T(128)} %bitcast.4.index_ref, bf16[1024,384]{1,0:T(8,128)(2,1)} %convolution_convert_fusion.4.grad_ref, bf16[3,1024,128]{2,1,0:T(8,128)(2,1)} %get-tuple-element.178.q_ref, bf16[3,1024,128]{2,1,0:T(8,128)(2,1)} %get-tuple-element.179.k_ref, ...), custom_call_target="tpu_custom_call" | custom-call | flops 6000000000 | bytes 12000000 | tf_op jit(solution)/shard_map/attend_back/pallas_call | solution.py:167
  332.3 7.4 %convolution_convert_fusion = bf16[1536,1152]{1,0:T(8,128)(2,1)S(1)} fusion(bf16[1024,1536]{1,0:T(8,128)(2,1)} %constant_dynamic-update-slice_fusion, bf16[1024,1152]{1,0:T(8,128)(2,1)} %attend_back.1), kind=kOutput, calls=%fused_computation.2 | convolution fusion | flops 3625648128 | bytes 9043968 | tf_op jit(solution)/shard_map/dot_general | solution.py:48
  345.2 4.2 fusion.44
  350.8 2.9 copy-done.3
  353.6 3.2 fusion.19
  362.2 2.7 fusion.20
  364.9 4.8 collective-permute-start.35
  374.3 7.8 %collective-permute-start.34 = (bf16[384,1536]{1,0:T(8,128)(2,1)}, bf16[384,1536]{1,0:T(8,128)(2,1)}, u32[]{:S(2)}, u32[]{:S(2)}) collective-permute-start(bf16[384,1536]{1,0:T(8,128)(2,1)} %reduce-scatter.6.cloned.1.call-done), channel_id=1, source_target_pairs={{2,0},{3,1},{4,6},{5,7},{10,8},{11,9},{12,14},{13,15},{18,16},{19,... | collective-permute-start | bytes 3538952 | tf_op jit(solution)/shard_map/ppermute | solution.py:232
  394.9 9.3 %collective-permute-done.33 = bf16[384,1152]{1,0:T(8,128)(2,1)} collective-permute-done((bf16[384,1152]{1,0:T(8,128)(2,1)}, bf16[384,1152]{1,0:T(8,128)(2,1)}, u32[]{:S(2)}, u32[]{:S(2)}) %collective-permute-start.33) | collective-permute-done | bytes 884768 | tf_op jit(solution)/shard_map/ppermute | solution.py:192
  405.9 2.8 multiply_reduce_fusion.3
  409.3 14.7 %collective-permute-start.36 = (f32[4,1536]{1,0:T(4,128)S(1)}, f32[4,1536]{1,0:T(4,128)S(1)}, u32[]{:S(2)}, u32[]{:S(2)}) collective-permute-start(f32[4,1536]{1,0:T(4,128)S(1)} %pad_maximum_fusion.7), channel_id=1, source_target_pairs={{0,4},{1,5},{2,6},{3,7},{4,0},{5,1},{6,2},{7,3},{8,12},{9,13},{10,... | collective-permute-start | bytes 73736 | tf_op jit(solution)/shard_map/ppermute | solution.py:192
  430.4 5.0 %collective-permute-done.37 = f32[4,1536]{1,0:T(4,128)S(1)} collective-permute-done((f32[4,1536]{1,0:T(4,128)S(1)}, f32[4,1536]{1,0:T(4,128)S(1)}, u32[]{:S(2)}, u32[]{:S(2)}) %collective-permute-start.37) | collective-permute-done | bytes 24608 | tf_op jit(solution)/shard_map/ppermute | solution.py:192
  435.4 8.6 %collective-permute-done.38 = bf16[256,1536]{1,0:T(8,128)(2,1)S(1)} collective-permute-done((bf16[256,1536]{1,0:T(8,128)(2,1)S(1)}, bf16[256,1536]{1,0:T(8,128)(2,1)S(1)}, u32[]{:S(2)}, u32[]{:S(2)}) %collective-permute-start.38) | collective-permute-done | bytes 786464 | tf_op jit(solution)/shard_map/ppermute | solution.py:192
  444.0 3.6 collective-permute-done.41
  448.3 3.2 collective-permute-start.39
  455.8 20.2 %collective-permute-done.39 = bf16[192,1536]{1,0:T(8,128)(2,1)S(1)} collective-permute-done((bf16[192,1536]{1,0:T(8,128)(2,1)S(1)}, bf16[192,1536]{1,0:T(8,128)(2,1)S(1)}, u32[]{:S(2)}, u32[]{:S(2)}) %collective-permute-start.39) | collective-permute-done | bytes 589856 | tf_op jit(solution)/shard_map/ppermute | solution.py:192
  (271 shorter events, 131.7 us)
Async XLA Ops:
  7.2 77.0 %all-gather.4.cloned.1.call-start = ((), (), s32[]{:S(2)}) async-start(), calls=%async_computation.3 | async-start | bytes 4423680 | tf_op jit(solution)/shard_map/all_gather | solution.py:247
  9.9 22.5 %collective-permute-start.2 = (bf16[192,1152]{1,0:T(8,128)(2,1)S(1)}, bf16[192,1152]{1,0:T(8,128)(2,1)S(1)}, u32[]{:S(2)}, u32[]{:S(2)}) collective-permute-start(bf16[192,1152]{1,0:T(8,128)(2,1)S(1)} %bitcast.41), channel_id=1, source_target_pairs={{0,2},{1,3},{2,6},{3,7},{4,0},{5,1},{6,4},{7,5},{8,10},{9,11},{10,... | collective-permute-start | bytes 1327112 | tf_op jit(solution)/shard_map/ppermute | solution.py:192
  10.4 23.2 %collective-permute-start.1 = (bf16[192,1152]{1,0:T(8,128)(2,1)S(1)}, bf16[192,1152]{1,0:T(8,128)(2,1)S(1)}, u32[]{:S(2)}, u32[]{:S(2)}) collective-permute-start(bf16[192,1152]{1,0:T(8,128)(2,1)S(1)} %bitcast.42), channel_id=1, source_target_pairs={{0,0},{1,1},{2,4},{3,5},{4,2},{5,3},{6,6},{7,7},{8,8},{9,9},{10,12... | collective-permute-start | bytes 1327112 | tf_op jit(solution)/shard_map/ppermute | solution.py:192
  34.8 88.2 %all-gather.6.cloned.1.call-start = ((), (), s32[]{:S(2)}) async-start(), calls=%async_computation.4 | async-start | bytes 1474560 | tf_op jit(solution)/shard_map/all_gather | solution.py:247
  35.3 5.3 %collective-permute-start.4 = (bf16[192,1536]{1,0:T(8,128)(2,1)S(1)}, bf16[192,1536]{1,0:T(8,128)(2,1)S(1)}, u32[]{:S(2)}, u32[]{:S(2)}) collective-permute-start(bf16[192,1536]{1,0:T(8,128)(2,1)S(1)} %copy-done.29), channel_id=1, source_target_pairs={{0,4},{1,5},{2,6},{3,7},{4,0},{5,1},{6,2},{7,3},{8,12},{9,13},{10,... | collective-permute-start | bytes 1769480 | tf_op jit(solution)/shard_map/ppermute | solution.py:192
  35.4 22.7 %collective-permute-start.3 = (bf16[256,1536]{1,0:T(8,128)(2,1)S(1)}, bf16[256,1536]{1,0:T(8,128)(2,1)S(1)}, u32[]{:S(2)}, u32[]{:S(2)}) collective-permute-start(bf16[256,1536]{1,0:T(8,128)(2,1)S(1)} %copy-done.42), channel_id=1, source_target_pairs={{0,0},{1,1},{2,4},{3,5},{4,2},{5,3},{6,6},{7,7},{8,8},{9,9},{10,12... | collective-permute-start | bytes 2359304 | tf_op jit(solution)/shard_map/ppermute | solution.py:192
  58.1 14.4 %collective-permute-start.5 = (bf16[256,1536]{1,0:T(8,128)(2,1)S(1)}, bf16[256,1536]{1,0:T(8,128)(2,1)S(1)}, u32[]{:S(2)}, u32[]{:S(2)}) collective-permute-start(bf16[256,1536]{1,0:T(8,128)(2,1)S(1)} %collective-permute-done.3), channel_id=1, source_target_pairs={{0,1},{1,0},{2,3},{3,2},{4,5},{5,4},{6,7},{7,6},{8,9},{9,8},{10,11... | collective-permute-start | bytes 2359304 | tf_op jit(solution)/shard_map/ppermute | solution.py:192
  58.2 5.3 %collective-permute-start.7 = (bf16[48,1536]{1,0:T(8,128)(2,1)S(1)}, bf16[48,1536]{1,0:T(8,128)(2,1)S(1)}, u32[]{:S(2)}, u32[]{:S(2)}) collective-permute-start(bf16[48,1536]{1,0:T(8,128)(2,1)S(1)} %copy-done.43), channel_id=1, source_target_pairs={{0,2},{1,3},{2,6},{3,7},{4,0},{5,1},{6,4},{7,5},{8,10},{9,11},{10,... | collective-permute-start | bytes 442376 | tf_op jit(solution)/shard_map/ppermute | solution.py:192
  58.2 12.1 %collective-permute-start.6 = (bf16[48,1536]{1,0:T(8,128)(2,1)S(1)}, bf16[48,1536]{1,0:T(8,128)(2,1)S(1)}, u32[]{:S(2)}, u32[]{:S(2)}) collective-permute-start(bf16[48,1536]{1,0:T(8,128)(2,1)S(1)} %copy-done.43), channel_id=1, source_target_pairs={{0,0},{1,1},{2,4},{3,5},{4,2},{5,3},{6,6},{7,7},{8,8},{9,9},{10,12... | collective-permute-start | bytes 442376 | tf_op jit(solution)/shard_map/ppermute | solution.py:192
  75.8 5.8 %collective-permute-start.8 = (bf16[512,1536]{1,0:T(8,128)(2,1)S(1)}, bf16[512,1536]{1,0:T(8,128)(2,1)}, u32[]{:S(2)}, u32[]{:S(2)}) collective-permute-start(bf16[512,1536]{1,0:T(8,128)(2,1)S(1)} %get-tuple-element.122), channel_id=1, source_target_pairs={{0,4},{1,5},{2,6},{3,7},{4,0},{5,1},{6,2},{7,3},{8,12},{9,13},{10,... | collective-permute-start | bytes 4718600 | tf_op jit(solution)/shard_map/ppermute | solution.py:192
  75.8 152.2 %all-gather.8.cloned.1.call-start = ((), (), s32[]{:S(2)}) async-start(), calls=%async_computation.5 | async-start | bytes 5898240 | tf_op jit(solution)/shard_map/all_gather | solution.py:247
  75.8 27.2 %collective-permute-start.10 = (bf16[192,1536]{1,0:T(8,128)(2,1)}, bf16[192,1536]{1,0:T(8,128)(2,1)}, u32[]{:S(2)}, u32[]{:S(2)}) collective-permute-start(bf16[192,1536]{1,0:T(8,128)(2,1)} %param.22), channel_id=1, source_target_pairs={{0,2},{1,3},{2,6},{3,7},{4,0},{5,1},{6,4},{7,5},{8,10},{9,11},{10,... | collective-permute-start | bytes 1769480 | tf_op jit(solution)/shard_map/ppermute | solution.py:192
  76.4 28.4 %collective-permute-start.9 = (bf16[192,1536]{1,0:T(8,128)(2,1)}, bf16[192,1536]{1,0:T(8,128)(2,1)}, u32[]{:S(2)}, u32[]{:S(2)}) collective-permute-start(bf16[192,1536]{1,0:T(8,128)(2,1)} %param.22), channel_id=1, source_target_pairs={{0,0},{1,1},{2,4},{3,5},{4,2},{5,3},{6,6},{7,7},{8,8},{9,9},{10,12... | collective-permute-start | bytes 1769480 | tf_op jit(solution)/shard_map/ppermute | solution.py:192
  106.9 30.8 %collective-permute-start.13 = (bf16[384,1536]{1,0:T(8,128)(2,1)}, bf16[384,1536]{1,0:T(8,128)(2,1)}, u32[]{:S(2)}, u32[]{:S(2)}) collective-permute-start(bf16[384,1536]{1,0:T(8,128)(2,1)} %maximum_select_fusion), channel_id=1, source_target_pairs={{0,2},{1,3},{6,4},{7,5},{8,10},{9,11},{14,12},{15,13},{16,18},{17,... | collective-permute-start | bytes 3538952 | tf_op jit(solution)/shard_map/ppermute | solution.py:232
  108.7 30.0 %collective-permute-start.12 = (bf16[384,1536]{1,0:T(8,128)(2,1)S(1)}, bf16[384,1536]{1,0:T(8,128)(2,1)}, u32[]{:S(2)}, u32[]{:S(2)}) collective-permute-start(bf16[384,1536]{1,0:T(8,128)(2,1)S(1)} %maximum_select_fusion.1), channel_id=1, source_target_pairs={{0,16},{1,17},{2,18},{3,19},{4,20},{5,21},{6,22},{7,23},{8,24},{9,... | collective-permute-start | bytes 3538952 | tf_op jit(solution)/shard_map/ppermute | solution.py:192
  110.0 28.6 %collective-permute-start.11 = (bf16[384,1536]{1,0:T(8,128)(2,1)S(1)}, bf16[384,1536]{1,0:T(8,128)(2,1)}, u32[]{:S(2)}, u32[]{:S(2)}) collective-permute-start(bf16[384,1536]{1,0:T(8,128)(2,1)S(1)} %maximum_select_fusion.1), channel_id=1, source_target_pairs={{0,8},{1,9},{2,10},{3,11},{4,12},{5,13},{6,14},{7,15},{8,0},{9,1},... | collective-permute-start | bytes 3538952 | tf_op jit(solution)/shard_map/ppermute | solution.py:192
  138.6 4.2 collective-permute-start.14
  144.4 44.2 %collective-permute-start.15 = (bf16[512,1536]{1,0:T(8,128)(2,1)}, bf16[512,1536]{1,0:T(8,128)(2,1)S(1)}, u32[]{:S(2)}, u32[]{:S(2)}) collective-permute-start(bf16[512,1536]{1,0:T(8,128)(2,1)} %fusion.12), channel_id=1, source_target_pairs={{0,1},{1,0},{2,3},{3,2},{4,5},{5,4},{6,7},{7,6},{8,9},{9,8},{10,11... | collective-permute-start | bytes 4718600 | tf_op jit(solution)/shard_map/ppermute | solution.py:192
  145.6 43.0 %collective-permute-start.18 = (bf16[256,1536]{1,0:T(8,128)(2,1)}, bf16[256,1536]{1,0:T(8,128)(2,1)}, u32[]{:S(2)}, u32[]{:S(2)}) collective-permute-start(bf16[256,1536]{1,0:T(8,128)(2,1)} %param.13), channel_id=1, source_target_pairs={{0,0},{1,1},{2,4},{3,5},{4,2},{5,3},{6,6},{7,7},{8,8},{9,9},{10,12... | collective-permute-start | bytes 2359304 | tf_op jit(solution)/shard_map/ppermute | solution.py:192
  155.5 11.8 %collective-permute-start.17 = (bf16[192,1536]{1,0:T(8,128)(2,1)}, bf16[192,1536]{1,0:T(8,128)(2,1)}, u32[]{:S(2)}, u32[]{:S(2)}) collective-permute-start(bf16[192,1536]{1,0:T(8,128)(2,1)} %slice.131), channel_id=1, source_target_pairs={{0,8},{1,9},{2,10},{3,11},{4,12},{5,13},{6,14},{7,15},{8,0},{9,1},... | collective-permute-start | bytes 1769480 | tf_op jit(solution)/shard_map/ppermute | solution.py:192
  156.7 11.6 %collective-permute-start.16 = (bf16[192,1536]{1,0:T(8,128)(2,1)}, bf16[192,1536]{1,0:T(8,128)(2,1)}, u32[]{:S(2)}, u32[]{:S(2)}) collective-permute-start(bf16[192,1536]{1,0:T(8,128)(2,1)} %slice.130), channel_id=1, source_target_pairs={{0,16},{1,17},{2,18},{3,19},{4,20},{5,21},{6,22},{7,23},{8,24},{9,... | collective-permute-start | bytes 1769480 | tf_op jit(solution)/shard_map/ppermute | solution.py:192
  159.4 138.5 %reduce-scatter.4.cloned.1.call-start = ((), (), s32[]{:S(2)}) async-start(), calls=%async_computation.6 | async-start | bytes 5898240 | tf_op jit(solution)/shard_map/reduce_scatter | solution.py:279
  192.8 21.1 %collective-permute-start.20 = (bf16[256,1536]{1,0:T(8,128)(2,1)}, bf16[256,1536]{1,0:T(8,128)(2,1)S(1)}, u32[]{:S(2)}, u32[]{:S(2)}) collective-permute-start(bf16[256,1536]{1,0:T(8,128)(2,1)} %collective-permute-done.18), channel_id=1, source_target_pairs={{0,1},{1,0},{2,3},{3,2},{4,5},{5,4},{6,7},{7,6},{8,9},{9,8},{10,11... | collective-permute-start | bytes 2359304 | tf_op jit(solution)/shard_map/ppermute | solution.py:192
  196.0 7.4 %collective-permute-start.19 = (bf16[512,1536]{1,0:T(8,128)(2,1)S(1)}, bf16[512,1536]{1,0:T(8,128)(2,1)S(1)}, u32[]{:S(2)}, u32[]{:S(2)}) collective-permute-start(bf16[512,1536]{1,0:T(8,128)(2,1)S(1)} %get-tuple-element.160), channel_id=1, source_target_pairs={{0,4},{1,5},{2,6},{3,7},{4,0},{5,1},{6,2},{7,3},{8,12},{9,13},{10,... | collective-permute-start | bytes 4718600 | tf_op jit(solution)/shard_map/ppermute | solution.py:192
  215.3 3.7 collective-permute-start.21
  227.7 137.2 %reduce-scatter.6.cloned.1.call-start = ((), (), s32[]{:S(2)}) async-start(), calls=%async_computation.7 | async-start | bytes 5898240 | tf_op jit(solution)/shard_map/reduce_scatter | solution.py:279
  252.3 35.9 %collective-permute-start.23 = (bf16[512,1536]{1,0:T(8,128)(2,1)}, bf16[512,1536]{1,0:T(8,128)(2,1)}, u32[]{:S(2)}, u32[]{:S(2)}) collective-permute-start(bf16[512,1536]{1,0:T(8,128)(2,1)} %fusion.13), channel_id=1, source_target_pairs={{0,1},{1,0},{2,3},{3,2},{4,5},{5,4},{6,7},{7,6},{8,9},{9,8},{10,11... | collective-permute-start | bytes 4718600 | tf_op jit(solution)/shard_map/ppermute | solution.py:192
  270.7 118.7 %reduce-scatter.8.cloned.1.call-start = ((), (), s32[]{:S(2)}) async-start(), calls=%async_computation.8 | async-start | bytes 1474560 | tf_op jit(solution)/shard_map/reduce_scatter | solution.py:279
  297.8 6.9 %collective-permute-start.24 = (bf16[512,1536]{1,0:T(8,128)(2,1)}, bf16[512,1536]{1,0:T(8,128)(2,1)}, u32[]{:S(2)}, u32[]{:S(2)}) collective-permute-start(bf16[512,1536]{1,0:T(8,128)(2,1)} %get-tuple-element.174), channel_id=1, source_target_pairs={{0,4},{1,5},{2,6},{3,7},{4,0},{5,1},{6,2},{7,3},{8,12},{9,13},{10,... | collective-permute-start | bytes 4718600 | tf_op jit(solution)/shard_map/ppermute | solution.py:192
  299.0 11.5 %collective-permute-start.25 = (bf16[512,1536]{1,0:T(8,128)(2,1)}, bf16[512,1536]{1,0:T(8,128)(2,1)}, u32[]{:S(2)}, u32[]{:S(2)}) collective-permute-start(bf16[512,1536]{1,0:T(8,128)(2,1)} %slice.248), channel_id=1, source_target_pairs={{0,4},{1,5},{2,6},{3,7},{4,0},{5,1},{6,2},{7,3},{8,12},{9,13},{10,... | collective-permute-start | bytes 4718600 | tf_op jit(solution)/shard_map/ppermute | solution.py:192
  299.0 43.5 %collective-permute-start.26 = (bf16[384,1536]{1,0:T(8,128)(2,1)}, bf16[384,1536]{1,0:T(8,128)(2,1)}, u32[]{:S(2)}, u32[]{:S(2)}) collective-permute-start(bf16[384,1536]{1,0:T(8,128)(2,1)} %reduce-scatter.4.cloned.1.call-done), channel_id=1, source_target_pairs={{2,0},{3,1},{4,6},{5,7},{10,8},{11,9},{12,14},{13,15},{18,16},{19,... | collective-permute-start | bytes 3538952 | tf_op jit(solution)/shard_map/ppermute | solution.py:232
  313.3 30.5 %collective-permute-start.27 = (bf16[256,1536]{1,0:T(8,128)(2,1)}, bf16[256,1536]{1,0:T(8,128)(2,1)}, u32[]{:S(2)}, u32[]{:S(2)}) collective-permute-start(bf16[256,1536]{1,0:T(8,128)(2,1)} %fusion.21), channel_id=1, source_target_pairs={{0,1},{1,0},{2,3},{3,2},{4,5},{5,4},{6,7},{7,6},{8,9},{9,8},{10,11... | collective-permute-start | bytes 2359304 | tf_op jit(solution)/shard_map/ppermute | solution.py:192
  343.8 13.0 %collective-permute-start.28 = (bf16[192,1152]{1,0:T(8,128)(2,1)S(1)}, bf16[192,1152]{1,0:T(8,128)(2,1)S(1)}, u32[]{:S(2)}, u32[]{:S(2)}) collective-permute-start(bf16[192,1152]{1,0:T(8,128)(2,1)S(1)} %get-tuple-element.184), channel_id=1, source_target_pairs={{0,8},{1,9},{2,10},{3,11},{4,12},{5,13},{6,14},{7,15},{8,0},{9,1},... | collective-permute-start | bytes 1327112 | tf_op jit(solution)/shard_map/ppermute | solution.py:192
  345.1 12.4 %collective-permute-start.29 = (bf16[192,1152]{1,0:T(8,128)(2,1)S(1)}, bf16[192,1152]{1,0:T(8,128)(2,1)S(1)}, u32[]{:S(2)}, u32[]{:S(2)}) collective-permute-start(bf16[192,1152]{1,0:T(8,128)(2,1)S(1)} %get-tuple-element.185), channel_id=1, source_target_pairs={{0,16},{1,17},{2,18},{3,19},{4,20},{5,21},{6,22},{7,23},{8,24},{9,... | collective-permute-start | bytes 1327112 | tf_op jit(solution)/shard_map/ppermute | solution.py:192
  358.4 3.8 collective-permute-start.30
  364.8 28.3 %collective-permute-start.31 = (bf16[256,1536]{1,0:T(8,128)(2,1)}, bf16[256,1536]{1,0:T(8,128)(2,1)}, u32[]{:S(2)}, u32[]{:S(2)}) collective-permute-start(bf16[256,1536]{1,0:T(8,128)(2,1)} %fusion.20), channel_id=1, source_target_pairs={{0,1},{1,0},{2,3},{3,2},{4,5},{5,4},{6,7},{7,6},{8,9},{9,8},{10,11... | collective-permute-start | bytes 2359304 | tf_op jit(solution)/shard_map/ppermute | solution.py:192
  364.9 29.4 %collective-permute-start.35 = (bf16[256,1536]{1,0:T(8,128)(2,1)}, bf16[256,1536]{1,0:T(8,128)(2,1)}, u32[]{:S(2)}, u32[]{:S(2)}) collective-permute-start(bf16[256,1536]{1,0:T(8,128)(2,1)} %fusion.19), channel_id=1, source_target_pairs={{0,0},{1,1},{2,4},{3,5},{4,2},{5,3},{6,6},{7,7},{8,8},{9,9},{10,12... | collective-permute-start | bytes 2359304 | tf_op jit(solution)/shard_map/ppermute | solution.py:192
  373.4 21.5 %collective-permute-start.32 = (bf16[384,1152]{1,0:T(8,128)(2,1)}, bf16[384,1152]{1,0:T(8,128)(2,1)}, u32[]{:S(2)}, u32[]{:S(2)}) collective-permute-start(bf16[384,1152]{1,0:T(8,128)(2,1)} %pad_maximum_fusion.2), channel_id=1, source_target_pairs={{0,8},{1,9},{2,10},{3,11},{4,12},{5,13},{6,14},{7,15},{8,0},{9,1},... | collective-permute-start | bytes 2654216 | tf_op jit(solution)/shard_map/ppermute | solution.py:192
  374.3 29.8 %collective-permute-start.34 = (bf16[384,1536]{1,0:T(8,128)(2,1)}, bf16[384,1536]{1,0:T(8,128)(2,1)}, u32[]{:S(2)}, u32[]{:S(2)}) collective-permute-start(bf16[384,1536]{1,0:T(8,128)(2,1)} %reduce-scatter.6.cloned.1.call-done), channel_id=1, source_target_pairs={{2,0},{3,1},{4,6},{5,7},{10,8},{11,9},{12,14},{13,15},{18,16},{19,... | collective-permute-start | bytes 3538952 | tf_op jit(solution)/shard_map/ppermute | solution.py:232
  383.1 21.0 %collective-permute-start.33 = (bf16[384,1152]{1,0:T(8,128)(2,1)}, bf16[384,1152]{1,0:T(8,128)(2,1)}, u32[]{:S(2)}, u32[]{:S(2)}) collective-permute-start(bf16[384,1152]{1,0:T(8,128)(2,1)} %pad_maximum_fusion.3), channel_id=1, source_target_pairs={{0,16},{1,17},{2,18},{3,19},{4,20},{5,21},{6,22},{7,23},{8,24},{9,... | collective-permute-start | bytes 2654216 | tf_op jit(solution)/shard_map/ppermute | solution.py:192
  393.1 59.6 %collective-permute-start.44 = (f32[192,1536]{1,0:T(8,128)}, f32[192,1536]{1,0:T(8,128)S(1)}, u32[]{:S(2)}, u32[]{:S(2)}) collective-permute-start(f32[192,1536]{1,0:T(8,128)} %slice_select_fusion.1), channel_id=1, source_target_pairs={{0,4},{1,5},{2,6},{3,7},{4,0},{5,1},{6,2},{7,3},{8,12},{9,13},{10,... | collective-permute-start | bytes 3538952 | tf_op jit(solution)/shard_map/ppermute | solution.py:192
  409.3 20.6 %collective-permute-start.36 = (f32[4,1536]{1,0:T(4,128)S(1)}, f32[4,1536]{1,0:T(4,128)S(1)}, u32[]{:S(2)}, u32[]{:S(2)}) collective-permute-start(f32[4,1536]{1,0:T(4,128)S(1)} %pad_maximum_fusion.7), channel_id=1, source_target_pairs={{0,4},{1,5},{2,6},{3,7},{4,0},{5,1},{6,2},{7,3},{8,12},{9,13},{10,... | collective-permute-start | bytes 73736 | tf_op jit(solution)/shard_map/ppermute | solution.py:192
  424.0 20.0 %collective-permute-start.38 = (bf16[256,1536]{1,0:T(8,128)(2,1)S(1)}, bf16[256,1536]{1,0:T(8,128)(2,1)S(1)}, u32[]{:S(2)}, u32[]{:S(2)}) collective-permute-start(bf16[256,1536]{1,0:T(8,128)(2,1)S(1)} %fusion.16), channel_id=1, source_target_pairs={{0,0},{1,1},{2,4},{3,5},{4,2},{5,3},{6,6},{7,7},{8,8},{9,9},{10,12... | collective-permute-start | bytes 2359304 | tf_op jit(solution)/shard_map/ppermute | solution.py:192
  428.0 26.6 %collective-permute-start.45 = (f32[192,1536]{1,0:T(8,128)S(1)}, f32[192,1536]{1,0:T(8,128)S(1)}, u32[]{:S(2)}, u32[]{:S(2)}) collective-permute-start(f32[192,1536]{1,0:T(8,128)S(1)} %slice_select_fusion), channel_id=1, source_target_pairs={{0,4},{1,5},{2,6},{3,7},{4,0},{5,1},{6,2},{7,3},{8,12},{9,13},{10,... | collective-permute-start | bytes 3538952 | tf_op jit(solution)/shard_map/ppermute | solution.py:192
  429.9 5.5 %collective-permute-start.37 = (f32[4,1536]{1,0:T(4,128)S(1)}, f32[4,1536]{1,0:T(4,128)S(1)}, u32[]{:S(2)}, u32[]{:S(2)}) collective-permute-start(f32[4,1536]{1,0:T(4,128)S(1)} %add.263), channel_id=1, source_target_pairs={{0,1},{1,0},{2,3},{3,2},{4,5},{5,4},{6,7},{7,6},{8,9},{9,8},{10,11... | collective-permute-start | bytes 73736 | tf_op jit(solution)/shard_map/ppermute | solution.py:192
  447.6 3.9 collective-permute-start.42
  448.2 7.6 %collective-permute-start.40 = (bf16[192,1536]{1,0:T(8,128)(2,1)S(1)}, bf16[192,1536]{1,0:T(8,128)(2,1)S(1)}, u32[]{:S(2)}, u32[]{:S(2)}) collective-permute-start(bf16[192,1536]{1,0:T(8,128)(2,1)S(1)} %get-tuple-element.254), channel_id=1, source_target_pairs={{0,4},{1,5},{2,0},{3,1},{4,6},{5,7},{6,2},{7,3},{8,12},{9,13},{10,... | collective-permute-start | bytes 1769480 | tf_op jit(solution)/shard_map/ppermute | solution.py:192
  448.3 27.8 %collective-permute-start.39 = (bf16[192,1536]{1,0:T(8,128)(2,1)S(1)}, bf16[192,1536]{1,0:T(8,128)(2,1)S(1)}, u32[]{:S(2)}, u32[]{:S(2)}) collective-permute-start(bf16[192,1536]{1,0:T(8,128)(2,1)S(1)} %get-tuple-element.255), channel_id=1, source_target_pairs={{0,0},{1,1},{2,4},{3,5},{4,2},{5,3},{6,6},{7,7},{8,8},{9,9},{10,12... | collective-permute-start | bytes 1769480 | tf_op jit(solution)/shard_map/ppermute | solution.py:192
  (52 other events, 775.9 us)
Sparse Core Ops, SparseCore 0:
  34.9 48.9 all-gather.3
  86.3 29.3 all-gather.5
  159.5 58.5 all-gather.7
  227.8 55.3 reduce-scatter.3
  286.1 57.0 reduce-scatter.5
  358.9 30.4 reduce-scatter.7

commit v5 on v4

--- a/solution.py
+++ b/solution.py
@@ -477,9 +477,10 @@
 
     got_qkv = layout.scatter_near(grad_qkv_part, near_qkv)
     one_part = dot_nt(projected_grad, wide_qkv)
-    output = resid_one[:rows] + out_part[:rows] + out_got[:rows].astype(F32) + out_other.astype(F32)
-    one_send, got_qkv, output = hold(one_part[2 * rows :].astype(BF16), got_qkv, output.astype(BF16))
-    (one_got,) = hold(layout.core(one_send))
+    one_send, got_qkv = hold(one_part[2 * rows :].astype(BF16), got_qkv)
+    one_got = layout.core(one_send)
+    output = resid_one[:rows] + out_part[:rows] + out_got[:rows].astype(F32) + after(out_other, one_send).astype(F32)
+    one_got, output = hold(one_got, output.astype(BF16))
     one_send = (one_part[rows : 2 * rows] + one_got[rows:].astype(F32)).astype(BF16)
     one_send, got_qkv, output, near_two_grad, up_sum = hold(one_send, got_qkv, output, near_two_grad, grad_up_sum)
     one_other = layout.pair(one_send)

time: 498 us -> 496 us (level)
  waiting for transfers between devices: 180 us -> 187 us
  local copies, waits for them, and re-layouts: 54.5 us -> 48.4 us
  starting transfers between devices: 79.6 us -> 74.1 us
    unnamed x100 -> x90, local copies, waits for them, and re-layouts: 26.8 us -> 20.6 us
  transfers between devices with their start and end apart: 52 -> 52, of which waited for: 30 -> 31; matrix products, arithmetic and copies ran while one was open for 33% -> 34% of each run, Pallas kernels for 5% -> 5%
where the time goes in v5:
time: 496 us; the launch traced here: 487 us
  waiting for transfers between devices  187 us (38%)
  matrix products  79.7 us (16%)
  starting transfers between devices  74.1 us (15%)
  other arithmetic  57.6 us (12%)
  local copies, waits for them, and re-layouts  48.4 us (10%)
  Pallas kernels  23.8 us (5%)
  between operations  16.7 us (3%)
    ppermute x43, waiting for transfers between devices, permute(): return lax.ppermute(value, AXES, pairs)  172 us
    ppermute x43, starting transfers between devices, permute(): return lax.ppermute(value, AXES, pairs)  60.3 us
    dot_general x4, matrix products, dot_nn(): lax.dot_general(left, right, (((1,), (0,)), ((), ())), preferred_element_...  28.5 us
    dot_general x4, matrix products, dot_nt(): lax.dot_general(left, right, (((1,), (1,)), ((), ())), preferred_element_...  27.6 us
    dot_general x4, matrix products, dot_tn(): lax.dot_general(left, right, (((0,), (0,)), ((), ())), preferred_element_...  23.5 us
    unnamed x90, local copies, waits for them, and re-layouts  20.6 us
    ppermute x3, waiting for transfers between devices, flip(): return lax.ppermute(value, AXES, pairs)  14.1 us
    ppermute x3, starting transfers between devices, flip(): return lax.ppermute(value, AXES, pairs)  13.2 us
  transfers between devices with their start and end apart: 52, of which 31 were waited for; matrix products, arithmetic and copies ran while one was open for 34% of the time, Pallas kernels for 5%

profile of v5, /device:TPU:1, one launch (start us, length us, event | category | flops | bytes accessed | tf_op | source)
XLA Modules:
  0.0 486.9 jit_solution(11759523056544777498)
XLA Ops:
  10.4 5.6 %collective-permute-start.1 = (bf16[192,1152]{1,0:T(8,128)(2,1)S(1)}, bf16[192,1152]{1,0:T(8,128)(2,1)S(1)}, u32[]{:S(2)}, u32[]{:S(2)}) collective-permute-start(bf16[192,1152]{1,0:T(8,128)(2,1)S(1)} %bitcast.42), channel_id=1, source_target_pairs={{0,0},{1,1},{2,4},{3,5},{4,2},{5,3},{6,6},{7,7},{8,8},{9,9},{10,12... | collective-permute-start | bytes 1327112 | tf_op jit(solution)/shard_map/ppermute | solution.py:192
  16.0 16.3 %collective-permute-done.2 = bf16[192,1152]{1,0:T(8,128)(2,1)S(1)} collective-permute-done((bf16[192,1152]{1,0:T(8,128)(2,1)S(1)}, bf16[192,1152]{1,0:T(8,128)(2,1)S(1)}, u32[]{:S(2)}, u32[]{:S(2)}) %collective-permute-start.2) | collective-permute-done | bytes 442400 | tf_op jit(solution)/shard_map/ppermute | solution.py:192
  42.1 16.1 %collective-permute-done.3 = bf16[256,1536]{1,0:T(8,128)(2,1)S(1)} collective-permute-done((bf16[256,1536]{1,0:T(8,128)(2,1)S(1)}, bf16[256,1536]{1,0:T(8,128)(2,1)S(1)}, u32[]{:S(2)}, u32[]{:S(2)}) %collective-permute-start.3) | collective-permute-done | bytes 786464 | tf_op jit(solution)/shard_map/ppermute | solution.py:192
  58.2 3.4 collective-permute-start.6
  63.5 6.8 %collective-permute-done.6 = bf16[48,1536]{1,0:T(8,128)(2,1)S(1)} collective-permute-done((bf16[48,1536]{1,0:T(8,128)(2,1)S(1)}, bf16[48,1536]{1,0:T(8,128)(2,1)S(1)}, u32[]{:S(2)}, u32[]{:S(2)}) %collective-permute-start.6) | collective-permute-done | bytes 147488 | tf_op jit(solution)/shard_map/ppermute | solution.py:192
  76.4 3.9 collective-permute-start.9
  81.6 2.6 constant_dynamic-update-slice_fusion
  84.3 9.3 %fusion.40.proj_ref = f32[1024,1152]{1,0:T(8,128)} fusion(bf16[1024,1536]{1,0:T(8,128)(2,1)} %constant_dynamic-update-slice_fusion, bf16[1536,1152]{1,0:T(8,128)(2,1)} %all-gather.4.cloned.1.call-done), kind=kOutput, calls=%fused_computation.150 | convolution fusion | flops 3623878656 | bytes 11403264 | tf_op jit(solution)/shard_map/dot_general | solution.py:52
  93.6 9.3 %collective-permute-done.10 = bf16[192,1536]{1,0:T(8,128)(2,1)} collective-permute-done((bf16[192,1536]{1,0:T(8,128)(2,1)}, bf16[192,1536]{1,0:T(8,128)(2,1)}, u32[]{:S(2)}, u32[]{:S(2)}) %collective-permute-start.10) | collective-permute-done | bytes 589856 | tf_op jit(solution)/shard_map/ppermute | solution.py:192
  112.2 10.7 %attend.1 = (bf16[1024,384]{1,0:T(8,128)(2,1)}, bf16[3,1024,128]{2,1,0:T(8,128)(2,1)}, bf16[3,1024,128]{2,1,0:T(8,128)(2,1)}, bf16[3,1024,128]{2,1,0:T(8,128)(2,1)}, f32[3,1024,1]{2,1,0:T(8,128)}) custom-call(s32[1]{0:T(128)} %bitcast.4.index_ref, f32[1024,1152]{1,0:T(8,128)} %fusion.40.proj_ref, f32[1024,128]{1,0:T(8,128)} %get-tuple-element.132.cos_ref, ...), custom_call_target="tpu_custom_call" | custom-call | flops 3000000000 | bytes 12000000 | tf_op jit(solution)/shard_map/attend/pallas_call | solution.py:149
  123.0 3.3 fusion.41
  126.5 11.2 %collective-permute-done.13 = bf16[384,1536]{1,0:T(8,128)(2,1)} collective-permute-done((bf16[384,1536]{1,0:T(8,128)(2,1)}, bf16[384,1536]{1,0:T(8,128)(2,1)}, u32[]{:S(2)}, u32[]{:S(2)}) %collective-permute-start.13) | collective-permute-done | bytes 1179680 | tf_op jit(solution)/shard_map/ppermute | solution.py:232
  139.7 3.0 collective-permute-done.14
  145.7 4.7 collective-permute-start.18
  159.6 7.7 %collective-permute-done.17 = bf16[192,1536]{1,0:T(8,128)(2,1)} collective-permute-done((bf16[192,1536]{1,0:T(8,128)(2,1)}, bf16[192,1536]{1,0:T(8,128)(2,1)}, u32[]{:S(2)}, u32[]{:S(2)}) %collective-permute-start.17) | collective-permute-done | bytes 589856 | tf_op jit(solution)/shard_map/ppermute | solution.py:192
  168.3 20.3 %collective-permute-done.18 = bf16[256,1536]{1,0:T(8,128)(2,1)} collective-permute-done((bf16[256,1536]{1,0:T(8,128)(2,1)}, bf16[256,1536]{1,0:T(8,128)(2,1)}, u32[]{:S(2)}, u32[]{:S(2)}) %collective-permute-start.18) | collective-permute-done | bytes 786464 | tf_op jit(solution)/shard_map/ppermute | solution.py:192
  192.8 3.1 collective-permute-start.20
  203.6 7.9 %multiply_convert_fusion = (bf16[1024,1536]{1,0:T(8,128)(2,1)S(1)}, f32[1024,1536]{1,0:T(8,128)}) fusion(f32[1536]{0:T(1024)S(1)} %fusion.27, bf16[1024,1536]{1,0:T(8,128)(2,1)S(1)} %constant_dynamic-update-slice_fusion.2, bf16[1536,1536]{1,0:T(8,128)(2,1)S(1)} %constant_dynamic-update-slice_fusion.11), kind=kOutput, calls=%fused_computation.13 | convolution fusion | flops 4847566848 | bytes 17307648 | tf_op jit(solution)/shard_map/dot_general | solution.py:52
  215.9 3.0 collective-permute-done.21
  220.8 6.9 %convolution_convert_fusion.2 = bf16[1536,1536]{1,0:T(8,128)(2,1)} fusion(bf16[1024,1536]{1,0:T(8,128)(2,1)S(1)} %get-tuple-element.172, bf16[1024,1536]{1,0:T(8,128)(2,1)S(1)} %constant_dynamic-update-slice_fusion.6), kind=kOutput, calls=%fused_computation.4 | convolution fusion | flops 4834197504 | bytes 11010048 | tf_op jit(solution)/shard_map/dot_general | solution.py:48
  228.0 11.8 %fusion.7 = bf16[1024,1536]{1,0:T(8,128)(2,1)S(1)} fusion(f32[1024,1536]{1,0:T(8,128)} %get-tuple-element.268, f32[1536]{0:T(1024)S(1)} %fusion.27, bf16[1024,1536]{1,0:T(8,128)(2,1)} %copy-done.29, bf16[1536,1536]{1,0:T(8,128)(2,1)} %all-gather.8.cloned.1.call-done), kind=kOutput, calls=%fused_computation.12 | convolution fusion | flops 4864868352 | bytes 17307648 | tf_op jit(solution)/shard_map/dot_general | solution.py:44
  239.9 7.0 %fusion.42 = f32[1024,1536]{1,0:T(8,128)S(1)} fusion(bf16[1024,1536]{1,0:T(8,128)(2,1)S(1)} %fusion.7, bf16[1536,1536]{1,0:T(8,128)(2,1)} %copy-done.14), kind=kOutput, calls=%fused_computation.152 | convolution fusion | flops 4831838208 | bytes 14155776 | tf_op jit(solution)/shard_map/dot_general | solution.py:44
  247.5 3.0 collective-permute-done.22
  252.7 6.8 %convolution_convert_fusion.1 = bf16[1536,1536]{1,0:T(8,128)(2,1)} fusion(bf16[1024,1536]{1,0:T(8,128)(2,1)S(1)} %copy-done.26, bf16[1024,1536]{1,0:T(8,128)(2,1)S(1)} %fusion.7), kind=kOutput, calls=%fused_computation.3 | convolution fusion | flops 4834197504 | bytes 11010048 | tf_op jit(solution)/shard_map/dot_general | solution.py:48
  259.6 7.9 %fusion.43 = f32[1024,1536]{1,0:T(8,128)S(1)} fusion(bf16[1024,1536]{1,0:T(8,128)(2,1)} %copy-done.40, bf16[1536,1536]{1,0:T(8,128)(2,1)} %all-gather.8.cloned.1.call-done), kind=kOutput, calls=%fused_computation.153 | convolution fusion | flops 4831838208 | bytes 14155776 | tf_op jit(solution)/shard_map/dot_general | solution.py:52
  269.1 19.1 %collective-permute-done.23 = bf16[512,1536]{1,0:T(8,128)(2,1)} collective-permute-done((bf16[512,1536]{1,0:T(8,128)(2,1)}, bf16[512,1536]{1,0:T(8,128)(2,1)}, u32[]{:S(2)}, u32[]{:S(2)}) %collective-permute-start.23) | collective-permute-done | bytes 1572896 | tf_op jit(solution)/shard_map/ppermute | solution.py:192
  290.0 3.1 multiply_reduce_fusion.2
  294.9 3.1 fusion.35
  299.2 4.1 collective-permute-start.26
  310.6 2.8 fusion.21
  314.9 4.6 convolution_convert_fusion.4.grad_ref
  319.5 13.0 %attend_back.1 = bf16[1024,1152]{1,0:T(8,128)(2,1)} custom-call(s32[1]{0:T(128)} %bitcast.4.index_ref, bf16[1024,384]{1,0:T(8,128)(2,1)} %convolution_convert_fusion.4.grad_ref, bf16[3,1024,128]{2,1,0:T(8,128)(2,1)} %get-tuple-element.180.q_ref, bf16[3,1024,128]{2,1,0:T(8,128)(2,1)} %get-tuple-element.181.k_ref, ...), custom_call_target="tpu_custom_call" | custom-call | flops 6000000000 | bytes 12000000 | tf_op jit(solution)/shard_map/attend_back/pallas_call | solution.py:167
  332.5 7.4 %convolution_convert_fusion = bf16[1536,1152]{1,0:T(8,128)(2,1)S(1)} fusion(bf16[1024,1536]{1,0:T(8,128)(2,1)} %constant_dynamic-update-slice_fusion, bf16[1024,1152]{1,0:T(8,128)(2,1)} %attend_back.1), kind=kOutput, calls=%fused_computation.2 | convolution fusion | flops 3625648128 | bytes 9043968 | tf_op jit(solution)/shard_map/dot_general | solution.py:48
  345.4 4.3 fusion.44
  349.6 2.7 copy-done.18
  360.1 3.8 fusion.19
  364.0 2.7 fusion.20
  372.5 7.3 %collective-permute-start.34 = (bf16[384,1536]{1,0:T(8,128)(2,1)}, bf16[384,1536]{1,0:T(8,128)(2,1)}, u32[]{:S(2)}, u32[]{:S(2)}) collective-permute-start(bf16[384,1536]{1,0:T(8,128)(2,1)} %reduce-scatter.6.cloned.1.call-done), channel_id=1, source_target_pairs={{2,0},{3,1},{4,6},{5,7},{10,8},{11,9},{12,14},{13,15},{18,16},{19,... | collective-permute-start | bytes 3538952 | tf_op jit(solution)/shard_map/ppermute | solution.py:232
  387.1 7.7 %collective-permute-done.31 = bf16[256,1536]{1,0:T(8,128)(2,1)} collective-permute-done((bf16[256,1536]{1,0:T(8,128)(2,1)}, bf16[256,1536]{1,0:T(8,128)(2,1)}, u32[]{:S(2)}, u32[]{:S(2)}) %collective-permute-start.31) | collective-permute-done | bytes 786464 | tf_op jit(solution)/shard_map/ppermute | solution.py:192
  395.5 7.1 %collective-permute-done.33 = bf16[384,1152]{1,0:T(8,128)(2,1)} collective-permute-done((bf16[384,1152]{1,0:T(8,128)(2,1)}, bf16[384,1152]{1,0:T(8,128)(2,1)}, u32[]{:S(2)}, u32[]{:S(2)}) %collective-permute-start.33) | collective-permute-done | bytes 884768 | tf_op jit(solution)/shard_map/ppermute | solution.py:192
  402.6 2.9 collective-permute-done.34
  407.2 2.8 multiply_reduce_fusion.3
  410.7 12.3 %collective-permute-start.36 = (f32[4,1536]{1,0:T(4,128)S(1)}, f32[4,1536]{1,0:T(4,128)S(1)}, u32[]{:S(2)}, u32[]{:S(2)}) collective-permute-start(f32[4,1536]{1,0:T(4,128)S(1)} %pad_maximum_fusion.7), channel_id=1, source_target_pairs={{0,4},{1,5},{2,6},{3,7},{4,0},{5,1},{6,2},{7,3},{8,12},{9,13},{10,... | collective-permute-start | bytes 73736 | tf_op jit(solution)/shard_map/ppermute | solution.py:192
  429.1 5.3 %collective-permute-done.37 = f32[4,1536]{1,0:T(4,128)S(1)} collective-permute-done((f32[4,1536]{1,0:T(4,128)S(1)}, f32[4,1536]{1,0:T(4,128)S(1)}, u32[]{:S(2)}, u32[]{:S(2)}) %collective-permute-start.37) | collective-permute-done | bytes 24608 | tf_op jit(solution)/shard_map/ppermute | solution.py:192
  434.4 7.1 %collective-permute-done.38 = bf16[256,1536]{1,0:T(8,128)(2,1)S(1)} collective-permute-done((bf16[256,1536]{1,0:T(8,128)(2,1)S(1)}, bf16[256,1536]{1,0:T(8,128)(2,1)S(1)}, u32[]{:S(2)}, u32[]{:S(2)}) %collective-permute-start.38) | collective-permute-done | bytes 786464 | tf_op jit(solution)/shard_map/ppermute | solution.py:192
  441.5 3.6 collective-permute-done.41
  446.7 3.2 collective-permute-start.39
  454.2 20.2 %collective-permute-done.39 = bf16[192,1536]{1,0:T(8,128)(2,1)S(1)} collective-permute-done((bf16[192,1536]{1,0:T(8,128)(2,1)S(1)}, bf16[192,1536]{1,0:T(8,128)(2,1)S(1)}, u32[]{:S(2)}, u32[]{:S(2)}) %collective-permute-start.39) | collective-permute-done | bytes 589856 | tf_op jit(solution)/shard_map/ppermute | solution.py:192
  (261 shorter events, 128.1 us)
Async XLA Ops:
  7.2 77.0 %all-gather.4.cloned.1.call-start = ((), (), s32[]{:S(2)}) async-start(), calls=%async_computation.3 | async-start | bytes 4423680 | tf_op jit(solution)/shard_map/all_gather | solution.py:247
  9.9 22.5 %collective-permute-start.2 = (bf16[192,1152]{1,0:T(8,128)(2,1)S(1)}, bf16[192,1152]{1,0:T(8,128)(2,1)S(1)}, u32[]{:S(2)}, u32[]{:S(2)}) collective-permute-start(bf16[192,1152]{1,0:T(8,128)(2,1)S(1)} %bitcast.41), channel_id=1, source_target_pairs={{0,2},{1,3},{2,6},{3,7},{4,0},{5,1},{6,4},{7,5},{8,10},{9,11},{10,... | collective-permute-start | bytes 1327112 | tf_op jit(solution)/shard_map/ppermute | solution.py:192
  10.4 23.2 %collective-permute-start.1 = (bf16[192,1152]{1,0:T(8,128)(2,1)S(1)}, bf16[192,1152]{1,0:T(8,128)(2,1)S(1)}, u32[]{:S(2)}, u32[]{:S(2)}) collective-permute-start(bf16[192,1152]{1,0:T(8,128)(2,1)S(1)} %bitcast.42), channel_id=1, source_target_pairs={{0,0},{1,1},{2,4},{3,5},{4,2},{5,3},{6,6},{7,7},{8,8},{9,9},{10,12... | collective-permute-start | bytes 1327112 | tf_op jit(solution)/shard_map/ppermute | solution.py:192
  34.8 88.2 %all-gather.6.cloned.1.call-start = ((), (), s32[]{:S(2)}) async-start(), calls=%async_computation.4 | async-start | bytes 1474560 | tf_op jit(solution)/shard_map/all_gather | solution.py:247
  35.3 5.4 %collective-permute-start.4 = (bf16[192,1536]{1,0:T(8,128)(2,1)S(1)}, bf16[192,1536]{1,0:T(8,128)(2,1)S(1)}, u32[]{:S(2)}, u32[]{:S(2)}) collective-permute-start(bf16[192,1536]{1,0:T(8,128)(2,1)S(1)} %copy-done.28), channel_id=1, source_target_pairs={{0,4},{1,5},{2,6},{3,7},{4,0},{5,1},{6,2},{7,3},{8,12},{9,13},{10,... | collective-permute-start | bytes 1769480 | tf_op jit(solution)/shard_map/ppermute | solution.py:192
  35.4 22.7 %collective-permute-start.3 = (bf16[256,1536]{1,0:T(8,128)(2,1)S(1)}, bf16[256,1536]{1,0:T(8,128)(2,1)S(1)}, u32[]{:S(2)}, u32[]{:S(2)}) collective-permute-start(bf16[256,1536]{1,0:T(8,128)(2,1)S(1)} %copy-done.38), channel_id=1, source_target_pairs={{0,0},{1,1},{2,4},{3,5},{4,2},{5,3},{6,6},{7,7},{8,8},{9,9},{10,12... | collective-permute-start | bytes 2359304 | tf_op jit(solution)/shard_map/ppermute | solution.py:192
  58.2 14.4 %collective-permute-start.5 = (bf16[256,1536]{1,0:T(8,128)(2,1)S(1)}, bf16[256,1536]{1,0:T(8,128)(2,1)S(1)}, u32[]{:S(2)}, u32[]{:S(2)}) collective-permute-start(bf16[256,1536]{1,0:T(8,128)(2,1)S(1)} %collective-permute-done.3), channel_id=1, source_target_pairs={{0,1},{1,0},{2,3},{3,2},{4,5},{5,4},{6,7},{7,6},{8,9},{9,8},{10,11... | collective-permute-start | bytes 2359304 | tf_op jit(solution)/shard_map/ppermute | solution.py:192
  58.2 5.3 %collective-permute-start.7 = (bf16[48,1536]{1,0:T(8,128)(2,1)S(1)}, bf16[48,1536]{1,0:T(8,128)(2,1)S(1)}, u32[]{:S(2)}, u32[]{:S(2)}) collective-permute-start(bf16[48,1536]{1,0:T(8,128)(2,1)S(1)} %copy-done.39), channel_id=1, source_target_pairs={{0,2},{1,3},{2,6},{3,7},{4,0},{5,1},{6,4},{7,5},{8,10},{9,11},{10,... | collective-permute-start | bytes 442376 | tf_op jit(solution)/shard_map/ppermute | solution.py:192
  58.2 12.1 %collective-permute-start.6 = (bf16[48,1536]{1,0:T(8,128)(2,1)S(1)}, bf16[48,1536]{1,0:T(8,128)(2,1)S(1)}, u32[]{:S(2)}, u32[]{:S(2)}) collective-permute-start(bf16[48,1536]{1,0:T(8,128)(2,1)S(1)} %copy-done.39), channel_id=1, source_target_pairs={{0,0},{1,1},{2,4},{3,5},{4,2},{5,3},{6,6},{7,7},{8,8},{9,9},{10,12... | collective-permute-start | bytes 442376 | tf_op jit(solution)/shard_map/ppermute | solution.py:192
  75.7 5.9 %collective-permute-start.8 = (bf16[512,1536]{1,0:T(8,128)(2,1)S(1)}, bf16[512,1536]{1,0:T(8,128)(2,1)}, u32[]{:S(2)}, u32[]{:S(2)}) collective-permute-start(bf16[512,1536]{1,0:T(8,128)(2,1)S(1)} %get-tuple-element.124), channel_id=1, source_target_pairs={{0,4},{1,5},{2,6},{3,7},{4,0},{5,1},{6,2},{7,3},{8,12},{9,13},{10,... | collective-permute-start | bytes 4718600 | tf_op jit(solution)/shard_map/ppermute | solution.py:192
  75.8 152.2 %all-gather.8.cloned.1.call-start = ((), (), s32[]{:S(2)}) async-start(), calls=%async_computation.5 | async-start | bytes 5898240 | tf_op jit(solution)/shard_map/all_gather | solution.py:247
  75.8 27.1 %collective-permute-start.10 = (bf16[192,1536]{1,0:T(8,128)(2,1)}, bf16[192,1536]{1,0:T(8,128)(2,1)}, u32[]{:S(2)}, u32[]{:S(2)}) collective-permute-start(bf16[192,1536]{1,0:T(8,128)(2,1)} %param.22), channel_id=1, source_target_pairs={{0,2},{1,3},{2,6},{3,7},{4,0},{5,1},{6,4},{7,5},{8,10},{9,11},{10,... | collective-permute-start | bytes 1769480 | tf_op jit(solution)/shard_map/ppermute | solution.py:192
  76.4 28.4 %collective-permute-start.9 = (bf16[192,1536]{1,0:T(8,128)(2,1)}, bf16[192,1536]{1,0:T(8,128)(2,1)}, u32[]{:S(2)}, u32[]{:S(2)}) collective-permute-start(bf16[192,1536]{1,0:T(8,128)(2,1)} %param.22), channel_id=1, source_target_pairs={{0,0},{1,1},{2,4},{3,5},{4,2},{5,3},{6,6},{7,7},{8,8},{9,9},{10,12... | collective-permute-start | bytes 1769480 | tf_op jit(solution)/shard_map/ppermute | solution.py:192
  106.9 30.8 %collective-permute-start.13 = (bf16[384,1536]{1,0:T(8,128)(2,1)}, bf16[384,1536]{1,0:T(8,128)(2,1)}, u32[]{:S(2)}, u32[]{:S(2)}) collective-permute-start(bf16[384,1536]{1,0:T(8,128)(2,1)} %maximum_select_fusion), channel_id=1, source_target_pairs={{0,2},{1,3},{6,4},{7,5},{8,10},{9,11},{14,12},{15,13},{16,18},{17,... | collective-permute-start | bytes 3538952 | tf_op jit(solution)/shard_map/ppermute | solution.py:232
  108.6 30.0 %collective-permute-start.12 = (bf16[384,1536]{1,0:T(8,128)(2,1)S(1)}, bf16[384,1536]{1,0:T(8,128)(2,1)}, u32[]{:S(2)}, u32[]{:S(2)}) collective-permute-start(bf16[384,1536]{1,0:T(8,128)(2,1)S(1)} %maximum_select_fusion.1), channel_id=1, source_target_pairs={{0,16},{1,17},{2,18},{3,19},{4,20},{5,21},{6,22},{7,23},{8,24},{9,... | collective-permute-start | bytes 3538952 | tf_op jit(solution)/shard_map/ppermute | solution.py:192
  110.0 28.6 %collective-permute-start.11 = (bf16[384,1536]{1,0:T(8,128)(2,1)S(1)}, bf16[384,1536]{1,0:T(8,128)(2,1)}, u32[]{:S(2)}, u32[]{:S(2)}) collective-permute-start(bf16[384,1536]{1,0:T(8,128)(2,1)S(1)} %maximum_select_fusion.1), channel_id=1, source_target_pairs={{0,8},{1,9},{2,10},{3,11},{4,12},{5,13},{6,14},{7,15},{8,0},{9,1},... | collective-permute-start | bytes 3538952 | tf_op jit(solution)/shard_map/ppermute | solution.py:192
  138.6 4.2 collective-permute-start.14
  144.5 44.2 %collective-permute-start.15 = (bf16[512,1536]{1,0:T(8,128)(2,1)}, bf16[512,1536]{1,0:T(8,128)(2,1)S(1)}, u32[]{:S(2)}, u32[]{:S(2)}) collective-permute-start(bf16[512,1536]{1,0:T(8,128)(2,1)} %fusion.12), channel_id=1, source_target_pairs={{0,1},{1,0},{2,3},{3,2},{4,5},{5,4},{6,7},{7,6},{8,9},{9,8},{10,11... | collective-permute-start | bytes 4718600 | tf_op jit(solution)/shard_map/ppermute | solution.py:192
  145.7 43.0 %collective-permute-start.18 = (bf16[256,1536]{1,0:T(8,128)(2,1)}, bf16[256,1536]{1,0:T(8,128)(2,1)}, u32[]{:S(2)}, u32[]{:S(2)}) collective-permute-start(bf16[256,1536]{1,0:T(8,128)(2,1)} %param.13), channel_id=1, source_target_pairs={{0,0},{1,1},{2,4},{3,5},{4,2},{5,3},{6,6},{7,7},{8,8},{9,9},{10,12... | collective-permute-start | bytes 2359304 | tf_op jit(solution)/shard_map/ppermute | solution.py:192
  155.5 11.8 %collective-permute-start.17 = (bf16[192,1536]{1,0:T(8,128)(2,1)}, bf16[192,1536]{1,0:T(8,128)(2,1)}, u32[]{:S(2)}, u32[]{:S(2)}) collective-permute-start(bf16[192,1536]{1,0:T(8,128)(2,1)} %slice.131), channel_id=1, source_target_pairs={{0,8},{1,9},{2,10},{3,11},{4,12},{5,13},{6,14},{7,15},{8,0},{9,1},... | collective-permute-start | bytes 1769480 | tf_op jit(solution)/shard_map/ppermute | solution.py:192
  156.8 11.6 %collective-permute-start.16 = (bf16[192,1536]{1,0:T(8,128)(2,1)}, bf16[192,1536]{1,0:T(8,128)(2,1)}, u32[]{:S(2)}, u32[]{:S(2)}) collective-permute-start(bf16[192,1536]{1,0:T(8,128)(2,1)} %slice.130), channel_id=1, source_target_pairs={{0,16},{1,17},{2,18},{3,19},{4,20},{5,21},{6,22},{7,23},{8,24},{9,... | collective-permute-start | bytes 1769480 | tf_op jit(solution)/shard_map/ppermute | solution.py:192
  159.4 138.6 %reduce-scatter.4.cloned.1.call-start = ((), (), s32[]{:S(2)}) async-start(), calls=%async_computation.6 | async-start | bytes 5898240 | tf_op jit(solution)/shard_map/reduce_scatter | solution.py:279
  192.8 21.1 %collective-permute-start.20 = (bf16[256,1536]{1,0:T(8,128)(2,1)}, bf16[256,1536]{1,0:T(8,128)(2,1)S(1)}, u32[]{:S(2)}, u32[]{:S(2)}) collective-permute-start(bf16[256,1536]{1,0:T(8,128)(2,1)} %collective-permute-done.18), channel_id=1, source_target_pairs={{0,1},{1,0},{2,3},{3,2},{4,5},{5,4},{6,7},{7,6},{8,9},{9,8},{10,11... | collective-permute-start | bytes 2359304 | tf_op jit(solution)/shard_map/ppermute | solution.py:192
  195.9 7.4 %collective-permute-start.19 = (bf16[512,1536]{1,0:T(8,128)(2,1)S(1)}, bf16[512,1536]{1,0:T(8,128)(2,1)S(1)}, u32[]{:S(2)}, u32[]{:S(2)}) collective-permute-start(bf16[512,1536]{1,0:T(8,128)(2,1)S(1)} %get-tuple-element.162), channel_id=1, source_target_pairs={{0,4},{1,5},{2,6},{3,7},{4,0},{5,1},{6,2},{7,3},{8,12},{9,13},{10,... | collective-permute-start | bytes 4718600 | tf_op jit(solution)/shard_map/ppermute | solution.py:192
  215.3 3.7 collective-permute-start.21
  227.7 139.0 %reduce-scatter.6.cloned.1.call-start = ((), (), s32[]{:S(2)}) async-start(), calls=%async_computation.7 | async-start | bytes 5898240 | tf_op jit(solution)/shard_map/reduce_scatter | solution.py:279
  252.3 35.9 %collective-permute-start.23 = (bf16[512,1536]{1,0:T(8,128)(2,1)}, bf16[512,1536]{1,0:T(8,128)(2,1)}, u32[]{:S(2)}, u32[]{:S(2)}) collective-permute-start(bf16[512,1536]{1,0:T(8,128)(2,1)} %fusion.13), channel_id=1, source_target_pairs={{0,1},{1,0},{2,3},{3,2},{4,5},{5,4},{6,7},{7,6},{8,9},{9,8},{10,11... | collective-permute-start | bytes 4718600 | tf_op jit(solution)/shard_map/ppermute | solution.py:192
  259.6 126.4 %reduce-scatter.8.cloned.1.call-start = ((), (), s32[]{:S(2)}) async-start(), calls=%async_computation.8 | async-start | bytes 1474560 | tf_op jit(solution)/shard_map/reduce_scatter | solution.py:279
  297.9 6.8 %collective-permute-start.24 = (bf16[512,1536]{1,0:T(8,128)(2,1)}, bf16[512,1536]{1,0:T(8,128)(2,1)}, u32[]{:S(2)}, u32[]{:S(2)}) collective-permute-start(bf16[512,1536]{1,0:T(8,128)(2,1)} %get-tuple-element.176), channel_id=1, source_target_pairs={{0,4},{1,5},{2,6},{3,7},{4,0},{5,1},{6,2},{7,3},{8,12},{9,13},{10,... | collective-permute-start | bytes 4718600 | tf_op jit(solution)/shard_map/ppermute | solution.py:192
  299.1 11.4 %collective-permute-start.25 = (bf16[512,1536]{1,0:T(8,128)(2,1)}, bf16[512,1536]{1,0:T(8,128)(2,1)}, u32[]{:S(2)}, u32[]{:S(2)}) collective-permute-start(bf16[512,1536]{1,0:T(8,128)(2,1)} %slice.246), channel_id=1, source_target_pairs={{0,4},{1,5},{2,6},{3,7},{4,0},{5,1},{6,2},{7,3},{8,12},{9,13},{10,... | collective-permute-start | bytes 4718600 | tf_op jit(solution)/shard_map/ppermute | solution.py:192
  299.2 43.5 %collective-permute-start.26 = (bf16[384,1536]{1,0:T(8,128)(2,1)}, bf16[384,1536]{1,0:T(8,128)(2,1)}, u32[]{:S(2)}, u32[]{:S(2)}) collective-permute-start(bf16[384,1536]{1,0:T(8,128)(2,1)} %reduce-scatter.4.cloned.1.call-done), channel_id=1, source_target_pairs={{2,0},{3,1},{4,6},{5,7},{10,8},{11,9},{12,14},{13,15},{18,16},{19,... | collective-permute-start | bytes 3538952 | tf_op jit(solution)/shard_map/ppermute | solution.py:232
  313.4 30.5 %collective-permute-start.27 = (bf16[256,1536]{1,0:T(8,128)(2,1)}, bf16[256,1536]{1,0:T(8,128)(2,1)}, u32[]{:S(2)}, u32[]{:S(2)}) collective-permute-start(bf16[256,1536]{1,0:T(8,128)(2,1)} %fusion.21), channel_id=1, source_target_pairs={{0,1},{1,0},{2,3},{3,2},{4,5},{5,4},{6,7},{7,6},{8,9},{9,8},{10,11... | collective-permute-start | bytes 2359304 | tf_op jit(solution)/shard_map/ppermute | solution.py:192
  343.9 11.7 %collective-permute-start.28 = (bf16[192,1152]{1,0:T(8,128)(2,1)S(1)}, bf16[192,1152]{1,0:T(8,128)(2,1)}, u32[]{:S(2)}, u32[]{:S(2)}) collective-permute-start(bf16[192,1152]{1,0:T(8,128)(2,1)S(1)} %get-tuple-element.186), channel_id=1, source_target_pairs={{0,8},{1,9},{2,10},{3,11},{4,12},{5,13},{6,14},{7,15},{8,0},{9,1},... | collective-permute-start | bytes 1327112 | tf_op jit(solution)/shard_map/ppermute | solution.py:192
  345.2 11.5 %collective-permute-start.29 = (bf16[192,1152]{1,0:T(8,128)(2,1)S(1)}, bf16[192,1152]{1,0:T(8,128)(2,1)}, u32[]{:S(2)}, u32[]{:S(2)}) collective-permute-start(bf16[192,1152]{1,0:T(8,128)(2,1)S(1)} %get-tuple-element.187), channel_id=1, source_target_pairs={{0,16},{1,17},{2,18},{3,19},{4,20},{5,21},{6,22},{7,23},{8,24},{9,... | collective-permute-start | bytes 1327112 | tf_op jit(solution)/shard_map/ppermute | solution.py:192
  356.8 7.2 %collective-permute-start.30 = (bf16[512,1536]{1,0:T(8,128)(2,1)}, bf16[512,1536]{1,0:T(8,128)(2,1)}, u32[]{:S(2)}, u32[]{:S(2)}) collective-permute-start(bf16[512,1536]{1,0:T(8,128)(2,1)} %slice.245), channel_id=1, source_target_pairs={{0,4},{1,5},{2,6},{3,7},{4,0},{5,1},{6,2},{7,3},{8,12},{9,13},{10,... | collective-permute-start | bytes 4718600 | tf_op jit(solution)/shard_map/ppermute | solution.py:192
  366.7 28.1 %collective-permute-start.31 = (bf16[256,1536]{1,0:T(8,128)(2,1)}, bf16[256,1536]{1,0:T(8,128)(2,1)}, u32[]{:S(2)}, u32[]{:S(2)}) collective-permute-start(bf16[256,1536]{1,0:T(8,128)(2,1)} %fusion.20), channel_id=1, source_target_pairs={{0,1},{1,0},{2,3},{3,2},{4,5},{5,4},{6,7},{7,6},{8,9},{9,8},{10,11... | collective-permute-start | bytes 2359304 | tf_op jit(solution)/shard_map/ppermute | solution.py:192
  366.7 28.8 %collective-permute-start.35 = (bf16[256,1536]{1,0:T(8,128)(2,1)}, bf16[256,1536]{1,0:T(8,128)(2,1)}, u32[]{:S(2)}, u32[]{:S(2)}) collective-permute-start(bf16[256,1536]{1,0:T(8,128)(2,1)} %fusion.19), channel_id=1, source_target_pairs={{0,0},{1,1},{2,4},{3,5},{4,2},{5,3},{6,6},{7,7},{8,8},{9,9},{10,12... | collective-permute-start | bytes 2359304 | tf_op jit(solution)/shard_map/ppermute | solution.py:192
  372.5 23.1 %collective-permute-start.32 = (bf16[384,1152]{1,0:T(8,128)(2,1)}, bf16[384,1152]{1,0:T(8,128)(2,1)}, u32[]{:S(2)}, u32[]{:S(2)}) collective-permute-start(bf16[384,1152]{1,0:T(8,128)(2,1)} %pad_maximum_fusion.2), channel_id=1, source_target_pairs={{0,8},{1,9},{2,10},{3,11},{4,12},{5,13},{6,14},{7,15},{8,0},{9,1},... | collective-permute-start | bytes 2654216 | tf_op jit(solution)/shard_map/ppermute | solution.py:192
  372.5 33.0 %collective-permute-start.34 = (bf16[384,1536]{1,0:T(8,128)(2,1)}, bf16[384,1536]{1,0:T(8,128)(2,1)}, u32[]{:S(2)}, u32[]{:S(2)}) collective-permute-start(bf16[384,1536]{1,0:T(8,128)(2,1)} %reduce-scatter.6.cloned.1.call-done), channel_id=1, source_target_pairs={{2,0},{3,1},{4,6},{5,7},{10,8},{11,9},{12,14},{13,15},{18,16},{19,... | collective-permute-start | bytes 3538952 | tf_op jit(solution)/shard_map/ppermute | solution.py:232
  380.7 21.9 %collective-permute-start.33 = (bf16[384,1152]{1,0:T(8,128)(2,1)}, bf16[384,1152]{1,0:T(8,128)(2,1)}, u32[]{:S(2)}, u32[]{:S(2)}) collective-permute-start(bf16[384,1152]{1,0:T(8,128)(2,1)} %pad_maximum_fusion.3), channel_id=1, source_target_pairs={{0,16},{1,17},{2,18},{3,19},{4,20},{5,21},{6,22},{7,23},{8,24},{9,... | collective-permute-start | bytes 2654216 | tf_op jit(solution)/shard_map/ppermute | solution.py:192
  394.8 55.8 %collective-permute-start.44 = (f32[192,1536]{1,0:T(8,128)}, f32[192,1536]{1,0:T(8,128)S(1)}, u32[]{:S(2)}, u32[]{:S(2)}) collective-permute-start(f32[192,1536]{1,0:T(8,128)} %slice_select_fusion.1), channel_id=1, source_target_pairs={{0,4},{1,5},{2,6},{3,7},{4,0},{5,1},{6,2},{7,3},{8,12},{9,13},{10,... | collective-permute-start | bytes 3538952 | tf_op jit(solution)/shard_map/ppermute | solution.py:192
  410.7 18.2 %collective-permute-start.36 = (f32[4,1536]{1,0:T(4,128)S(1)}, f32[4,1536]{1,0:T(4,128)S(1)}, u32[]{:S(2)}, u32[]{:S(2)}) collective-permute-start(f32[4,1536]{1,0:T(4,128)S(1)} %pad_maximum_fusion.7), channel_id=1, source_target_pairs={{0,4},{1,5},{2,6},{3,7},{4,0},{5,1},{6,2},{7,3},{8,12},{9,13},{10,... | collective-permute-start | bytes 73736 | tf_op jit(solution)/shard_map/ppermute | solution.py:192
  423.0 18.5 %collective-permute-start.38 = (bf16[256,1536]{1,0:T(8,128)(2,1)S(1)}, bf16[256,1536]{1,0:T(8,128)(2,1)S(1)}, u32[]{:S(2)}, u32[]{:S(2)}) collective-permute-start(bf16[256,1536]{1,0:T(8,128)(2,1)S(1)} %fusion.16), channel_id=1, source_target_pairs={{0,0},{1,1},{2,4},{3,5},{4,2},{5,3},{6,6},{7,7},{8,8},{9,9},{10,12... | collective-permute-start | bytes 2359304 | tf_op jit(solution)/shard_map/ppermute | solution.py:192
  427.0 25.9 %collective-permute-start.45 = (f32[192,1536]{1,0:T(8,128)S(1)}, f32[192,1536]{1,0:T(8,128)S(1)}, u32[]{:S(2)}, u32[]{:S(2)}) collective-permute-start(f32[192,1536]{1,0:T(8,128)S(1)} %slice_select_fusion), channel_id=1, source_target_pairs={{0,4},{1,5},{2,6},{3,7},{4,0},{5,1},{6,2},{7,3},{8,12},{9,13},{10,... | collective-permute-start | bytes 3538952 | tf_op jit(solution)/shard_map/ppermute | solution.py:192
  428.9 5.4 %collective-permute-start.37 = (f32[4,1536]{1,0:T(4,128)S(1)}, f32[4,1536]{1,0:T(4,128)S(1)}, u32[]{:S(2)}, u32[]{:S(2)}) collective-permute-start(f32[4,1536]{1,0:T(4,128)S(1)} %add.263), channel_id=1, source_target_pairs={{0,1},{1,0},{2,3},{3,2},{4,5},{5,4},{6,7},{7,6},{8,9},{9,8},{10,11... | collective-permute-start | bytes 73736 | tf_op jit(solution)/shard_map/ppermute | solution.py:192
  445.1 4.7 collective-permute-start.42
  446.6 7.6 %collective-permute-start.40 = (bf16[192,1536]{1,0:T(8,128)(2,1)S(1)}, bf16[192,1536]{1,0:T(8,128)(2,1)S(1)}, u32[]{:S(2)}, u32[]{:S(2)}) collective-permute-start(bf16[192,1536]{1,0:T(8,128)(2,1)S(1)} %get-tuple-element.258), channel_id=1, source_target_pairs={{0,4},{1,5},{2,0},{3,1},{4,6},{5,7},{6,2},{7,3},{8,12},{9,13},{10,... | collective-permute-start | bytes 1769480 | tf_op jit(solution)/shard_map/ppermute | solution.py:192
  446.7 27.8 %collective-permute-start.39 = (bf16[192,1536]{1,0:T(8,128)(2,1)S(1)}, bf16[192,1536]{1,0:T(8,128)(2,1)S(1)}, u32[]{:S(2)}, u32[]{:S(2)}) collective-permute-start(bf16[192,1536]{1,0:T(8,128)(2,1)S(1)} %get-tuple-element.259), channel_id=1, source_target_pairs={{0,0},{1,1},{2,4},{3,5},{4,2},{5,3},{6,6},{7,7},{8,8},{9,9},{10,12... | collective-permute-start | bytes 1769480 | tf_op jit(solution)/shard_map/ppermute | solution.py:192
  (47 other events, 773.5 us)
Sparse Core Ops, SparseCore 0:
  34.9 48.9 all-gather.3
  86.3 29.3 all-gather.5
  159.5 58.5 all-gather.7
  227.8 55.4 reduce-scatter.3
  286.2 57.0 reduce-scatter.5
  358.1 27.8 reduce-scatter.7

commit v6 on v5

--- a/solution.py
+++ b/solution.py
@@ -463,9 +463,7 @@
     out_got = layout.core(out_send)
     resid_all = jnp.concatenate([resid_low, layout.core(resid_low)])
     mixed_grad = dot_nt(resid_all, wide_out).astype(BF16)
-    grad_out_part = dot_tn(mixed, resid_all).astype(BF16)
-    grad_out_sum = layout.scatter(grad_out_part)
-    out_got = after(out_got, grad_out_part)
+    out_got = after(out_got, mixed_grad)
     out_send = (out_part[rows : 2 * rows] + out_got[rows:].astype(F32)).astype(BF16)
     out_other = layout.pair(out_send)
     projected_grad = attend_back(
@@ -477,7 +475,10 @@
 
     got_qkv = layout.scatter_near(grad_qkv_part, near_qkv)
     one_part = dot_nt(projected_grad, wide_qkv)
-    one_send, got_qkv = hold(one_part[2 * rows :].astype(BF16), got_qkv)
+    one_send = one_part[2 * rows :].astype(BF16)
+    grad_out_part = dot_tn(mixed, after(resid_all, one_send)).astype(BF16)
+    one_send, got_qkv, grad_out_part = hold(one_send, got_qkv, grad_out_part)
+    grad_out_sum = layout.scatter(grad_out_part)
     one_got = layout.core(one_send)
     output = resid_one[:rows] + out_part[:rows] + out_got[:rows].astype(F32) + after(out_other, one_send).astype(F32)
     one_got, output = hold(one_got, output.astype(BF16))

time: 496 us -> 497 us (level)
    unnamed x90 -> x92, local copies, waits for them, and re-layouts: 20.6 us -> 18.8 us
  transfers between devices with their start and end apart: 52 -> 52, of which waited for: 31 -> 31; matrix products, arithmetic and copies ran while one was open for 34% -> 33% of each run, Pallas kernels for 5% -> 5%
where the time goes in v6:
time: 497 us; the launch traced here: 487 us
  waiting for transfers between devices  187 us (38%)
  matrix products  78.4 us (16%)
  starting transfers between devices  77.3 us (16%)
  other arithmetic  57.3 us (12%)
  local copies, waits for them, and re-layouts  46.8 us (9%)
  Pallas kernels  23.8 us (5%)
  between operations  16.8 us (3%)
    ppermute x43, waiting for transfers between devices, permute(): return lax.ppermute(value, AXES, pairs)  173 us
    ppermute x43, starting transfers between devices, permute(): return lax.ppermute(value, AXES, pairs)  62.5 us
    dot_general x4, matrix products, dot_nn(): lax.dot_general(left, right, (((1,), (0,)), ((), ())), preferred_element_...  28.5 us
    dot_general x4, matrix products, dot_nt(): lax.dot_general(left, right, (((1,), (1,)), ((), ())), preferred_element_...  25.8 us
    dot_general x4, matrix products, dot_tn(): lax.dot_general(left, right, (((0,), (0,)), ((), ())), preferred_element_...  24.2 us
    unnamed x92, local copies, waits for them, and re-layouts  18.8 us
    ppermute x3, starting transfers between devices, flip(): return lax.ppermute(value, AXES, pairs)  14.2 us
    pallas_call x1, Pallas kernels, attend_back(): pl.pallas_call(functools.partial(attend_back_kernel, heads, slots), in_sp...  13.1 us
  transfers between devices with their start and end apart: 52, of which 31 were waited for; matrix products, arithmetic and copies ran while one was open for 33% of the time, Pallas kernels for 5%

profile of v6, /device:TPU:1, one launch (start us, length us, event | category | flops | bytes accessed | tf_op | source)
XLA Modules:
  0.0 487.2 jit_solution(2281015235039616914)
XLA Ops:
  10.4 5.6 %collective-permute-start.1 = (bf16[192,1152]{1,0:T(8,128)(2,1)S(1)}, bf16[192,1152]{1,0:T(8,128)(2,1)S(1)}, u32[]{:S(2)}, u32[]{:S(2)}) collective-permute-start(bf16[192,1152]{1,0:T(8,128)(2,1)S(1)} %bitcast.42), channel_id=1, source_target_pairs={{0,0},{1,1},{2,4},{3,5},{4,2},{5,3},{6,6},{7,7},{8,8},{9,9},{10,12... | collective-permute-start | bytes 1327112 | tf_op jit(solution)/shard_map/ppermute | solution.py:192
  16.0 16.3 %collective-permute-done.2 = bf16[192,1152]{1,0:T(8,128)(2,1)S(1)} collective-permute-done((bf16[192,1152]{1,0:T(8,128)(2,1)S(1)}, bf16[192,1152]{1,0:T(8,128)(2,1)S(1)}, u32[]{:S(2)}, u32[]{:S(2)}) %collective-permute-start.2) | collective-permute-done | bytes 442400 | tf_op jit(solution)/shard_map/ppermute | solution.py:192
  42.0 16.2 %collective-permute-done.3 = bf16[256,1536]{1,0:T(8,128)(2,1)S(1)} collective-permute-done((bf16[256,1536]{1,0:T(8,128)(2,1)S(1)}, bf16[256,1536]{1,0:T(8,128)(2,1)S(1)}, u32[]{:S(2)}, u32[]{:S(2)}) %collective-permute-start.3) | collective-permute-done | bytes 786464 | tf_op jit(solution)/shard_map/ppermute | solution.py:192
  58.2 3.4 collective-permute-start.6
  63.5 6.8 %collective-permute-done.6 = bf16[48,1536]{1,0:T(8,128)(2,1)S(1)} collective-permute-done((bf16[48,1536]{1,0:T(8,128)(2,1)S(1)}, bf16[48,1536]{1,0:T(8,128)(2,1)S(1)}, u32[]{:S(2)}, u32[]{:S(2)}) %collective-permute-start.6) | collective-permute-done | bytes 147488 | tf_op jit(solution)/shard_map/ppermute | solution.py:192
  76.4 3.8 collective-permute-start.9
  81.4 2.7 constant_dynamic-update-slice_fusion
  84.1 9.3 %fusion.40.proj_ref = f32[1024,1152]{1,0:T(8,128)} fusion(bf16[1024,1536]{1,0:T(8,128)(2,1)} %constant_dynamic-update-slice_fusion, bf16[1536,1152]{1,0:T(8,128)(2,1)} %all-gather.4.cloned.1.call-done), kind=kOutput, calls=%fused_computation.150 | convolution fusion | flops 3623878656 | bytes 11403264 | tf_op jit(solution)/shard_map/dot_general | solution.py:52
  93.5 9.5 %collective-permute-done.10 = bf16[192,1536]{1,0:T(8,128)(2,1)} collective-permute-done((bf16[192,1536]{1,0:T(8,128)(2,1)}, bf16[192,1536]{1,0:T(8,128)(2,1)}, u32[]{:S(2)}, u32[]{:S(2)}) %collective-permute-start.10) | collective-permute-done | bytes 589856 | tf_op jit(solution)/shard_map/ppermute | solution.py:192
  112.2 10.7 %attend.1 = (bf16[1024,384]{1,0:T(8,128)(2,1)}, bf16[3,1024,128]{2,1,0:T(8,128)(2,1)}, bf16[3,1024,128]{2,1,0:T(8,128)(2,1)}, bf16[3,1024,128]{2,1,0:T(8,128)(2,1)}, f32[3,1024,1]{2,1,0:T(8,128)}) custom-call(s32[1]{0:T(128)} %bitcast.4.index_ref, f32[1024,1152]{1,0:T(8,128)} %fusion.40.proj_ref, f32[1024,128]{1,0:T(8,128)} %get-tuple-element.134.cos_ref, ...), custom_call_target="tpu_custom_call" | custom-call | flops 3000000000 | bytes 12000000 | tf_op jit(solution)/shard_map/attend/pallas_call | solution.py:149
  123.0 3.3 fusion.41
  126.5 11.2 %collective-permute-done.13 = bf16[384,1536]{1,0:T(8,128)(2,1)} collective-permute-done((bf16[384,1536]{1,0:T(8,128)(2,1)}, bf16[384,1536]{1,0:T(8,128)(2,1)}, u32[]{:S(2)}, u32[]{:S(2)}) %collective-permute-start.13) | collective-permute-done | bytes 1179680 | tf_op jit(solution)/shard_map/ppermute | solution.py:232
  139.7 3.0 collective-permute-done.14
  145.7 4.7 collective-permute-start.18
  159.7 7.7 %collective-permute-done.17 = bf16[192,1536]{1,0:T(8,128)(2,1)} collective-permute-done((bf16[192,1536]{1,0:T(8,128)(2,1)}, bf16[192,1536]{1,0:T(8,128)(2,1)}, u32[]{:S(2)}, u32[]{:S(2)}) %collective-permute-start.17) | collective-permute-done | bytes 589856 | tf_op jit(solution)/shard_map/ppermute | solution.py:192
  168.4 20.3 %collective-permute-done.18 = bf16[256,1536]{1,0:T(8,128)(2,1)} collective-permute-done((bf16[256,1536]{1,0:T(8,128)(2,1)}, bf16[256,1536]{1,0:T(8,128)(2,1)}, u32[]{:S(2)}, u32[]{:S(2)}) %collective-permute-start.18) | collective-permute-done | bytes 786464 | tf_op jit(solution)/shard_map/ppermute | solution.py:192
  193.0 3.1 collective-permute-start.20
  203.7 7.9 %multiply_convert_fusion = (bf16[1024,1536]{1,0:T(8,128)(2,1)S(1)}, f32[1024,1536]{1,0:T(8,128)}) fusion(f32[1536]{0:T(1024)S(1)} %fusion.27, bf16[1024,1536]{1,0:T(8,128)(2,1)S(1)} %constant_dynamic-update-slice_fusion.2, bf16[1536,1536]{1,0:T(8,128)(2,1)S(1)} %constant_dynamic-update-slice_fusion.11), kind=kOutput, calls=%fused_computation.13 | convolution fusion | flops 4847566848 | bytes 17307648 | tf_op jit(solution)/shard_map/dot_general | solution.py:52
  216.1 3.0 collective-permute-done.21
  220.9 6.9 %convolution_convert_fusion.2 = bf16[1536,1536]{1,0:T(8,128)(2,1)} fusion(bf16[1024,1536]{1,0:T(8,128)(2,1)S(1)} %get-tuple-element.174, bf16[1024,1536]{1,0:T(8,128)(2,1)S(1)} %constant_dynamic-update-slice_fusion.6), kind=kOutput, calls=%fused_computation.4 | convolution fusion | flops 4834197504 | bytes 11010048 | tf_op jit(solution)/shard_map/dot_general | solution.py:48
  228.2 11.9 %fusion.7 = bf16[1024,1536]{1,0:T(8,128)(2,1)S(1)} fusion(f32[1024,1536]{1,0:T(8,128)} %get-tuple-element.272, f32[1536]{0:T(1024)S(1)} %fusion.27, bf16[1024,1536]{1,0:T(8,128)(2,1)} %copy-done.30, bf16[1536,1536]{1,0:T(8,128)(2,1)} %all-gather.8.cloned.1.call-done), kind=kOutput, calls=%fused_computation.12 | convolution fusion | flops 4864868352 | bytes 17307648 | tf_op jit(solution)/shard_map/dot_general | solution.py:44
  240.0 7.0 %fusion.42 = f32[1024,1536]{1,0:T(8,128)S(1)} fusion(bf16[1024,1536]{1,0:T(8,128)(2,1)S(1)} %fusion.7, bf16[1536,1536]{1,0:T(8,128)(2,1)} %copy-done.14), kind=kOutput, calls=%fused_computation.152 | convolution fusion | flops 4831838208 | bytes 14155776 | tf_op jit(solution)/shard_map/dot_general | solution.py:44
  247.7 3.0 collective-permute-done.22
  252.9 6.9 %convolution_convert_fusion.1 = bf16[1536,1536]{1,0:T(8,128)(2,1)} fusion(bf16[1024,1536]{1,0:T(8,128)(2,1)S(1)} %copy-done.26, bf16[1024,1536]{1,0:T(8,128)(2,1)S(1)} %fusion.7), kind=kOutput, calls=%fused_computation.3 | convolution fusion | flops 4834197504 | bytes 11010048 | tf_op jit(solution)/shard_map/dot_general | solution.py:48
  259.8 8.0 %fusion.43 = f32[1024,1536]{1,0:T(8,128)S(1)} fusion(bf16[1024,1536]{1,0:T(8,128)(2,1)} %copy-done.41, bf16[1536,1536]{1,0:T(8,128)(2,1)} %all-gather.8.cloned.1.call-done), kind=kOutput, calls=%fused_computation.153 | convolution fusion | flops 4831838208 | bytes 14155776 | tf_op jit(solution)/shard_map/dot_general | solution.py:52
  269.3 19.1 %collective-permute-done.23 = bf16[512,1536]{1,0:T(8,128)(2,1)} collective-permute-done((bf16[512,1536]{1,0:T(8,128)(2,1)}, bf16[512,1536]{1,0:T(8,128)(2,1)}, u32[]{:S(2)}, u32[]{:S(2)}) %collective-permute-start.23) | collective-permute-done | bytes 1572896 | tf_op jit(solution)/shard_map/ppermute | solution.py:192
  290.2 3.1 multiply_reduce_fusion.2
  294.9 3.0 fusion.35
  299.2 4.2 collective-permute-start.26
  306.7 2.7 convolution_convert_fusion.4.grad_ref
  313.5 13.1 %attend_back.1 = bf16[1024,1152]{1,0:T(8,128)(2,1)} custom-call(s32[1]{0:T(128)} %bitcast.4.index_ref, bf16[1024,384]{1,0:T(8,128)(2,1)} %convolution_convert_fusion.4.grad_ref, bf16[3,1024,128]{2,1,0:T(8,128)(2,1)} %get-tuple-element.182.q_ref, bf16[3,1024,128]{2,1,0:T(8,128)(2,1)} %get-tuple-element.183.k_ref, ...), custom_call_target="tpu_custom_call" | custom-call | flops 6000000000 | bytes 12000000 | tf_op jit(solution)/shard_map/attend_back/pallas_call | solution.py:167
  326.5 7.9 %convolution_convert_fusion = bf16[1536,1152]{1,0:T(8,128)(2,1)S(1)} fusion(bf16[1024,1536]{1,0:T(8,128)(2,1)} %constant_dynamic-update-slice_fusion, bf16[1024,1152]{1,0:T(8,128)(2,1)} %attend_back.1), kind=kOutput, calls=%fused_computation.2 | convolution fusion | flops 3625648128 | bytes 9043968 | tf_op jit(solution)/shard_map/dot_general | solution.py:48
  337.5 5.0 %collective-permute-done.27 = bf16[256,1536]{1,0:T(8,128)(2,1)} collective-permute-done((bf16[256,1536]{1,0:T(8,128)(2,1)}, bf16[256,1536]{1,0:T(8,128)(2,1)}, u32[]{:S(2)}, u32[]{:S(2)}) %collective-permute-start.27) | collective-permute-done | bytes 786464 | tf_op jit(solution)/shard_map/ppermute | solution.py:192
  343.8 4.2 fusion.44
  348.0 2.7 copy-done.18
  358.8 3.6 fusion.19
  362.5 2.7 fusion.20
  365.2 2.8 collective-permute-start.35
  372.7 8.2 %collective-permute-start.34 = (bf16[384,1536]{1,0:T(8,128)(2,1)}, bf16[384,1536]{1,0:T(8,128)(2,1)}, u32[]{:S(2)}, u32[]{:S(2)}) collective-permute-start(bf16[384,1536]{1,0:T(8,128)(2,1)} %reduce-scatter.6.cloned.1.call-done), channel_id=1, source_target_pairs={{2,0},{3,1},{4,6},{5,7},{10,8},{11,9},{12,14},{13,15},{18,16},{19,... | collective-permute-start | bytes 3538952 | tf_op jit(solution)/shard_map/ppermute | solution.py:232
  388.9 5.2 %collective-permute-done.31 = bf16[256,1536]{1,0:T(8,128)(2,1)} collective-permute-done((bf16[256,1536]{1,0:T(8,128)(2,1)}, bf16[256,1536]{1,0:T(8,128)(2,1)}, u32[]{:S(2)}, u32[]{:S(2)}) %collective-permute-start.31) | collective-permute-done | bytes 786464 | tf_op jit(solution)/shard_map/ppermute | solution.py:192
  394.8 7.8 %collective-permute-done.33 = bf16[384,1152]{1,0:T(8,128)(2,1)} collective-permute-done((bf16[384,1152]{1,0:T(8,128)(2,1)}, bf16[384,1152]{1,0:T(8,128)(2,1)}, u32[]{:S(2)}, u32[]{:S(2)}) %collective-permute-start.33) | collective-permute-done | bytes 884768 | tf_op jit(solution)/shard_map/ppermute | solution.py:192
  405.7 2.8 multiply_reduce_fusion.3
  409.1 13.3 %collective-permute-start.36 = (f32[4,1536]{1,0:T(4,128)S(1)}, f32[4,1536]{1,0:T(4,128)S(1)}, u32[]{:S(2)}, u32[]{:S(2)}) collective-permute-start(f32[4,1536]{1,0:T(4,128)S(1)} %pad_maximum_fusion.7), channel_id=1, source_target_pairs={{0,4},{1,5},{2,6},{3,7},{4,0},{5,1},{6,2},{7,3},{8,12},{9,13},{10,... | collective-permute-start | bytes 73736 | tf_op jit(solution)/shard_map/ppermute | solution.py:192
  429.1 4.8 collective-permute-done.37
  433.9 8.9 %collective-permute-done.38 = bf16[256,1536]{1,0:T(8,128)(2,1)S(1)} collective-permute-done((bf16[256,1536]{1,0:T(8,128)(2,1)S(1)}, bf16[256,1536]{1,0:T(8,128)(2,1)S(1)}, u32[]{:S(2)}, u32[]{:S(2)}) %collective-permute-start.38) | collective-permute-done | bytes 786464 | tf_op jit(solution)/shard_map/ppermute | solution.py:192
  442.7 3.6 collective-permute-done.41
  447.0 3.2 collective-permute-start.39
  454.5 20.2 %collective-permute-done.39 = bf16[192,1536]{1,0:T(8,128)(2,1)S(1)} collective-permute-done((bf16[192,1536]{1,0:T(8,128)(2,1)S(1)}, bf16[192,1536]{1,0:T(8,128)(2,1)S(1)}, u32[]{:S(2)}, u32[]{:S(2)}) %collective-permute-start.39) | collective-permute-done | bytes 589856 | tf_op jit(solution)/shard_map/ppermute | solution.py:192
  (263 shorter events, 126.3 us)
Async XLA Ops:
  7.2 76.9 %all-gather.4.cloned.1.call-start = ((), (), s32[]{:S(2)}) async-start(), calls=%async_computation.3 | async-start | bytes 4423680 | tf_op jit(solution)/shard_map/all_gather | solution.py:247
  9.9 22.5 %collective-permute-start.2 = (bf16[192,1152]{1,0:T(8,128)(2,1)S(1)}, bf16[192,1152]{1,0:T(8,128)(2,1)S(1)}, u32[]{:S(2)}, u32[]{:S(2)}) collective-permute-start(bf16[192,1152]{1,0:T(8,128)(2,1)S(1)} %bitcast.41), channel_id=1, source_target_pairs={{0,2},{1,3},{2,6},{3,7},{4,0},{5,1},{6,4},{7,5},{8,10},{9,11},{10,... | collective-permute-start | bytes 1327112 | tf_op jit(solution)/shard_map/ppermute | solution.py:192
  10.4 23.2 %collective-permute-start.1 = (bf16[192,1152]{1,0:T(8,128)(2,1)S(1)}, bf16[192,1152]{1,0:T(8,128)(2,1)S(1)}, u32[]{:S(2)}, u32[]{:S(2)}) collective-permute-start(bf16[192,1152]{1,0:T(8,128)(2,1)S(1)} %bitcast.42), channel_id=1, source_target_pairs={{0,0},{1,1},{2,4},{3,5},{4,2},{5,3},{6,6},{7,7},{8,8},{9,9},{10,12... | collective-permute-start | bytes 1327112 | tf_op jit(solution)/shard_map/ppermute | solution.py:192
  34.8 88.2 %all-gather.6.cloned.1.call-start = ((), (), s32[]{:S(2)}) async-start(), calls=%async_computation.4 | async-start | bytes 1474560 | tf_op jit(solution)/shard_map/all_gather | solution.py:247
  35.3 5.3 %collective-permute-start.4 = (bf16[192,1536]{1,0:T(8,128)(2,1)S(1)}, bf16[192,1536]{1,0:T(8,128)(2,1)S(1)}, u32[]{:S(2)}, u32[]{:S(2)}) collective-permute-start(bf16[192,1536]{1,0:T(8,128)(2,1)S(1)} %copy-done.29), channel_id=1, source_target_pairs={{0,4},{1,5},{2,6},{3,7},{4,0},{5,1},{6,2},{7,3},{8,12},{9,13},{10,... | collective-permute-start | bytes 1769480 | tf_op jit(solution)/shard_map/ppermute | solution.py:192
  35.4 22.7 %collective-permute-start.3 = (bf16[256,1536]{1,0:T(8,128)(2,1)S(1)}, bf16[256,1536]{1,0:T(8,128)(2,1)S(1)}, u32[]{:S(2)}, u32[]{:S(2)}) collective-permute-start(bf16[256,1536]{1,0:T(8,128)(2,1)S(1)} %copy-done.39), channel_id=1, source_target_pairs={{0,0},{1,1},{2,4},{3,5},{4,2},{5,3},{6,6},{7,7},{8,8},{9,9},{10,12... | collective-permute-start | bytes 2359304 | tf_op jit(solution)/shard_map/ppermute | solution.py:192
  58.1 14.4 %collective-permute-start.5 = (bf16[256,1536]{1,0:T(8,128)(2,1)S(1)}, bf16[256,1536]{1,0:T(8,128)(2,1)S(1)}, u32[]{:S(2)}, u32[]{:S(2)}) collective-permute-start(bf16[256,1536]{1,0:T(8,128)(2,1)S(1)} %collective-permute-done.3), channel_id=1, source_target_pairs={{0,1},{1,0},{2,3},{3,2},{4,5},{5,4},{6,7},{7,6},{8,9},{9,8},{10,11... | collective-permute-start | bytes 2359304 | tf_op jit(solution)/shard_map/ppermute | solution.py:192
  58.2 5.3 %collective-permute-start.7 = (bf16[48,1536]{1,0:T(8,128)(2,1)S(1)}, bf16[48,1536]{1,0:T(8,128)(2,1)S(1)}, u32[]{:S(2)}, u32[]{:S(2)}) collective-permute-start(bf16[48,1536]{1,0:T(8,128)(2,1)S(1)} %copy-done.40), channel_id=1, source_target_pairs={{0,2},{1,3},{2,6},{3,7},{4,0},{5,1},{6,4},{7,5},{8,10},{9,11},{10,... | collective-permute-start | bytes 442376 | tf_op jit(solution)/shard_map/ppermute | solution.py:192
  58.2 12.1 %collective-permute-start.6 = (bf16[48,1536]{1,0:T(8,128)(2,1)S(1)}, bf16[48,1536]{1,0:T(8,128)(2,1)S(1)}, u32[]{:S(2)}, u32[]{:S(2)}) collective-permute-start(bf16[48,1536]{1,0:T(8,128)(2,1)S(1)} %copy-done.40), channel_id=1, source_target_pairs={{0,0},{1,1},{2,4},{3,5},{4,2},{5,3},{6,6},{7,7},{8,8},{9,9},{10,12... | collective-permute-start | bytes 442376 | tf_op jit(solution)/shard_map/ppermute | solution.py:192
  75.7 5.7 %collective-permute-start.8 = (bf16[512,1536]{1,0:T(8,128)(2,1)S(1)}, bf16[512,1536]{1,0:T(8,128)(2,1)}, u32[]{:S(2)}, u32[]{:S(2)}) collective-permute-start(bf16[512,1536]{1,0:T(8,128)(2,1)S(1)} %get-tuple-element.126), channel_id=1, source_target_pairs={{0,4},{1,5},{2,6},{3,7},{4,0},{5,1},{6,2},{7,3},{8,12},{9,13},{10,... | collective-permute-start | bytes 4718600 | tf_op jit(solution)/shard_map/ppermute | solution.py:192
  75.8 152.4 %all-gather.8.cloned.1.call-start = ((), (), s32[]{:S(2)}) async-start(), calls=%async_computation.5 | async-start | bytes 5898240 | tf_op jit(solution)/shard_map/all_gather | solution.py:247
  75.8 27.2 %collective-permute-start.10 = (bf16[192,1536]{1,0:T(8,128)(2,1)}, bf16[192,1536]{1,0:T(8,128)(2,1)}, u32[]{:S(2)}, u32[]{:S(2)}) collective-permute-start(bf16[192,1536]{1,0:T(8,128)(2,1)} %param.22), channel_id=1, source_target_pairs={{0,2},{1,3},{2,6},{3,7},{4,0},{5,1},{6,4},{7,5},{8,10},{9,11},{10,... | collective-permute-start | bytes 1769480 | tf_op jit(solution)/shard_map/ppermute | solution.py:192
  76.4 28.4 %collective-permute-start.9 = (bf16[192,1536]{1,0:T(8,128)(2,1)}, bf16[192,1536]{1,0:T(8,128)(2,1)}, u32[]{:S(2)}, u32[]{:S(2)}) collective-permute-start(bf16[192,1536]{1,0:T(8,128)(2,1)} %param.22), channel_id=1, source_target_pairs={{0,0},{1,1},{2,4},{3,5},{4,2},{5,3},{6,6},{7,7},{8,8},{9,9},{10,12... | collective-permute-start | bytes 1769480 | tf_op jit(solution)/shard_map/ppermute | solution.py:192
  106.9 30.8 %collective-permute-start.13 = (bf16[384,1536]{1,0:T(8,128)(2,1)}, bf16[384,1536]{1,0:T(8,128)(2,1)}, u32[]{:S(2)}, u32[]{:S(2)}) collective-permute-start(bf16[384,1536]{1,0:T(8,128)(2,1)} %maximum_select_fusion), channel_id=1, source_target_pairs={{0,2},{1,3},{6,4},{7,5},{8,10},{9,11},{14,12},{15,13},{16,18},{17,... | collective-permute-start | bytes 3538952 | tf_op jit(solution)/shard_map/ppermute | solution.py:232
  108.6 30.0 %collective-permute-start.12 = (bf16[384,1536]{1,0:T(8,128)(2,1)S(1)}, bf16[384,1536]{1,0:T(8,128)(2,1)}, u32[]{:S(2)}, u32[]{:S(2)}) collective-permute-start(bf16[384,1536]{1,0:T(8,128)(2,1)S(1)} %maximum_select_fusion.1), channel_id=1, source_target_pairs={{0,16},{1,17},{2,18},{3,19},{4,20},{5,21},{6,22},{7,23},{8,24},{9,... | collective-permute-start | bytes 3538952 | tf_op jit(solution)/shard_map/ppermute | solution.py:192
  110.0 28.6 %collective-permute-start.11 = (bf16[384,1536]{1,0:T(8,128)(2,1)S(1)}, bf16[384,1536]{1,0:T(8,128)(2,1)}, u32[]{:S(2)}, u32[]{:S(2)}) collective-permute-start(bf16[384,1536]{1,0:T(8,128)(2,1)S(1)} %maximum_select_fusion.1), channel_id=1, source_target_pairs={{0,8},{1,9},{2,10},{3,11},{4,12},{5,13},{6,14},{7,15},{8,0},{9,1},... | collective-permute-start | bytes 3538952 | tf_op jit(solution)/shard_map/ppermute | solution.py:192
  138.6 4.2 collective-permute-start.14
  144.5 44.2 %collective-permute-start.15 = (bf16[512,1536]{1,0:T(8,128)(2,1)}, bf16[512,1536]{1,0:T(8,128)(2,1)S(1)}, u32[]{:S(2)}, u32[]{:S(2)}) collective-permute-start(bf16[512,1536]{1,0:T(8,128)(2,1)} %fusion.12), channel_id=1, source_target_pairs={{0,1},{1,0},{2,3},{3,2},{4,5},{5,4},{6,7},{7,6},{8,9},{9,8},{10,11... | collective-permute-start | bytes 4718600 | tf_op jit(solution)/shard_map/ppermute | solution.py:192
  145.7 43.0 %collective-permute-start.18 = (bf16[256,1536]{1,0:T(8,128)(2,1)}, bf16[256,1536]{1,0:T(8,128)(2,1)}, u32[]{:S(2)}, u32[]{:S(2)}) collective-permute-start(bf16[256,1536]{1,0:T(8,128)(2,1)} %param.13), channel_id=1, source_target_pairs={{0,0},{1,1},{2,4},{3,5},{4,2},{5,3},{6,6},{7,7},{8,8},{9,9},{10,12... | collective-permute-start | bytes 2359304 | tf_op jit(solution)/shard_map/ppermute | solution.py:192
  155.6 11.8 %collective-permute-start.17 = (bf16[192,1536]{1,0:T(8,128)(2,1)}, bf16[192,1536]{1,0:T(8,128)(2,1)}, u32[]{:S(2)}, u32[]{:S(2)}) collective-permute-start(bf16[192,1536]{1,0:T(8,128)(2,1)} %slice.131), channel_id=1, source_target_pairs={{0,8},{1,9},{2,10},{3,11},{4,12},{5,13},{6,14},{7,15},{8,0},{9,1},... | collective-permute-start | bytes 1769480 | tf_op jit(solution)/shard_map/ppermute | solution.py:192
  156.8 11.6 %collective-permute-start.16 = (bf16[192,1536]{1,0:T(8,128)(2,1)}, bf16[192,1536]{1,0:T(8,128)(2,1)}, u32[]{:S(2)}, u32[]{:S(2)}) collective-permute-start(bf16[192,1536]{1,0:T(8,128)(2,1)} %slice.130), channel_id=1, source_target_pairs={{0,16},{1,17},{2,18},{3,19},{4,20},{5,21},{6,22},{7,23},{8,24},{9,... | collective-permute-start | bytes 1769480 | tf_op jit(solution)/shard_map/ppermute | solution.py:192
  159.5 138.5 %reduce-scatter.4.cloned.1.call-start = ((), (), s32[]{:S(2)}) async-start(), calls=%async_computation.6 | async-start | bytes 5898240 | tf_op jit(solution)/shard_map/reduce_scatter | solution.py:279
  193.0 21.1 %collective-permute-start.20 = (bf16[256,1536]{1,0:T(8,128)(2,1)}, bf16[256,1536]{1,0:T(8,128)(2,1)S(1)}, u32[]{:S(2)}, u32[]{:S(2)}) collective-permute-start(bf16[256,1536]{1,0:T(8,128)(2,1)} %collective-permute-done.18), channel_id=1, source_target_pairs={{0,1},{1,0},{2,3},{3,2},{4,5},{5,4},{6,7},{7,6},{8,9},{9,8},{10,11... | collective-permute-start | bytes 2359304 | tf_op jit(solution)/shard_map/ppermute | solution.py:192
  196.1 7.4 %collective-permute-start.19 = (bf16[512,1536]{1,0:T(8,128)(2,1)S(1)}, bf16[512,1536]{1,0:T(8,128)(2,1)S(1)}, u32[]{:S(2)}, u32[]{:S(2)}) collective-permute-start(bf16[512,1536]{1,0:T(8,128)(2,1)S(1)} %get-tuple-element.164), channel_id=1, source_target_pairs={{0,4},{1,5},{2,6},{3,7},{4,0},{5,1},{6,2},{7,3},{8,12},{9,13},{10,... | collective-permute-start | bytes 4718600 | tf_op jit(solution)/shard_map/ppermute | solution.py:192
  215.3 3.8 collective-permute-start.21
  227.9 137.3 %reduce-scatter.6.cloned.1.call-start = ((), (), s32[]{:S(2)}) async-start(), calls=%async_computation.7 | async-start | bytes 5898240 | tf_op jit(solution)/shard_map/reduce_scatter | solution.py:279
  252.5 35.9 %collective-permute-start.23 = (bf16[512,1536]{1,0:T(8,128)(2,1)}, bf16[512,1536]{1,0:T(8,128)(2,1)}, u32[]{:S(2)}, u32[]{:S(2)}) collective-permute-start(bf16[512,1536]{1,0:T(8,128)(2,1)} %fusion.13), channel_id=1, source_target_pairs={{0,1},{1,0},{2,3},{3,2},{4,5},{5,4},{6,7},{7,6},{8,9},{9,8},{10,11... | collective-permute-start | bytes 4718600 | tf_op jit(solution)/shard_map/ppermute | solution.py:192
  259.8 127.9 %reduce-scatter.8.cloned.1.call-start = ((), (), s32[]{:S(2)}) async-start(), calls=%async_computation.8 | async-start | bytes 1474560 | tf_op jit(solution)/shard_map/reduce_scatter | solution.py:279
  298.0 7.0 %collective-permute-start.24 = (bf16[512,1536]{1,0:T(8,128)(2,1)}, bf16[512,1536]{1,0:T(8,128)(2,1)}, u32[]{:S(2)}, u32[]{:S(2)}) collective-permute-start(bf16[512,1536]{1,0:T(8,128)(2,1)} %get-tuple-element.178), channel_id=1, source_target_pairs={{0,4},{1,5},{2,6},{3,7},{4,0},{5,1},{6,2},{7,3},{8,12},{9,13},{10,... | collective-permute-start | bytes 4718600 | tf_op jit(solution)/shard_map/ppermute | solution.py:192
  299.2 10.2 %collective-permute-start.25 = (bf16[512,1536]{1,0:T(8,128)(2,1)}, bf16[512,1536]{1,0:T(8,128)(2,1)}, u32[]{:S(2)}, u32[]{:S(2)}) collective-permute-start(bf16[512,1536]{1,0:T(8,128)(2,1)} %slice.246), channel_id=1, source_target_pairs={{0,4},{1,5},{2,6},{3,7},{4,0},{5,1},{6,2},{7,3},{8,12},{9,13},{10,... | collective-permute-start | bytes 4718600 | tf_op jit(solution)/shard_map/ppermute | solution.py:192
  299.2 38.3 %collective-permute-start.26 = (bf16[384,1536]{1,0:T(8,128)(2,1)}, bf16[384,1536]{1,0:T(8,128)(2,1)}, u32[]{:S(2)}, u32[]{:S(2)}) collective-permute-start(bf16[384,1536]{1,0:T(8,128)(2,1)} %reduce-scatter.4.cloned.1.call-done), channel_id=1, source_target_pairs={{2,0},{3,1},{4,6},{5,7},{10,8},{11,9},{12,14},{13,15},{18,16},{19,... | collective-permute-start | bytes 3538952 | tf_op jit(solution)/shard_map/ppermute | solution.py:232
  312.1 30.4 %collective-permute-start.27 = (bf16[256,1536]{1,0:T(8,128)(2,1)}, bf16[256,1536]{1,0:T(8,128)(2,1)}, u32[]{:S(2)}, u32[]{:S(2)}) collective-permute-start(bf16[256,1536]{1,0:T(8,128)(2,1)} %fusion.21), channel_id=1, source_target_pairs={{0,1},{1,0},{2,3},{3,2},{4,5},{5,4},{6,7},{7,6},{8,9},{9,8},{10,11... | collective-permute-start | bytes 2359304 | tf_op jit(solution)/shard_map/ppermute | solution.py:192
  342.5 12.2 %collective-permute-start.28 = (bf16[192,1152]{1,0:T(8,128)(2,1)}, bf16[192,1152]{1,0:T(8,128)(2,1)}, u32[]{:S(2)}, u32[]{:S(2)}) collective-permute-start(bf16[192,1152]{1,0:T(8,128)(2,1)} %get-tuple-element.188), channel_id=1, source_target_pairs={{0,8},{1,9},{2,10},{3,11},{4,12},{5,13},{6,14},{7,15},{8,0},{9,1},... | collective-permute-start | bytes 1327112 | tf_op jit(solution)/shard_map/ppermute | solution.py:192
  343.7 11.9 %collective-permute-start.29 = (bf16[192,1152]{1,0:T(8,128)(2,1)}, bf16[192,1152]{1,0:T(8,128)(2,1)}, u32[]{:S(2)}, u32[]{:S(2)}) collective-permute-start(bf16[192,1152]{1,0:T(8,128)(2,1)} %get-tuple-element.189), channel_id=1, source_target_pairs={{0,16},{1,17},{2,18},{3,19},{4,20},{5,21},{6,22},{7,23},{8,24},{9,... | collective-permute-start | bytes 1327112 | tf_op jit(solution)/shard_map/ppermute | solution.py:192
  355.7 6.8 %collective-permute-start.30 = (bf16[512,1536]{1,0:T(8,128)(2,1)}, bf16[512,1536]{1,0:T(8,128)(2,1)}, u32[]{:S(2)}, u32[]{:S(2)}) collective-permute-start(bf16[512,1536]{1,0:T(8,128)(2,1)} %slice.245), channel_id=1, source_target_pairs={{0,4},{1,5},{2,6},{3,7},{4,0},{5,1},{6,2},{7,3},{8,12},{9,13},{10,... | collective-permute-start | bytes 4718600 | tf_op jit(solution)/shard_map/ppermute | solution.py:192
  365.2 28.8 %collective-permute-start.31 = (bf16[256,1536]{1,0:T(8,128)(2,1)}, bf16[256,1536]{1,0:T(8,128)(2,1)}, u32[]{:S(2)}, u32[]{:S(2)}) collective-permute-start(bf16[256,1536]{1,0:T(8,128)(2,1)} %fusion.20), channel_id=1, source_target_pairs={{0,1},{1,0},{2,3},{3,2},{4,5},{5,4},{6,7},{7,6},{8,9},{9,8},{10,11... | collective-permute-start | bytes 2359304 | tf_op jit(solution)/shard_map/ppermute | solution.py:192
  365.2 29.6 %collective-permute-start.35 = (bf16[256,1536]{1,0:T(8,128)(2,1)}, bf16[256,1536]{1,0:T(8,128)(2,1)}, u32[]{:S(2)}, u32[]{:S(2)}) collective-permute-start(bf16[256,1536]{1,0:T(8,128)(2,1)} %fusion.19), channel_id=1, source_target_pairs={{0,0},{1,1},{2,4},{3,5},{4,2},{5,3},{6,6},{7,7},{8,8},{9,9},{10,12... | collective-permute-start | bytes 2359304 | tf_op jit(solution)/shard_map/ppermute | solution.py:192
  371.7 23.2 %collective-permute-start.32 = (bf16[384,1152]{1,0:T(8,128)(2,1)}, bf16[384,1152]{1,0:T(8,128)(2,1)}, u32[]{:S(2)}, u32[]{:S(2)}) collective-permute-start(bf16[384,1152]{1,0:T(8,128)(2,1)} %pad_maximum_fusion.2), channel_id=1, source_target_pairs={{0,8},{1,9},{2,10},{3,11},{4,12},{5,13},{6,14},{7,15},{8,0},{9,1},... | collective-permute-start | bytes 2654216 | tf_op jit(solution)/shard_map/ppermute | solution.py:192
  372.7 31.2 %collective-permute-start.34 = (bf16[384,1536]{1,0:T(8,128)(2,1)}, bf16[384,1536]{1,0:T(8,128)(2,1)}, u32[]{:S(2)}, u32[]{:S(2)}) collective-permute-start(bf16[384,1536]{1,0:T(8,128)(2,1)} %reduce-scatter.6.cloned.1.call-done), channel_id=1, source_target_pairs={{2,0},{3,1},{4,6},{5,7},{10,8},{11,9},{12,14},{13,15},{18,16},{19,... | collective-permute-start | bytes 3538952 | tf_op jit(solution)/shard_map/ppermute | solution.py:232
  381.9 20.7 %collective-permute-start.33 = (bf16[384,1152]{1,0:T(8,128)(2,1)}, bf16[384,1152]{1,0:T(8,128)(2,1)}, u32[]{:S(2)}, u32[]{:S(2)}) collective-permute-start(bf16[384,1152]{1,0:T(8,128)(2,1)} %pad_maximum_fusion.3), channel_id=1, source_target_pairs={{0,16},{1,17},{2,18},{3,19},{4,20},{5,21},{6,22},{7,23},{8,24},{9,... | collective-permute-start | bytes 2654216 | tf_op jit(solution)/shard_map/ppermute | solution.py:192
  394.0 57.4 %collective-permute-start.44 = (f32[192,1536]{1,0:T(8,128)}, f32[192,1536]{1,0:T(8,128)S(1)}, u32[]{:S(2)}, u32[]{:S(2)}) collective-permute-start(f32[192,1536]{1,0:T(8,128)} %slice_select_fusion.1), channel_id=1, source_target_pairs={{0,4},{1,5},{2,6},{3,7},{4,0},{5,1},{6,2},{7,3},{8,12},{9,13},{10,... | collective-permute-start | bytes 3538952 | tf_op jit(solution)/shard_map/ppermute | solution.py:192
  409.1 19.3 %collective-permute-start.36 = (f32[4,1536]{1,0:T(4,128)S(1)}, f32[4,1536]{1,0:T(4,128)S(1)}, u32[]{:S(2)}, u32[]{:S(2)}) collective-permute-start(f32[4,1536]{1,0:T(4,128)S(1)} %pad_maximum_fusion.7), channel_id=1, source_target_pairs={{0,4},{1,5},{2,6},{3,7},{4,0},{5,1},{6,2},{7,3},{8,12},{9,13},{10,... | collective-permute-start | bytes 73736 | tf_op jit(solution)/shard_map/ppermute | solution.py:192
  422.5 20.3 %collective-permute-start.38 = (bf16[256,1536]{1,0:T(8,128)(2,1)S(1)}, bf16[256,1536]{1,0:T(8,128)(2,1)S(1)}, u32[]{:S(2)}, u32[]{:S(2)}) collective-permute-start(bf16[256,1536]{1,0:T(8,128)(2,1)S(1)} %fusion.16), channel_id=1, source_target_pairs={{0,0},{1,1},{2,4},{3,5},{4,2},{5,3},{6,6},{7,7},{8,8},{9,9},{10,12... | collective-permute-start | bytes 2359304 | tf_op jit(solution)/shard_map/ppermute | solution.py:192
  426.5 26.7 %collective-permute-start.45 = (f32[192,1536]{1,0:T(8,128)S(1)}, f32[192,1536]{1,0:T(8,128)S(1)}, u32[]{:S(2)}, u32[]{:S(2)}) collective-permute-start(f32[192,1536]{1,0:T(8,128)S(1)} %slice_select_fusion), channel_id=1, source_target_pairs={{0,4},{1,5},{2,6},{3,7},{4,0},{5,1},{6,2},{7,3},{8,12},{9,13},{10,... | collective-permute-start | bytes 3538952 | tf_op jit(solution)/shard_map/ppermute | solution.py:192
  428.4 5.5 %collective-permute-start.37 = (f32[4,1536]{1,0:T(4,128)S(1)}, f32[4,1536]{1,0:T(4,128)S(1)}, u32[]{:S(2)}, u32[]{:S(2)}) collective-permute-start(f32[4,1536]{1,0:T(4,128)S(1)} %add.263), channel_id=1, source_target_pairs={{0,1},{1,0},{2,3},{3,2},{4,5},{5,4},{6,7},{7,6},{8,9},{9,8},{10,11... | collective-permute-start | bytes 73736 | tf_op jit(solution)/shard_map/ppermute | solution.py:192
  446.3 3.8 collective-permute-start.42
  446.9 7.6 %collective-permute-start.40 = (bf16[192,1536]{1,0:T(8,128)(2,1)S(1)}, bf16[192,1536]{1,0:T(8,128)(2,1)S(1)}, u32[]{:S(2)}, u32[]{:S(2)}) collective-permute-start(bf16[192,1536]{1,0:T(8,128)(2,1)S(1)} %get-tuple-element.262), channel_id=1, source_target_pairs={{0,4},{1,5},{2,0},{3,1},{4,6},{5,7},{6,2},{7,3},{8,12},{9,13},{10,... | collective-permute-start | bytes 1769480 | tf_op jit(solution)/shard_map/ppermute | solution.py:192
  447.0 27.8 %collective-permute-start.39 = (bf16[192,1536]{1,0:T(8,128)(2,1)S(1)}, bf16[192,1536]{1,0:T(8,128)(2,1)S(1)}, u32[]{:S(2)}, u32[]{:S(2)}) collective-permute-start(bf16[192,1536]{1,0:T(8,128)(2,1)S(1)} %get-tuple-element.263), channel_id=1, source_target_pairs={{0,0},{1,1},{2,4},{3,5},{4,2},{5,3},{6,6},{7,7},{8,8},{9,9},{10,12... | collective-permute-start | bytes 1769480 | tf_op jit(solution)/shard_map/ppermute | solution.py:192
  (48 other events, 787.0 us)
Sparse Core Ops, SparseCore 0:
  34.9 48.9 all-gather.3
  86.3 29.3 all-gather.5
  159.6 58.4 all-gather.7
  228.0 55.3 reduce-scatter.3
  286.2 57.0 reduce-scatter.5
  359.0 28.6 reduce-scatter.7
